TPU v7x, 32 devices: a whole 2x2x4 slice. The times are simulated.
32 devices in a mesh: wide: 8 (over y, x, core), samp: 4 (over z).
Axes of the slice: x: 2, y: 2, z: 4, core: 2. Of those that a mesh axis runs over, the one named last changes fastest.
Arguments:
- features: bfloat16 [4, 32, 96, 128], P('samp', 'wide'), may hold values from -6 to 6
- labels: int32 [4, 32, 96], P('samp', 'wide'), may hold values from 0 to 8
- conv_weight: bfloat16 [3, 3, 128, 128], replicated, may hold values from -0.1875 to 0.1875
- down_weight: bfloat16 [512, 1024], replicated, may hold values from -0.25 to 0.25
- expand_weight: bfloat16 [3, 3, 1024, 2048], P(None, None, None, 'wide'), may hold values from -0.0625 to 0.0625
- reduce_weight: bfloat16 [3, 3, 2048, 1024], P(None, None, 'wide'), may hold values from -0.046875 to 0.046875
- up_weight: bfloat16 [1024, 512], replicated, may hold values from -0.1875 to 0.1875
- class_weight: bfloat16 [128, 9], replicated, may hold values from -3 to 3
Outputs:
- conv_grad: float32 [3, 3, 128, 128], replicated
- down_grad: float32 [512, 1024], replicated
- expand_grad: float32 [3, 3, 1024, 2048], P(None, None, 'samp', 'wide')
- reduce_grad: float32 [3, 3, 2048, 1024], P(None, None, 'wide', 'samp')
- up_grad: float32 [1024, 512], replicated
- class_grad: float32 [128, 9], replicated
All inputs are finite; a program needn't handle non-finite values.
Results may differ from a plain program's by a relative error of at most 0.012.
Values may be sent and summed in bfloat16 or wider, within the bound.
No kernel may reach another device: no remote copies, remote signals or barrier semaphores. Data moves between devices by JAX's collectives and lax.ppermute only.
A program may use at most 192 MiB of HBM per device.

v0:
```python
import math

import jax
import jax.numpy as jnp
from jax import lax
from jax.sharding import PartitionSpec as P


def extended(block, sides, width):
    for axis, dim in sides:
        count = lax.axis_size(axis)
        forward = [(i, i + 1) for i in range(count - 1)]
        backward = [(target, source) for source, target in forward]
        low = lax.ppermute(
            lax.slice_in_dim(block, block.shape[dim] - width, None, axis=dim), axis, forward
        )
        high = lax.ppermute(lax.slice_in_dim(block, 0, width, axis=dim), axis, backward)
        block = jnp.concatenate([low, block, high], axis=dim)
    return block


def silu_slope(value):
    logistic = jax.nn.sigmoid(value)
    return logistic * (1.0 + value * (1.0 - logistic))


def pad_both(values):
    return jnp.pad(values, ((1, 1), (1, 1), (0, 0)))


def to_depth(grid):
    height, across, channels = grid.shape
    blocks = grid.reshape(height // 2, 2, across // 2, 2, channels)
    return jnp.transpose(blocks, (0, 2, 1, 3, 4)).reshape(height // 2, across // 2, 4 * channels)


def from_depth(grid):
    height, across, channels = grid.shape
    blocks = grid.reshape(height, across, 2, 2, channels // 4)
    return jnp.transpose(blocks, (0, 2, 1, 3, 4)).reshape(2 * height, 2 * across, channels // 4)


def taps_in(padded, height, across):
    return jnp.concatenate(
        [padded[p : p + height, q : q + across] for p in range(3) for q in range(3)], axis=-1
    )


def taps_out(values):
    return jnp.concatenate(
        [jnp.pad(values, ((p, 2 - p), (q, 2 - q), (0, 0))) for p in range(3) for q in range(3)],
        axis=-1,
    )


def conv_padded(padded, weight):
    height = padded.shape[0] - 2
    across = padded.shape[1] - 2
    inward = weight.shape[2]
    outward = weight.shape[3]
    if inward <= outward:
        window = taps_in(padded, height, across).reshape(height * across, 9 * inward)
        result = jnp.dot(
            window, weight.reshape(9 * inward, outward), preferred_element_type=jnp.float32
        )
        return result.reshape(height, across, outward)
    flattened = padded.reshape((height + 2) * (across + 2), inward)
    stacked = jnp.transpose(weight, (2, 0, 1, 3)).reshape(inward, 9 * outward)
    spread_out = jnp.dot(flattened, stacked, preferred_element_type=jnp.float32).reshape(
        height + 2, across + 2, 9, outward
    )
    summed = spread_out[0:height, 0:across, 0]
    for offset in range(1, 9):
        p = offset // 3
        q = offset % 3
        summed = summed + spread_out[p : p + height, q : q + across, offset]
    return summed


def correlate(padded, values):
    height, across, outward = values.shape
    inward = padded.shape[-1]
    if inward <= outward:
        window = taps_in(padded, height, across).reshape(height * across, 9 * inward)
        result = lax.dot_general(
            window,
            values.reshape(height * across, outward),
            (((0,), (0,)), ((), ())),
            preferred_element_type=jnp.float32,
        )
        return result.reshape(3, 3, inward, outward)
    shifted = taps_out(values).reshape((height + 2) * (across + 2), 9 * outward)
    result = lax.dot_general(
        padded.reshape(-1, inward),
        shifted,
        (((0,), (0,)), ((), ())),
        preferred_element_type=jnp.float32,
    )
    return jnp.transpose(result.reshape(inward, 3, 3, outward), (1, 2, 0, 3))


def contract_rows(left, right):
    left_flat = left.reshape(-1, left.shape[-1])
    right_flat = right.reshape(-1, right.shape[-1])
    return lax.dot_general(
        left_flat, right_flat, (((0,), (0,)), ((), ())), preferred_element_type=jnp.float32
    )


def flip_kernel(weight):
    return jnp.transpose(weight[::-1, ::-1], (0, 1, 3, 2))


def keep_rows(block_rows, first_row):
    return block_rows


def project_rows(values, weight):
    return jnp.dot(values, weight, preferred_element_type=jnp.float32).astype(jnp.bfloat16)


def widen_rows(values, weight):
    return lax.dot_general(
        values, weight, (((2,), (1,)), ((), ())), preferred_element_type=jnp.float32
    ).astype(jnp.bfloat16)


def collect(values, transform):
    return transform(lax.all_gather(values, "wide", axis=0, tiled=True), jnp.int32(0))


def spread_sum(term_rows, all_rows):
    whole_term = term_rows(0, all_rows)[None]
    pieces = lax.all_to_all(
        whole_term.astype(jnp.bfloat16), "wide", split_axis=1, concat_axis=0, tiled=True
    ).astype(whole_term.dtype)
    return jnp.sum(pieces, axis=0)


def local(
    features,
    labels,
    conv_weight,
    down_weight,
    expand_weight,
    reduce_weight,
    up_weight,
    class_weight,
):
    crop_rows = features[0]
    label_map = labels[0]
    height, across, channels = crop_rows.shape
    pixel_count = lax.axis_size("wide") * lax.axis_size("samp") * height * across
    loss_scale = 8.0 / math.sqrt(pixel_count)
    classes = lax.broadcasted_iota(jnp.int32, (1, 1, class_weight.shape[1]), 2)
    near_rows = extended(crop_rows, (("wide", 0),), 1)
    padded_in = jnp.pad(near_rows, ((0, 0), (1, 1), (0, 0)))
    hidden_pre = conv_padded(padded_in, conv_weight)
    hidden = jax.nn.silu(hidden_pre).astype(jnp.bfloat16)
    stacked = to_depth(hidden)
    coarse = project_rows(stacked, down_weight)
    coarse_all = collect(coarse, keep_rows)
    all_rows = coarse_all.shape[0]
    coarse_pad = pad_both(coarse_all)
    expand_pre = conv_padded(coarse_pad, expand_weight)
    expanded = jax.nn.silu(expand_pre).astype(jnp.bfloat16)
    expand_pad = pad_both(expanded)

    def reduce_block(first_row, row_count):
        return conv_padded(expand_pad, reduce_weight)

    bottom = (coarse.astype(jnp.float32) + spread_sum(reduce_block, all_rows)).astype(jnp.bfloat16)
    upward = from_depth(jnp.dot(bottom, up_weight, preferred_element_type=jnp.float32))
    joined_pre = upward + hidden.astype(jnp.float32)
    joined = jax.nn.silu(joined_pre).astype(jnp.bfloat16)
    logits = jnp.dot(joined, class_weight, preferred_element_type=jnp.float32)
    exp_logits = jnp.exp(logits)
    probability = exp_logits / jnp.sum(exp_logits, axis=-1, keepdims=True)
    onehot = (label_map[:, :, None] == classes).astype(jnp.float32)
    logit_grad = ((probability - onehot) * loss_scale).astype(jnp.bfloat16)
    class_grad = contract_rows(joined, logit_grad)
    joined_grad = lax.dot_general(
        logit_grad, class_weight, (((2,), (1,)), ((), ())), preferred_element_type=jnp.float32
    )
    upward_grad = (joined_grad * silu_slope(joined_pre)).astype(jnp.bfloat16)
    stacked_grad = to_depth(upward_grad)
    up_grad = contract_rows(bottom, stacked_grad)
    bottom_grad = widen_rows(stacked_grad, up_weight)
    bottom_all = collect(bottom_grad, keep_rows)
    reduce_grad = correlate(expand_pad, bottom_all)
    expanded_back = conv_padded(pad_both(bottom_all), flip_kernel(reduce_weight))
    expanded_grad = (expanded_back * silu_slope(expand_pre)).astype(jnp.bfloat16)
    expand_grad = correlate(coarse_pad, expanded_grad)
    grad_pad = pad_both(expanded_grad)
    back_expand = flip_kernel(expand_weight)

    def expand_back_block(first_row, row_count):
        return conv_padded(grad_pad, back_expand)

    coarse_grad = (
        bottom_grad.astype(jnp.float32) + spread_sum(expand_back_block, all_rows)
    ).astype(jnp.bfloat16)
    down_grad = contract_rows(stacked, coarse_grad)
    down_back = lax.dot_general(
        coarse_grad, down_weight, (((2,), (1,)), ((), ())), preferred_element_type=jnp.float32
    )
    hidden_sum = from_depth(down_back) + upward_grad.astype(jnp.float32)
    hidden_grad = (hidden_sum * silu_slope(hidden_pre)).astype(jnp.bfloat16)
    conv_grad = correlate(padded_in, hidden_grad)
    conv_grad, down_grad, up_grad, class_grad = lax.psum(
        (conv_grad, down_grad, up_grad, class_grad), ("wide", "samp")
    )
    expand_grad, reduce_grad = (
        lax.psum_scatter(
            expand_grad.astype(jnp.bfloat16), "samp", scatter_dimension=2, tiled=True
        ).astype(jnp.float32),
        lax.psum_scatter(
            reduce_grad.astype(jnp.bfloat16), "samp", scatter_dimension=3, tiled=True
        ).astype(jnp.float32),
    )
    return (conv_grad, down_grad, expand_grad, reduce_grad, up_grad, class_grad)


def solution(mesh):
    return jax.shard_map(
        local,
        mesh=mesh,
        in_specs=(
            P("samp", "wide", None, None),
            P("samp", "wide", None),
            P(),
            P(),
            P(None, None, None, "wide"),
            P(None, None, "wide", None),
            P(),
            P(),
        ),
        out_specs=(
            P(),
            P(),
            P(None, None, "samp", "wide"),
            P(None, None, "wide", "samp"),
            P(),
            P(),
        ),
        check_vma=False,
    )
```

profile of v0, /device:TPU:0, one launch (start us, length us, event | category | flops | bytes accessed | tf_op | source)
XLA Modules:
  0.0 500.4 jit_solution(18291208784481795078)
XLA Ops:
  11.8 3.9 collective-permute-done.1
  24.9 6.7 %copy.50 = bf16[3,3,1024,256]{2,3,1,0:T(8,128)(2,1)} copy(bf16[3,3,1024,256]{3,2,1,0:T(8,128)(2,1)} %param.12) | data formatting | bytes 9437184 | tf_op args[4]
  31.5 22.4 %all-gather.3.cloned.1.call-done = bf16[16,48,1024]{2,1,0:T(8,128)(2,1)} async-done(((bf16[2,48,1024]{2,1,0:T(8,128)(2,1)}), bf16[16,48,1024]{2,1,0:T(8,128)(2,1)}) %all-gather.3.cloned.1.call-update) | async-done | bytes 1572880 | tf_op jit(solution)/shard_map/all_gather | solution.py:129
  54.0 8.0 %fusion.1 = f32[18,50,9,256]{3,1,2,0:T(8,128)S(1)} fusion(bf16[9,256,1024,1]{2,1,0,3:T(8,128)(2,1)} %bitcast.158, bf16[16,48,1024]{2,1,0:T(8,128)(2,1)} %all-gather.3.cloned.1.call-done), kind=kOutput, calls=%fused_computation.5 | convolution fusion | flops 4246732800 | bytes 14585856 | tf_op jit(solution)/shard_map/dot_general | solution.py:69
  64.4 3.8 fusion.7
  68.3 23.6 %all_to_all.8 = bf16[1,16,48,1024]{3,2,0,1:T(8,128)(2,1)S(1)} all-to-all(bf16[1,16,48,1024]{3,2,0,1:T(8,128)(2,1)S(1)} %fusion.7), channel_id=1, replica_groups=mesh['wide'=8,'samp'=4] {'wide'}, dimensions={1} | all-to-all | bytes 3145728 | tf_op jit(solution)/shard_map/all_to_all | solution.py:134
  96.0 4.9 rev.6
  104.7 15.8 %all-gather.5.cloned.1.call-done = bf16[16,48,1024]{2,1,0:T(8,128)(2,1)} async-done(((bf16[2,48,1024]{2,1,0:T(8,128)(2,1)}), bf16[16,48,1024]{2,1,0:T(8,128)(2,1)}) %all-gather.5.cloned.1.call-update) | async-done | bytes 1572880 | tf_op jit(solution)/shard_map/all_gather | solution.py:129
  120.5 7.9 %fusion.3 = f32[18,50,9,256]{3,1,0,2:T(8,128)S(1)} fusion(bf16[9,256,1024,1]{2,1,3,0:T(8,128)(2,1)} %bitcast.165, bf16[16,48,1024]{2,1,0:T(8,128)(2,1)} %all-gather.5.cloned.1.call-done), kind=kOutput, calls=%fused_computation.7 | convolution fusion | flops 4246732800 | bytes 14585856 | tf_op jit(solution)/shard_map/dot_general | solution.py:69
  137.9 6.0 %reshape.153 = bf16[900,2304]{1,0:T(8,128)(2,1)} reshape(bf16[18,50,2304]{2,1,0:T(8,128)(2,1)} %pad_dynamic-update-slice_fusion.1) | data formatting | bytes 8294400 | tf_op jit(solution)/shard_map/reshape | solution.py:92
  143.9 6.6 %copy.66 = bf16[900,2304]{0,1:T(8,128)(2,1)} copy(bf16[900,2304]{1,0:T(8,128)(2,1)} %reshape.153) | data formatting | bytes 8294400 | tf_op jit(solution)/shard_map/reshape | solution.py:92
  150.5 9.3 %convert_bitcast_fusion = bf16[3,3,1024,256]{3,2,1,0:T(8,128)(2,1)} fusion(bf16[3,3,256,900]{3,2,1,0:T(8,128)(2,1)} %bitcast.166, bf16[900,1024,1,1]{1,0,2,3:T(8,128)(2,1)S(1)} %copy-done.9), kind=kOutput, calls=%fused_computation.1 | convolution fusion | flops 4249092096 | bytes 10708992 | tf_op jit(solution)/shard_map/dot_general | solution.py:93
  160.1 5.9 %copy.68 = bf16[2304,768]{1,0:T(8,128)(2,1)} copy(bf16[2304,768]{0,1:T(8,128)(2,1)} %bitcast.167) | data formatting | bytes 7077888 | tf_op jit(solution)/shard_map/dot_general | solution.py:85
  166.0 7.9 %convolution_convert_fusion = bf16[3,3,256,1024]{3,2,1,0:T(8,128)(2,1)} fusion(bf16[3,3,256,768]{3,2,1,0:T(8,128)(2,1)} %bitcast.168, bf16[768,1024,1,1]{1,0,3,2:T(8,128)(2,1)S(1)} %bitcast.195), kind=kOutput, calls=%fused_computation.4 | convolution fusion | flops 3626237952 | bytes 9830400 | tf_op jit(solution)/shard_map/dot_general | solution.py:85
  173.9 5.0 %rev.7 = bf16[3,3,1024,256]{2,3,1,0:T(8,128)(2,1)} reverse(bf16[3,3,1024,256]{2,3,1,0:T(8,128)(2,1)} %copy.50), dimensions={0,1} | reverse | bytes 9437184 | tf_op jit(solution)/shard_map/rev | solution.py:111
  181.2 4.9 fusion.8
  186.1 3.7 all-to-all-start.1
  198.1 12.8 %all-to-all-done.1 = bf16[1,16,48,1024]{3,2,0,1:T(8,128)(2,1)S(1)} async-done(((bf16[1,16,48,1024]{3,2,0,1:T(8,128)(2,1)}), bf16[1,16,48,1024]{3,2,0,1:T(8,128)(2,1)S(1)}, u32[]{:S(2)}, u32[]{:S(2)}) %all-to-all-start.1) | async-done | bytes 1572896 | tf_op jit(solution)/shard_map/all_to_all | solution.py:134
  217.1 42.5 %psum.31 = f32[128,9]{0,1:T(8,128)} all-reduce(f32[128,9]{0,1:T(8,128)S(1)} %convolution_bitcast_fusion), channel_id=1, replica_groups=mesh['wide'=8,'samp'=4] {'wide','samp'}, use_global_device_ids=true, to_apply=%region_8.9 | all-reduce | flops 1152 | bytes 9216 | tf_op jit(solution)/shard_map/psum | solution.py:210
  259.6 2.9 convert_element_type.144
  262.5 71.5 %reduce-scatter.5.cloned.1.call-done = bf16[3,3,256,256]{3,2,1,0:T(8,128)(2,1)} async-done(((bf16[3,3,256,1024]{3,2,1,0:T(8,128)(2,1)}), bf16[3,3,256,256]{3,2,1,0:T(8,128)(2,1)}) %reduce-scatter.5.cloned.1.call-update) | async-done | bytes 1179664 | tf_op jit(solution)/shard_map/reduce_scatter | solution.py:217
  334.0 2.9 convert_element_type.146
  336.9 150.4 %all-reduce.16.cloned.1.call-done = (f32[3,3,128,128]{3,2,1,0:T(8,128)}, f32[512,1024]{1,0:T(8,128)}, f32[1024,512]{1,0:T(8,128)}) async-done(((f32[3,3,128,128]{3,2,1,0:T(8,128)}, f32[512,1024]{1,0:T(8,128)}, f32[1024,512]{1,0:T(8,128)}), (f32[3,3,128,128]{3,2,1,0:T(8,128)}, f32[512,1024]{1,0:T(8,128)}, f32[1024,512]{1,0:T(8,128)})) %all-reduce.16.cloned.1.call-update) | async-done | bytes 4784144 | tf_op jit(solution)/shard_map/psum | solution.py:210
  489.4 3.2 copy.124
  (152 shorter events, 53.6 us)
Async XLA Ops:
  7.2 85.8 %copy-start = (bf16[1024,512]{1,0:T(8,128)(2,1)S(1)}, bf16[1024,512]{1,0:T(8,128)(2,1)}, u32[]{:S(2)}) copy-start(bf16[1024,512]{1,0:T(8,128)(2,1)} %param.14) | copy-start | bytes 3145732
  7.2 16.6 %copy-start.4 = (bf16[512,1024]{1,0:T(8,128)(2,1)S(1)}, bf16[512,1024]{1,0:T(8,128)(2,1)}, u32[]{:S(2)}) copy-start(bf16[512,1024]{1,0:T(8,128)(2,1)} %param.11) | copy-start | bytes 3145732
  7.2 46.8 %all-gather.3.cloned.1.call-start = ((), (), s32[]{:S(2)}) async-start(), calls=%async_computation.4 | async-start | bytes 1769472 | tf_op jit(solution)/shard_map/all_gather | solution.py:129
  8.1 3.7 collective-permute-start
  10.5 5.2 %collective-permute-start.1 = (bf16[1,96,128]{2,1,0:T(8,128)(2,1)S(1)}, bf16[1,96,128]{2,1,0:T(8,128)(2,1)S(1)}, u32[]{:S(2)}, u32[]{:S(2)}) collective-permute-start(bf16[1,96,128]{2,1,0:T(8,128)(2,1)S(1)} %get-tuple-element.23), channel_id=1, source_target_pairs={{4,0},{8,4},{12,8},{16,12},{20,16},{24,20},{28,24},{5,1},{9,5},{13... | collective-permute-start | bytes 73736 | tf_op jit(solution)/shard_map/ppermute | solution.py:17
  24.8 95.7 %all-gather.5.cloned.1.call-start = ((), (), s32[]{:S(2)}) async-start(), calls=%async_computation.5 | async-start | bytes 1769472 | tf_op jit(solution)/shard_map/all_gather | solution.py:129
  54.0 10.4 %slice-start = ((s8[4718592]{0:T(1024)(128)(4,1)}), s8[4194304]{0:T(1024)(128)(4,1)S(1)}, s32[]{:S(2)}) async-start(s8[4718592]{0:T(1024)(128)(4,1)} %bitcast.161), calls=%async_computation.9 | async-start | bytes 8388608
  54.0 10.4 %slice-start.1 = ((s8[4718592]{0:T(1024)(128)(4,1)}), s8[524288]{0:T(1024)(128)(4,1)S(1)}, s32[]{:S(2)}) async-start(s8[4718592]{0:T(1024)(128)(4,1)} %bitcast.161), calls=%async_computation.10 | async-start | bytes 1048576
  68.3 23.9 %copy-start.11 = (bf16[2,48,1024]{2,1,0:T(8,128)(2,1)S(1)}, bf16[2,48,1024]{2,1,0:T(8,128)(2,1)}, u32[]{:S(2)}) copy-start(bf16[2,48,1024]{2,1,0:T(8,128)(2,1)} %convolution_convert_fusion.4) | copy-start | bytes 589828
  68.3 25.3 %copy-start.23 = (bf16[128,9]{0,1:T(8,128)(2,1)S(1)}, bf16[128,9]{0,1:T(8,128)(2,1)}, u32[]{:S(2)}) copy-start(bf16[128,9]{0,1:T(8,128)(2,1)} %param.15) | copy-start | bytes 6916
  95.7 163.9 %reduce-scatter.3.cloned.1.call-start = ((), (), s32[]{:S(2)}) async-start(), calls=%async_computation.6 | async-start | bytes 5898240 | tf_op jit(solution)/shard_map/reduce_scatter | solution.py:214
  120.5 7.9 %copy-start.6 = (f32[16,48,256]{2,1,0:T(8,128)S(1)}, f32[16,48,256]{2,1,0:T(8,128)}, u32[]{:S(2)}) copy-start(f32[16,48,256]{2,1,0:T(8,128)} %get-tuple-element.10) | copy-start | bytes 2359300
  143.9 6.6 %copy-start.9 = (bf16[900,1024,1,1]{1,0,2,3:T(8,128)(2,1)S(1)}, bf16[900,1024,1,1]{1,0,2,3:T(8,128)(2,1)}, u32[]{:S(2)}) copy-start(bf16[900,1024,1,1]{1,0,2,3:T(8,128)(2,1)} %reshape.178) | copy-start | bytes 5529604
  159.8 174.2 %reduce-scatter.5.cloned.1.call-start = ((), (), s32[]{:S(2)}) async-start(), calls=%async_computation.7 | async-start | bytes 5898240 | tf_op jit(solution)/shard_map/reduce_scatter | solution.py:217
  160.1 5.9 %copy-start.24 = (bf16[16,48,1024]{2,1,0:T(8,128)(2,1)S(1)}, bf16[16,48,1024]{2,1,0:T(8,128)(2,1)}, u32[]{:S(2)}) copy-start(bf16[16,48,1024]{2,1,0:T(8,128)(2,1)} %all-gather.5.cloned.1.call-done) | copy-start | bytes 4718596
  181.2 9.4 %copy-start.17 = (bf16[4,96,128]{2,1,0:T(8,128)(2,1)S(1)}, bf16[4,96,128]{2,1,0:T(8,128)(2,1)}, u32[]{:S(2)}) copy-start(bf16[4,96,128]{2,1,0:T(8,128)(2,1)} %get-tuple-element.20) | copy-start | bytes 294916
  186.1 4.6 copy-start.15
  186.1 4.7 copy-start.7
  186.1 4.8 copy-start.19
  186.1 24.7 %all-to-all-start.1 = ((bf16[1,16,48,1024]{3,2,0,1:T(8,128)(2,1)}), bf16[1,16,48,1024]{3,2,0,1:T(8,128)(2,1)S(1)}, u32[]{:S(2)}, u32[]{:S(2)}) async-start(bf16[1,16,48,1024]{3,2,0,1:T(8,128)(2,1)} %fusion.8), calls=%async_computation.1 | async-start | bytes 3145728 | tf_op jit(solution)/shard_map/all_to_all | solution.py:134
  189.9 297.4 %all-reduce.16.cloned.1.call-start = ((), (), s32[]{:S(2)}) async-start(), calls=%async_computation.8 | async-start | bytes 9568256 | tf_op jit(solution)/shard_map/psum | solution.py:210
  191.9 20.3 %copy-start.5 = (bf16[512,1024]{1,0:T(8,128)(2,1)S(1)}, bf16[512,1024]{1,0:T(8,128)(2,1)}, u32[]{:S(2)}) copy-start(bf16[512,1024]{1,0:T(8,128)(2,1)} %param.11) | copy-start | bytes 3145732
  487.3 5.2 %copy-start.8 = (f32[1024,512]{1,0:T(8,128)S(1)}, f32[1024,512]{1,0:T(8,128)}, u32[]{:S(2)}) copy-start(f32[1024,512]{1,0:T(8,128)} %get-tuple-element.30) | copy-start | bytes 6291460
  487.3 6.6 %copy-start.1 = (bf16[1024,512]{1,0:T(8,128)(2,1)S(1)}, bf16[1024,512]{1,0:T(8,128)(2,1)}, u32[]{:S(2)}) copy-start(bf16[1024,512]{1,0:T(8,128)(2,1)} %param.14) | copy-start | bytes 3145732
  (12 other events, 28.6 us)
Sparse Core Ops, SparseCore 0:
  25.0 28.9 all-gather.2
  95.8 24.6 all-gather.4
  159.9 85.9 reduce-scatter.2
  248.1 85.8 reduce-scatter.4
  340.5 146.7 all-reduce.15
where the time goes:
time: 502 us; the launch traced here: 500 us
  waiting for transfers between devices  277 us (55%)
  local copies, waits for them, and re-layouts  66.8 us (13%)
  blocking collectives  66.1 us (13%)
  matrix products  53 us (11%)
  other arithmetic  15.1 us (3%)
  between operations  14.5 us (3%)
  starting transfers between devices  8.02 us (2%)
    psum x1, waiting for transfers between devices, local(): lax.psum((conv_grad, down_grad, up_grad, class_grad), ('wide', 'samp'))  150 us
    reduce_scatter x1, waiting for transfers between devices, local(): lax.psum_scatter(reduce_grad.astype(jnp.bfloat16), 'samp', scatter_dimens...  71.5 us
    psum x1, blocking collectives, local(): lax.psum((conv_grad, down_grad, up_grad, class_grad), ('wide', 'samp'))  42.5 us
    all_gather x2, waiting for transfers between devices, collect(): lax.all_gather(values, 'wide', axis=0, tiled=True)  38.2 us
    unnamed x98, local copies, waits for them, and re-layouts  27 us
    all_to_all x1, blocking collectives, spread_sum(): lax.all_to_all(whole_term.astype(jnp.bfloat16), 'wide', split_axis=1, con...  23.6 us
    dot_general x2, matrix products, conv_padded(): jnp.dot(flattened, stacked, preferred_element_type=jnp.float32)  15.9 us
    all_to_all x1, waiting for transfers between devices, spread_sum(): lax.all_to_all(whole_term.astype(jnp.bfloat16), 'wide', split_axis=1, con...  12.8 us
  transfers between devices with their start and end apart: 8, of which 6 were waited for; matrix products, arithmetic and copies ran while one was open for 12% of the time, Pallas kernels for 0%

commit v1 on v0

v1 whole, which is shorter than its diff:
```python
import functools
import math

import jax
import jax.numpy as jnp
from jax import lax
from jax.experimental import pallas as pl
from jax.experimental.pallas import tpu as pltpu
from jax.sharding import PartitionSpec as P


def swap(values, axis, mask):
    count = lax.axis_size(axis)
    return lax.ppermute(values, axis, [(i, i ^ mask) for i in range(count)])


def chip_count():
    return lax.axis_size("wide") // 2


def gather_chips(piece):
    return [piece] + [swap(piece, "wide", 2 * r) for r in range(1, chip_count())]


def swap_cores(pieces):
    return [swap(piece, "wide", 1) for piece in pieces]


def scatter_chips(own, sent):
    chips = len(own)
    order = list(range(1, chips)) + [0]
    partner = {r: swap(sent[r], "wide", 1) for r in order}
    sends = [add_all(own[r], [partner[r]]).astype(jnp.bfloat16) for r in range(1, chips)]
    return [own[0], partner[0]] + send_chips(sends)


def send_chips(sends):
    return [swap(piece, "wide", 2 * (r + 1)) for r, piece in enumerate(sends)]


def send_samples(sends):
    return [swap(piece, "samp", mask + 1) for mask, piece in enumerate(sends)]


def lane_block(values, target, count):
    narrow = values.shape[-1] // count
    return lax.dynamic_slice_in_dim(values, target * narrow, narrow, axis=values.ndim - 1)


def add_all(first, rest):
    total = first.astype(jnp.float32)
    for item in rest:
        total = total + item.astype(jnp.float32)
    return total


def silu_slope(value):
    logistic = jax.nn.sigmoid(value)
    return logistic * (1.0 + value * (1.0 - logistic))


def column_mask(shape, column):
    return lax.broadcasted_iota(jnp.int32, shape, 1) == column


def from_left(values, across):
    view = values.reshape(-1, across, values.shape[-1])
    moved = pltpu.roll(view, 1, 1)
    return jnp.where(column_mask(view.shape, 0), 0.0, moved).reshape(values.shape)


def from_right(values, across):
    view = values.reshape(-1, across, values.shape[-1])
    moved = pltpu.roll(view, across - 1, 1)
    return jnp.where(column_mask(view.shape, across - 1), 0.0, moved).reshape(values.shape)


def block_start(place_ref, relative, half, rows, offset=0):
    chip = place_ref[1] ^ relative
    core = place_ref[0] ^ half
    return pl.multiple_of(offset + (2 * chip + core) * rows, 16)


def clear_edges(padded, across):
    total = padded.shape[0]
    blank = jnp.zeros((across, padded.shape[1]), padded.dtype)
    padded[0:across, :] = blank
    padded[total - across : total, :] = blank


def weight_copies(expand_hbm, reduce_hbm, expand_buf, reduce_buf, sems):
    inner = expand_hbm.shape[-1]
    base = expand_hbm.shape[-2]
    expand_copies = []
    reduce_copies = []
    for p in range(3):
        for q in range(3):
            expand_copies.append(
                pltpu.make_async_copy(
                    expand_hbm.at[p, q],
                    expand_buf.at[pl.ds(p * base, base), pl.ds(q * inner, inner)],
                    sems.at[3 * p + q],
                )
            )
            reduce_copies.append(
                pltpu.make_async_copy(
                    reduce_hbm.at[p, q],
                    reduce_buf.at[pl.ds((3 * p + q) * inner, inner), :],
                    sems.at[9 + 3 * p + q],
                )
            )
    return expand_copies, reduce_copies


def wait_all(copies):
    for copy in copies:
        copy.wait()


def plain_dot(left, right):
    return jnp.dot(left, right, preferred_element_type=jnp.float32)


def transposed_dot(left, right):
    return lax.dot_general(
        left, right, (((1,), (1,)), ((), ())), preferred_element_type=jnp.float32
    )


def gather_blocks(shifted, place_ref, half, offset, rows, blocks):
    return jnp.concatenate(
        [
            shifted[pl.ds(block_start(place_ref, block, half, rows, offset), rows), :]
            for block in range(blocks)
        ],
        axis=0,
    )


def store_rows(value, targets):
    rows = targets[0].shape[0]
    for index, target in enumerate(targets):
        target[...] = value[index * rows : (index + 1) * rows, :]


def forward_kernel(place_ref, *refs, blocks, rows, across):
    pieces = refs[: 2 * blocks]
    expand_hbm, reduce_hbm, pre_ref, exp_ref = refs[2 * blocks : 2 * blocks + 4]
    own_refs = refs[2 * blocks + 4 : 3 * blocks + 4]
    sent_refs = refs[3 * blocks + 4 : 4 * blocks + 4]
    padded, shifted, expand_buf, reduce_buf, sems = refs[4 * blocks + 4 :]
    expand_copies, reduce_copies = weight_copies(
        expand_hbm, reduce_hbm, expand_buf, reduce_buf, sems
    )
    for copy in expand_copies + reduce_copies:
        copy.start()
    clear_edges(padded, across)
    clear_edges(shifted, across)
    for index, piece in enumerate(pieces):
        start = block_start(place_ref, index % blocks, index // blocks, rows, across)
        padded[pl.ds(start, rows), :] = piece[...]
    inner = expand_hbm.shape[-1]
    base = expand_hbm.shape[-2]
    positions = pre_ref.shape[0]
    total = None
    for p in range(3):
        wait_all(expand_copies[3 * p : 3 * p + 3])
        term = plain_dot(
            padded[p * across : p * across + positions, :],
            expand_buf[p * base : (p + 1) * base, :],
        )
        total = term if total is None else total + term
    pre = (
        total[:, inner : 2 * inner]
        + from_left(total[:, 0:inner], across)
        + from_right(total[:, 2 * inner : 3 * inner], across)
    )
    pre_ref[...] = pre
    expanded = (pre * jax.nn.sigmoid(pre)).astype(jnp.bfloat16)
    exp_ref[...] = expanded
    wide = expanded.astype(jnp.float32)
    inside = pl.ds(across, positions)
    shifted[inside, 0:inner] = from_left(wide, across).astype(jnp.bfloat16)
    shifted[inside, inner : 2 * inner] = expanded
    shifted[inside, 2 * inner : 3 * inner] = from_right(wide, across).astype(jnp.bfloat16)
    wait_all(reduce_copies)
    for half, targets in ((1, sent_refs), (0, own_refs)):
        left = jnp.concatenate(
            [
                gather_blocks(shifted, place_ref, half, p * across, rows, blocks)
                for p in range(3)
            ],
            axis=1,
        )
        store_rows(plain_dot(left, reduce_buf[...]).astype(jnp.bfloat16), targets)


def backward_kernel(place_ref, *refs, blocks, rows, across):
    pieces = refs[: 2 * blocks]
    expand_hbm, reduce_hbm, pre_ref, grad_ref = refs[2 * blocks : 2 * blocks + 4]
    own_refs = refs[2 * blocks + 4 : 3 * blocks + 4]
    sent_refs = refs[3 * blocks + 4 : 4 * blocks + 4]
    padded, shifted, expand_buf, reduce_buf, sems = refs[4 * blocks + 4 :]
    expand_copies, reduce_copies = weight_copies(
        expand_hbm, reduce_hbm, expand_buf, reduce_buf, sems
    )
    for copy in reduce_copies + expand_copies:
        copy.start()
    clear_edges(padded, across)
    clear_edges(shifted, across)
    for index, piece in enumerate(pieces):
        start = block_start(place_ref, index % blocks, index // blocks, rows, across)
        padded[pl.ds(start, rows), :] = piece[...]
    inner = expand_hbm.shape[-1]
    base = expand_hbm.shape[-2]
    positions = pre_ref.shape[0]
    total = None
    for p in range(3):
        wait_all(reduce_copies[3 * p : 3 * p + 3])
        start = (2 - p) * across
        term = transposed_dot(
            padded[start : start + positions, :],
            reduce_buf[3 * p * inner : 3 * (p + 1) * inner, :],
        )
        total = term if total is None else total + term
    back = (
        total[:, inner : 2 * inner]
        + from_right(total[:, 0:inner], across)
        + from_left(total[:, 2 * inner : 3 * inner], across)
    )
    pre = pre_ref[...]
    grad = (back * silu_slope(pre)).astype(jnp.bfloat16)
    grad_ref[...] = grad
    wide = grad.astype(jnp.float32)
    inside = pl.ds(across, positions)
    shifted[inside, 0:inner] = from_right(wide, across).astype(jnp.bfloat16)
    shifted[inside, inner : 2 * inner] = grad
    shifted[inside, 2 * inner : 3 * inner] = from_left(wide, across).astype(jnp.bfloat16)
    wait_all(expand_copies)
    for half, targets in ((1, sent_refs), (0, own_refs)):
        out = None
        for p in range(3):
            left = gather_blocks(shifted, place_ref, half, (2 - p) * across, rows, blocks)
            term = transposed_dot(left, expand_buf[p * base : (p + 1) * base, :])
            out = term if out is None else out + term
        store_rows(out.astype(jnp.bfloat16), targets)


BOTTLENECK_MIB = 12
CORRELATE_MIB = 8
SMALL_MIB = 6

VMEM_SPEC = pl.BlockSpec(memory_space=pltpu.VMEM)
SMEM_SPEC = pl.BlockSpec(memory_space=pltpu.SMEM)
HBM_SPEC = pl.BlockSpec(memory_space=pltpu.HBM)


def granted(operands, outs, scratch, temporaries):
    total = sum(math.prod(item.shape) * item.dtype.itemsize for item in (*operands, *outs))
    total += sum(math.prod(shape) * jnp.dtype(dtype).itemsize for shape, dtype in scratch)
    limit = min(int(total * 1.1) + (temporaries << 20), 60 << 20)
    return pltpu.CompilerParams(vmem_limit_bytes=limit)


def bottleneck_call(kernel, place, pieces, expand_weight, reduce_weight, pre, across):
    rows, base = pieces[0].shape
    positions = len(pieces) * rows
    inner = expand_weight.shape[-1]
    inner_bf16 = jax.ShapeDtypeStruct((positions, inner), jnp.bfloat16)
    inner_f32 = jax.ShapeDtypeStruct((positions, inner), jnp.float32)
    parts = (jax.ShapeDtypeStruct((rows, base), jnp.bfloat16),) * len(pieces)
    operands = [place, *pieces, expand_weight, reduce_weight]
    specs = [SMEM_SPEC] + [VMEM_SPEC] * len(pieces) + [HBM_SPEC] * 2
    if pre is None:
        outs = (inner_f32, inner_bf16) + parts
    else:
        outs = (inner_bf16,) + parts
        operands.append(pre)
        specs.append(VMEM_SPEC)
    return pl.pallas_call(
        functools.partial(kernel, blocks=len(pieces) // 2, rows=rows, across=across),
        out_shape=outs,
        in_specs=specs,
        out_specs=tuple(VMEM_SPEC for _ in outs),
        scratch_shapes=[
            pltpu.VMEM((positions + 2 * across, base), jnp.bfloat16),
            pltpu.VMEM((positions + 2 * across, 3 * inner), jnp.bfloat16),
            pltpu.VMEM((3 * base, 3 * inner), jnp.bfloat16),
            pltpu.VMEM((9 * inner, base), jnp.bfloat16),
            pltpu.SemaphoreType.DMA((18,)),
        ],
        compiler_params=granted(
            (*pieces, expand_weight, reduce_weight), outs,
            (
                ((positions + 2 * across, base), jnp.bfloat16),
                ((positions + 2 * across, 3 * inner), jnp.bfloat16),
            ),
            BOTTLENECK_MIB,
        ),
    )(*operands)


def correlate_kernel(place_ref, *refs, count, blocks, across, first_slice, split_left):
    whole = refs[:count]
    own = refs[count : count + 2 * blocks]
    others = refs[count + 2 * blocks : count + 4 * blocks]
    out_ref, joined, shifted = refs[count + 4 * blocks :]
    rows = own[0].shape[0]
    outward = shifted.shape[-1] // 3
    narrow = joined.shape[-1]
    positions = whole[0].shape[0]
    clear_edges(shifted, across)
    inside = pl.ds(across, positions)
    lane = pl.multiple_of(place_ref[2] * narrow, 128)
    for sample in range(count):
        for index in range(2 * blocks):
            start = block_start(place_ref, index % blocks, index // blocks, rows)
            if sample == 0:
                piece = own[index][:, pl.ds(lane, narrow)]
            else:
                first = (first_slice + sample - 1) * rows
                piece = others[index][first : first + rows, :]
            joined[pl.ds(start, rows), :] = piece
        if split_left:
            left, right = joined[...], whole[sample][...]
        else:
            left, right = whole[sample][...], joined[...]
        turned = jnp.transpose(left, (1, 0))
        wide = right.astype(jnp.float32)
        shifted[inside, 0:outward] = from_right(wide, across).astype(jnp.bfloat16)
        shifted[inside, outward : 2 * outward] = right
        shifted[inside, 2 * outward : 3 * outward] = from_left(wide, across).astype(jnp.bfloat16)
        for p in range(3):
            start = (2 - p) * across
            term = plain_dot(turned, shifted[start : start + positions, :])
            for q in range(3):
                piece = term[:, q * outward : (q + 1) * outward]
                if sample == 0:
                    out_ref[p, q] = piece
                else:
                    out_ref[p, q] += piece


def correlate_call(place, whole, own, others, first_slice, split_left, across):
    count = len(whole)
    positions, full_lanes = whole[0].shape
    part_lanes = others[0].shape[1]
    inward, outward = (part_lanes, full_lanes) if split_left else (full_lanes, part_lanes)
    out = jax.ShapeDtypeStruct((3, 3, inward, outward), jnp.float32)
    scratch = (
        ((positions, part_lanes), jnp.bfloat16),
        ((positions + 2 * across, 3 * outward), jnp.bfloat16),
    )
    return pl.pallas_call(
        functools.partial(
            correlate_kernel, count=count, blocks=len(own) // 2, across=across,
            first_slice=first_slice, split_left=split_left,
        ),
        out_shape=out,
        in_specs=[SMEM_SPEC] + [VMEM_SPEC] * (count + len(own) + len(others)),
        out_specs=VMEM_SPEC,
        scratch_shapes=[pltpu.VMEM(*item) for item in scratch],
        compiler_params=granted((*whole, *own, *others), (out,), scratch, CORRELATE_MIB),
        name="correlate_kernel",
    )(place, *whole, *own, *others)


def fetch(source, target, sem):
    copy = pltpu.make_async_copy(source, target, sem)
    copy.start()
    return copy


def store_lane_blocks(place_ref, source, targets):
    narrow = targets[0].shape[1]
    for index, target in enumerate(targets):
        lane = pl.multiple_of((place_ref[2] ^ (index + 1)) * narrow, 128)
        target[...] = source[:, pl.ds(lane, narrow)]


def front_kernel(place_ref, crop_ref, above_ref, below_ref, conv_hbm, down_hbm, *refs, across):
    columns_ref, pre_ref, stacked_ref, coarse_ref = refs[:4]
    slice_refs = refs[4:-5]
    near_ref, grid_ref, conv_buf, down_buf, sems = refs[-5:]
    conv_copy = fetch(conv_hbm, conv_buf, sems.at[0])
    down_copy = fetch(down_hbm, down_buf, sems.at[1])
    positions = crop_ref.shape[0]
    channels = crop_ref.shape[1]
    near_ref[0:across, :] = above_ref[...]
    near_ref[across : across + positions, :] = crop_ref[...]
    near_ref[across + positions :, :] = below_ref[...]
    wide = near_ref[...].astype(jnp.float32)
    columns_ref[:, 0:channels] = from_left(wide, across).astype(jnp.bfloat16)
    columns_ref[:, channels : 2 * channels] = near_ref[...]
    columns_ref[:, 2 * channels :] = from_right(wide, across).astype(jnp.bfloat16)
    left = jnp.concatenate(
        [columns_ref[p * across : p * across + positions, :] for p in range(3)], axis=1
    )
    conv_copy.wait()
    grid_ref[...] = plain_dot(left, conv_buf[...])
    out = grid_ref.shape[1]
    half = across // 2
    for i in range(positions // (2 * across)):
        for a in range(2):
            for b in range(2):
                lane = (2 * a + b) * out
                pre_ref[i * half : (i + 1) * half, lane : lane + out] = grid_ref[
                    pl.ds((2 * i + a) * across + b, half, stride=2), :
                ]
    pre = pre_ref[...]
    stacked = (pre * jax.nn.sigmoid(pre)).astype(jnp.bfloat16)
    stacked_ref[...] = stacked
    down_copy.wait()
    coarse_ref[...] = plain_dot(stacked, down_buf[...]).astype(jnp.bfloat16)
    store_lane_blocks(place_ref, coarse_ref, slice_refs)


def front_call(place, crop, above, below, conv_flat, down_weight, across, samples):
    positions, channels = crop.shape
    out = conv_flat.shape[1]
    low = positions // 4
    base = down_weight.shape[1]
    outs = (
        jax.ShapeDtypeStruct((positions + 2 * across, 3 * channels), jnp.bfloat16),
        jax.ShapeDtypeStruct((low, 4 * out), jnp.float32),
        jax.ShapeDtypeStruct((low, 4 * out), jnp.bfloat16),
        jax.ShapeDtypeStruct((low, base), jnp.bfloat16),
    )
    outs += (jax.ShapeDtypeStruct((low, base // samples), jnp.bfloat16),) * (samples - 1)
    scratch = (
        ((positions + 2 * across, channels), jnp.bfloat16),
        ((positions, out), jnp.float32),
        (conv_flat.shape, jnp.bfloat16),
        (down_weight.shape, jnp.bfloat16),
    )
    return pl.pallas_call(
        functools.partial(front_kernel, across=across),
        out_shape=outs,
        in_specs=[SMEM_SPEC] + [VMEM_SPEC] * 3 + [HBM_SPEC] * 2,
        out_specs=(VMEM_SPEC,) * len(outs),
        scratch_shapes=[pltpu.VMEM(*item) for item in scratch] + [pltpu.SemaphoreType.DMA((2,))],
        compiler_params=granted((crop, above, below), outs, scratch, SMALL_MIB),
        name="front_kernel",
    )(place, crop, above, below, conv_flat, down_weight)


def middle_kernel(place_ref, *refs, count, loss_scale, class_count):
    first_ref, terms = refs[0], refs[1:count]
    coarse_ref, stacked_ref, label_ref, class_turned_ref, up_hbm = refs[count : count + 5]
    bottom_ref, joined_ref, logit_grad_ref, stacked_grad_ref, bottom_grad_ref = refs[
        count + 5 : count + 10
    ]
    slice_refs = refs[count + 10 : -3]
    class_ref, up_ref, sems = refs[-3:]
    up_copy = fetch(up_hbm, up_ref, sems.at[0])
    lanes, channels = class_ref.shape
    class_ref[...] = jnp.zeros(class_ref.shape, class_ref.dtype)
    class_ref[0:class_count, :] = class_turned_ref[...]
    height, across = label_ref.shape[1:]
    half = across // 2
    label_rows = label_ref[0].astype(jnp.float32).astype(jnp.bfloat16)
    row = lax.broadcasted_iota(jnp.int32, (half, across), 0)
    pixel = lax.broadcasted_iota(jnp.int32, (half, across), 1)
    label_columns = [
        transposed_dot((pixel == 2 * row + b).astype(jnp.float32).astype(jnp.bfloat16), label_rows)
        for b in range(2)
    ]
    total = coarse_ref[...].astype(jnp.float32) + add_all(
        first_ref[...], [term[...] for term in terms]
    )
    bottom = total.astype(jnp.bfloat16)
    bottom_ref[...] = bottom
    up_copy.wait()
    joined_pre = plain_dot(bottom, up_ref[...]) + stacked_ref[...].astype(jnp.float32)
    joined_ref[...] = (joined_pre * jax.nn.sigmoid(joined_pre)).astype(jnp.bfloat16)
    slope = silu_slope(joined_pre)
    column = lax.broadcasted_iota(jnp.int32, (joined_pre.shape[0], lanes), 1)
    column_value = column.astype(jnp.float32)
    for a in range(2):
        for b in range(2):
            block = 2 * a + b
            span = slice(block * channels, (block + 1) * channels)
            label = jnp.concatenate(
                [label_columns[b][:, 2 * i + a : 2 * i + a + 1] for i in range(height // 2)],
                axis=0,
            )
            logits = transposed_dot(joined_ref[:, span], class_ref[...])
            powers = jnp.where(column < class_count, jnp.exp(logits), 0.0)
            probability = powers / jnp.sum(powers, axis=-1, keepdims=True)
            onehot = (column_value == label).astype(jnp.float32)
            logit_grad = ((probability - onehot) * loss_scale).astype(jnp.bfloat16)
            logit_grad_ref[:, block * lanes : (block + 1) * lanes] = logit_grad
            joined_grad = plain_dot(logit_grad, class_ref[...])
            stacked_grad_ref[:, span] = (joined_grad * slope[:, span]).astype(jnp.bfloat16)
    bottom_grad_ref[...] = transposed_dot(stacked_grad_ref[...], up_ref[...]).astype(jnp.bfloat16)
    store_lane_blocks(place_ref, bottom_grad_ref, slice_refs)


def middle_call(
    place, first, terms, coarse, stacked, labels, class_turned, up_weight, loss_scale, class_lanes,
    samples,
):
    rows, base = coarse.shape
    wide = stacked.shape[1]
    channels = class_turned.shape[1]
    shapes = (base, wide, wide // channels * class_lanes, wide, base)
    shapes += (base // samples,) * (samples - 1)
    outs = tuple(jax.ShapeDtypeStruct((rows, lanes), jnp.bfloat16) for lanes in shapes)
    operands = (first, *terms, coarse, stacked, labels, class_turned)
    scratch = (((class_lanes, channels), jnp.bfloat16), (up_weight.shape, jnp.bfloat16))
    return pl.pallas_call(
        functools.partial(
            middle_kernel, count=1 + len(terms), loss_scale=loss_scale,
            class_count=class_turned.shape[0],
        ),
        out_shape=outs,
        in_specs=[SMEM_SPEC] + [VMEM_SPEC] * len(operands) + [HBM_SPEC],
        out_specs=(VMEM_SPEC,) * len(outs),
        scratch_shapes=[pltpu.VMEM(*item) for item in scratch] + [pltpu.SemaphoreType.DMA((1,))],
        compiler_params=granted(operands, outs, scratch, SMALL_MIB),
        name="middle_kernel",
    )(place, *operands, up_weight)


def sum_kernel(place_ref, *refs, count, slices):
    first_ref, terms = refs[0], refs[1:count]
    slice_refs = refs[count : count + slices]
    own_ref = refs[count + slices]
    send_refs = refs[count + slices + 1 : -2]
    stack_ref, total_ref = refs[-2:]
    total_ref[...] = add_all(first_ref[...], [term[...] for term in terms]).astype(jnp.bfloat16)
    narrow = own_ref.shape[1]
    own_ref[...] = total_ref[:, pl.ds(pl.multiple_of(place_ref[2] * narrow, 128), narrow)]
    store_lane_blocks(place_ref, total_ref, send_refs)
    for index, source in enumerate(slice_refs):
        rows = source.shape[0]
        stack_ref[index * rows : (index + 1) * rows, :] = source[...]


def sum_call(place, first, terms, slices, samples):
    rows, lanes = first.shape
    block = jax.ShapeDtypeStruct((rows, lanes // samples), jnp.bfloat16)
    stack = jax.ShapeDtypeStruct((len(slices) * slices[0].shape[0], slices[0].shape[1]), jnp.bfloat16)
    outs = (block,) * samples + (stack,)
    operands = (first, *terms, *slices)
    scratch = ((first.shape, jnp.bfloat16),)
    return pl.pallas_call(
        functools.partial(sum_kernel, count=1 + len(terms), slices=len(slices)),
        out_shape=outs,
        in_specs=[SMEM_SPEC] + [VMEM_SPEC] * len(operands),
        out_specs=(VMEM_SPEC,) * len(outs),
        scratch_shapes=[pltpu.VMEM(*item) for item in scratch],
        compiler_params=granted(operands, outs, scratch, SMALL_MIB),
        name="sum_kernel",
    )(place, *operands)


def turned_dot(left, right):
    return lax.dot_general(
        left, right, (((0,), (0,)), ((), ())), preferred_element_type=jnp.float32
    )


def pack_kernel(place_ref, *refs, count, blocks, rows, across):
    first_ref, terms = refs[0], refs[1:count]
    (
        bottom_grad_ref, stacked_ref, stacked_grad_ref, pre_ref, bottom_ref,
        columns_ref, joined_ref, logit_grad_ref, down_hbm,
    ) = refs[count : count + 9]
    targets = refs[count + 9 : -4]
    pack_ref, grid_ref, down_ref, sems = refs[-4:]
    down_copy = fetch(down_hbm, down_ref, sems.at[0])
    lanes = pack_ref.shape[1]
    total = bottom_grad_ref[...].astype(jnp.float32) + add_all(
        first_ref[...], [term[...] for term in terms]
    )
    coarse_grad = total.astype(jnp.bfloat16)
    down_copy.wait()
    hidden_sum = transposed_dot(coarse_grad, down_ref[...]) + stacked_grad_ref[...].astype(
        jnp.float32
    )
    hidden_grad = (hidden_sum * silu_slope(pre_ref[...])).astype(jnp.bfloat16).astype(jnp.float32)
    positions, channels = grid_ref.shape
    half = across // 2
    for i in range(positions // (2 * across)):
        for a in range(2):
            for b in range(2):
                lane = (2 * a + b) * channels
                grid_ref[pl.ds((2 * i + a) * across + b, half, stride=2), :] = hidden_grad[
                    i * half : (i + 1) * half, lane : lane + channels
                ]
    grid = grid_ref[...].astype(jnp.bfloat16)

    def store(value, base):
        rounded = value.astype(jnp.bfloat16)
        times = lanes // value.shape[1]
        part = value.shape[0] // times
        for index in range(times):
            pack_ref[base : base + part, index * value.shape[1] : (index + 1) * value.shape[1]] = (
                rounded[index * part : (index + 1) * part, :]
            )
        return base + part

    base = store(turned_dot(stacked_ref[...], coarse_grad), 0)
    base = store(turned_dot(bottom_ref[...], stacked_grad_ref[...]), base)
    conv_grad = jnp.concatenate(
        [
            turned_dot(columns_ref[p * across : p * across + positions, :], grid)
            for p in range(3)
        ],
        axis=0,
    )
    base = store(conv_grad, base)
    class_grad = None
    class_lanes = logit_grad_ref.shape[1] // (joined_ref.shape[1] // channels)
    for block in range(joined_ref.shape[1] // channels):
        term = turned_dot(
            logit_grad_ref[:, block * class_lanes : (block + 1) * class_lanes],
            joined_ref[:, block * channels : (block + 1) * channels],
        )
        class_grad = term if class_grad is None else class_grad + term
    base = store(class_grad, base)
    if base < pack_ref.shape[0]:
        pack_ref[base:, :] = jnp.zeros((pack_ref.shape[0] - base, lanes), pack_ref.dtype)
    for index, target in enumerate(targets):
        start = block_start(place_ref, index % blocks, index // blocks, rows)
        target[...] = pack_ref[pl.ds(start, rows), :]


def pack_call(place, first, terms, operands, filled, blocks, across):
    lanes = first.shape[1]
    channels = operands[5].shape[1] // 3
    positions = 4 * first.shape[0]
    unit = 32 * blocks
    padded = -(-filled // unit) * unit
    block = jax.ShapeDtypeStruct((padded // (2 * blocks), lanes), jnp.bfloat16)
    return pl.pallas_call(
        functools.partial(
            pack_kernel, count=1 + len(terms), blocks=blocks, rows=padded // (2 * blocks),
            across=across,
        ),
        out_shape=(block,) * (2 * blocks),
        in_specs=[SMEM_SPEC] + [VMEM_SPEC] * (len(terms) + len(operands)) + [HBM_SPEC],
        out_specs=(VMEM_SPEC,) * (2 * blocks),
        scratch_shapes=[
            pltpu.VMEM((padded, lanes), jnp.bfloat16),
            pltpu.VMEM((positions, channels), jnp.float32),
            pltpu.VMEM(operands[-1].shape, jnp.bfloat16),
            pltpu.SemaphoreType.DMA((1,)),
        ],
        compiler_params=granted(
            (first, *terms, *operands), (block,) * (2 * blocks),
            (((padded, lanes), jnp.bfloat16), ((positions, channels), jnp.float32)),
            CORRELATE_MIB,
        ),
        name="pack_kernel",
    )(place, first, *terms, *operands)


def unpack_kernel(place_ref, *refs, blocks, count, shapes):
    pieces = refs[: 2 * blocks]
    out_refs, pack_ref = refs[2 * blocks : -1], refs[-1]
    lanes = pack_ref.shape[1]
    rows = pieces[0].shape[0]
    narrow = lanes // count
    for index, piece in enumerate(pieces):
        start = block_start(place_ref, index % blocks, index // blocks, rows)
        for mask in range(count):
            lane = pl.multiple_of((place_ref[2] ^ mask) * narrow, 128)
            pack_ref[pl.ds(start, rows), pl.ds(lane, narrow)] = piece[
                :, mask * narrow : (mask + 1) * narrow
            ]
    base = 0
    for out_ref, (height, width) in zip(out_refs, shapes):
        times = lanes // width
        part = height // times
        for index in range(times):
            value = pack_ref[base : base + part, index * width : (index + 1) * width]
            kept = min(part, out_ref.shape[0] - index * part)
            if kept > 0:
                out_ref[index * part : index * part + kept, :] = value.astype(jnp.float32)[:kept, :]
        base += part


def unpack_call(place, pieces, count, out_shapes, shapes):
    rows, lanes = pieces[0].shape
    outs = tuple(jax.ShapeDtypeStruct(shape, jnp.float32) for shape in out_shapes)
    scratch = ((rows * len(pieces), lanes), jnp.bfloat16)
    return pl.pallas_call(
        functools.partial(
            unpack_kernel, blocks=len(pieces) // 2, count=count, shapes=shapes
        ),
        out_shape=outs,
        in_specs=[SMEM_SPEC] + [VMEM_SPEC] * len(pieces),
        out_specs=(VMEM_SPEC,) * len(out_shapes),
        scratch_shapes=[pltpu.VMEM(*scratch)],
        compiler_params=granted(pieces, outs, (scratch,), SMALL_MIB),
        name="unpack_kernel",
    )(place, *pieces)


def shift_columns(grid, offset):
    across = grid.shape[-2]
    pads = [(0, 0)] * grid.ndim
    if offset > 0:
        pads[-2] = (0, offset)
        return jnp.pad(lax.slice_in_dim(grid, offset, across, axis=-2 % grid.ndim), pads)
    if offset < 0:
        pads[-2] = (-offset, 0)
        return jnp.pad(lax.slice_in_dim(grid, 0, across + offset, axis=-2 % grid.ndim), pads)
    return grid


def shift_rows(grid, offset):
    height = grid.shape[-3]
    pads = [(0, 0)] * grid.ndim
    if offset > 0:
        pads[-3] = (0, offset)
        return jnp.pad(lax.slice_in_dim(grid, offset, height, axis=-3 % grid.ndim), pads)
    if offset < 0:
        pads[-3] = (-offset, 0)
        return jnp.pad(lax.slice_in_dim(grid, 0, height + offset, axis=-3 % grid.ndim), pads)
    return grid


def taps(grid, sign):
    columns = [shift_columns(grid, sign * (q - 1)) for q in range(3)]
    return [shift_rows(columns[q], sign * (p - 1)) for p in range(3) for q in range(3)]


def conv_in(grid, weight, sign, transposed):
    height, across, channels = grid.shape
    window = jnp.concatenate(taps(grid, sign), axis=-1).reshape(height * across, 9 * channels)
    if transposed:
        flat = jnp.transpose(weight, (0, 1, 3, 2)).reshape(9 * channels, weight.shape[2])
    else:
        flat = weight.reshape(9 * channels, weight.shape[3])
    result = jnp.dot(window, flat, preferred_element_type=jnp.float32)
    return result.reshape(height, across, -1)


def correlate_samples(left, right):
    samples, height, across, inward = left.shape
    outward = right.shape[-1]
    flat = left.reshape(samples * height * across, inward)
    shifted = jnp.concatenate(taps(right, -1), axis=-1).reshape(-1, 9 * outward)
    result = lax.dot_general(
        flat, shifted, (((0,), (0,)), ((), ())), preferred_element_type=jnp.float32
    )
    return jnp.transpose(result.reshape(inward, 3, 3, outward), (1, 2, 0, 3))


def join_blocks(mine, other):
    wide = lax.axis_size("wide")
    own = lax.axis_index("wide")
    stacked = jnp.stack([mine, other], axis=1).reshape((wide,) + mine.shape[1:])
    return stacked[jnp.arange(wide) ^ own].reshape(-1, mine.shape[-1])


def part_blocks(whole):
    wide = lax.axis_size("wide")
    own = lax.axis_index("wide")
    blocks = whole.reshape(wide, -1, whole.shape[-1])[jnp.arange(wide) ^ own]
    halves = blocks.reshape(wide // 2, 2, -1, whole.shape[-1])
    return [halves[r, half] for half in range(2) for r in range(wide // 2)]


def step(
    features,
    labels,
    conv_weight,
    down_weight,
    expand_weight,
    reduce_weight,
    up_weight,
    class_weight,
):
    crop_rows = features[0]
    height, across, channels = crop_rows.shape
    wide = lax.axis_size("wide")
    samples = lax.axis_size("samp")
    chips = chip_count()
    pixel_count = wide * samples * height * across
    loss_scale = 8.0 / math.sqrt(pixel_count)
    own = lax.axis_index("wide")
    place = jnp.stack([own % 2, own // 2, lax.axis_index("samp")]).astype(jnp.int32)
    base = down_weight.shape[1]
    inner = expand_weight.shape[-1]
    narrow = base // samples
    low_rows, low_across = height // 2, across // 2
    block_rows = low_rows * low_across
    grid = (wide * low_rows, low_across)
    class_count = class_weight.shape[1]
    class_lanes = 128
    own_kernels = inner % 128 == 0 and narrow % 128 == 0

    forward = [(i, i + 1) for i in range(wide - 1)]
    backward = [(target, source) for source, target in forward]
    above = lax.ppermute(crop_rows[height - 1], "wide", forward)
    below = lax.ppermute(crop_rows[0], "wide", backward)
    columns, hidden_pre, stacked, coarse, *coarse_sends = front_call(
        place, crop_rows.reshape(height * across, channels), above, below,
        conv_weight.reshape(9 * channels, -1), down_weight, across, samples,
    )
    coarse_mine = gather_chips(coarse)
    coarse_other = swap_cores(coarse_mine)
    if own_kernels:
        expand_pre, expanded, *partial = bottleneck_call(
            forward_kernel, place, coarse_mine + coarse_other, expand_weight, reduce_weight,
            None, low_across,
        )
    else:
        coarse_all = join_blocks(jnp.stack(coarse_mine), jnp.stack(coarse_other))
        expand_grid = conv_in(coarse_all.reshape(*grid, base), expand_weight, 1, False)
        expanded_grid = jax.nn.silu(expand_grid).astype(jnp.bfloat16)
        partial = conv_in(expanded_grid, reduce_weight, 1, False).astype(jnp.bfloat16)
        partial = part_blocks(partial.reshape(-1, base))
        expanded = expanded_grid.reshape(-1, inner)
    coarse_slices = send_samples(coarse_sends)
    expanded_samples = [expanded] + send_samples([expanded] * (samples - 1))
    first, *terms = scatter_chips(partial[:chips], partial[chips:])
    bottom, joined, logit_grad, stacked_grad, bottom_grad, *bottom_sends = middle_call(
        place, first, terms, coarse, stacked, labels, class_weight.T, up_weight, loss_scale,
        class_lanes, samples,
    )
    bottom_mine = gather_chips(bottom_grad)
    bottom_other = swap_cores(bottom_mine)
    if own_kernels:
        expanded_grad, *back = bottleneck_call(
            backward_kernel, place, bottom_mine + bottom_other, expand_weight, reduce_weight,
            expand_pre, low_across,
        )
    else:
        bottom_all = join_blocks(jnp.stack(bottom_mine), jnp.stack(bottom_other))
        expanded_back = conv_in(bottom_all.reshape(*grid, base), reduce_weight, -1, True)
        grad_grid = (expanded_back * silu_slope(expand_grid)).astype(jnp.bfloat16)
        back = conv_in(grad_grid, expand_weight, -1, True).astype(jnp.bfloat16)
        back = part_blocks(back.reshape(-1, base))
        expanded_grad = grad_grid.reshape(-1, inner)
    bottom_slices = send_samples(bottom_sends)
    grad_samples = [expanded_grad] + send_samples([expanded_grad] * (samples - 1))
    first, *terms = scatter_chips(back[:chips], back[chips:])

    conv_out = conv_weight.shape[-1]
    shapes = (
        (down_weight.shape[0], base),
        (base, up_weight.shape[1]),
        (9 * channels, conv_out),
        (class_lanes, conv_out),
    )
    filled = sum(rows * lanes for rows, lanes in shapes) // base
    packed = pack_call(
        place, first, terms,
        (
            bottom_grad, stacked, stacked_grad, hidden_pre, bottom,
            columns, joined, logit_grad, down_weight,
        ),
        filled, chips, across,
    )
    first, *terms = scatter_chips(packed[:chips], packed[chips:])
    own_part, *part_sends, slices = sum_call(
        place, first, terms, coarse_slices + bottom_slices, samples
    )
    parts = send_samples(part_sends)
    slices_mine = gather_chips(slices)
    slices_other = swap_cores(slices_mine)
    total = add_all(own_part, parts).astype(jnp.bfloat16)
    own_total = jnp.concatenate(
        [total] + send_samples([total] * (samples - 1)), axis=1
    )
    total_mine = gather_chips(own_total)
    total_other = swap_cores(total_mine)
    out_shapes = shapes[:3] + ((class_count, conv_out),)
    down_total, up_total, conv_total, class_total = unpack_call(
        place, total_mine + total_other, samples, out_shapes, shapes,
    )

    if own_kernels:
        reduce_grad = correlate_call(
            place, expanded_samples, bottom_mine + bottom_other, slices_mine + slices_other,
            samples - 1, False, low_across,
        )
        expand_grad = correlate_call(
            place, grad_samples, coarse_mine + coarse_other, slices_mine + slices_other,
            0, True, low_across,
        )
    else:

        def join_samples(mine, other, first_slice):
            sample = lax.axis_index("samp")
            mine_all = jnp.stack(mine)
            other_all = jnp.stack(other)
            joined_ = [
                join_blocks(lane_block(mine_all, sample, samples), lane_block(other_all, sample, samples))
            ]
            for i in range(samples - 1):
                span = slice((first_slice + i) * block_rows, (first_slice + i + 1) * block_rows)
                joined_.append(
                    join_blocks(
                        jnp.stack([item[span] for item in slices_mine]),
                        jnp.stack([item[span] for item in slices_other]),
                    )
                )
            return jnp.stack(joined_).reshape(samples, *grid, narrow)

        reduce_grad = correlate_samples(
            jnp.stack(expanded_samples).reshape(samples, *grid, inner),
            join_samples(bottom_mine, bottom_other, samples - 1),
        )
        expand_grad = correlate_samples(
            join_samples(coarse_mine, coarse_other, 0),
            jnp.stack(grad_samples).reshape(samples, *grid, inner),
        )
    return (
        conv_total.reshape(conv_weight.shape),
        down_total,
        expand_grad,
        reduce_grad,
        up_total,
        class_total.T,
    )


def solution(mesh):
    return jax.shard_map(
        step,
        mesh=mesh,
        in_specs=(
            P("samp", "wide", None, None),
            P("samp", "wide", None),
            P(),
            P(),
            P(None, None, None, "wide"),
            P(None, None, "wide", None),
            P(),
            P(),
        ),
        out_specs=(
            P(),
            P(),
            P(None, None, "samp", "wide"),
            P(None, None, "wide", "samp"),
            P(),
            P(),
        ),
        check_vma=False,
    )
```

time: 502 us -> 263 us (0.52)
  waiting for transfers between devices: 277 us -> 126 us
  starting transfers between devices: 8.02 us -> 81.1 us
  blocking collectives: 66.1 us -> 0 us
  local copies, waits for them, and re-layouts: 66.8 us -> 8.54 us
  matrix products: 53 us -> 0 us
  Pallas kernels: 0 us -> 45.1 us
  other arithmetic: 15.1 us -> 0.75 us
  between operations: 14.5 us -> 0.93 us
    psum x1 -> x0, waiting for transfers between devices: 150 us -> none  [local(): lax.psum((conv_grad, down_grad, up_grad, class_grad), ('wide', 'samp'))]
    ppermute x2 -> x69, waiting for transfers between devices: 3.88 us -> 126 us  [the longest x67 125 us: swap(): return lax.ppermute(values, axis, [(i, i ^ mask) for i in range(count)])]
    ppermute x2 -> x69, starting transfers between devices: 3.68 us -> 81.1 us  [the longest x67 76.8 us: swap(): return lax.ppermute(values, axis, [(i, i ^ mask) for i in range(count)])]
    reduce_scatter x2 -> x0, waiting for transfers between devices: 71.5 us -> none  [the longest x1 71.5 us: local(): lax.psum_scatter(reduce_grad.astype(jnp.bfloat16), 'samp', scatter_dimens...]
    dot_general x17 -> x0, matrix products: 53 us -> none  [the longest x2 15.9 us: conv_padded(): jnp.dot(flattened, stacked, preferred_element_type=jnp.float32)]
    pallas_call x0 -> x9, Pallas kernels: none -> 45.1 us  [the longest x2 22.2 us: bottleneck_call(): pl.pallas_call(functools.partial(kernel, blocks=len(pieces) // 2, rows=ro...]
    psum x1 -> x0, blocking collectives: 42.5 us -> none  [local(): lax.psum((conv_grad, down_grad, up_grad, class_grad), ('wide', 'samp'))]
    all_gather x2 -> x0, waiting for transfers between devices: 38.2 us -> none  [collect(): lax.all_gather(values, 'wide', axis=0, tiled=True)]
  transfers between devices with their start and end apart: 8 -> 69, of which waited for: 6 -> 31; matrix products, arithmetic and copies ran while one was open for 12% -> 0% of each run, Pallas kernels for 0% -> 5%
where the time goes in v1:
time: 263 us; the launch traced here: 262 us
  waiting for transfers between devices  126 us (48%)
  starting transfers between devices  81.1 us (31%)
  Pallas kernels  45.1 us (17%)
  local copies, waits for them, and re-layouts  8.54 us (3%)
    ppermute x67, waiting for transfers between devices, swap(): return lax.ppermute(values, axis, [(i, i ^ mask) for i in range(count)])  125 us
    ppermute x67, starting transfers between devices, swap(): return lax.ppermute(values, axis, [(i, i ^ mask) for i in range(count)])  76.8 us
    pallas_call x2, Pallas kernels, bottleneck_call(): pl.pallas_call(functools.partial(kernel, blocks=len(pieces) // 2, rows=ro...  22.2 us
    pallas_call x2, Pallas kernels, correlate_call(): pl.pallas_call(functools.partial(correlate_kernel, count=count, blocks=le...  11.9 us
    unnamed x22, local copies, waits for them, and re-layouts  7.78 us
  transfers between devices with their start and end apart: 69, of which 31 were waited for; matrix products, arithmetic and copies ran while one was open for 0% of the time, Pallas kernels for 5%

profile of v1, /device:TPU:0, one launch (start us, length us, event | category | flops | bytes accessed | tf_op | source)
XLA Modules:
  0.0 262.2 jit_solution(13318757885988524114)
XLA Ops:
  11.5 5.9 %collective-permute-start.4 = (bf16[96,1024]{1,0:T(8,128)(2,1)S(1)}, bf16[96,1024]{1,0:T(8,128)(2,1)S(1)}, u32[]{:S(2)}, u32[]{:S(2)}) collective-permute-start(bf16[96,1024]{1,0:T(8,128)(2,1)S(1)} %get-tuple-element.57.refs_0_.refs_5_.refs_4_), channel_id=1, source_target_pairs={{0,24},{4,28},{8,16},{12,20},{16,8},{20,12},{24,0},{28,4},{1,25},{... | collective-permute-start | bytes 589832 | tf_op jit(solution)/shard_map/ppermute | solution.py:14
  19.7 3.5 %collective-permute-done.4.refs_3_.refs_7_ = bf16[96,1024]{1,0:T(8,128)(2,1)S(1)} collective-permute-done((bf16[96,1024]{1,0:T(8,128)(2,1)S(1)}, bf16[96,1024]{1,0:T(8,128)(2,1)S(1)}, u32[]{:S(2)}, u32[]{:S(2)}) %collective-permute-start.4) | collective-permute-done | bytes 196640 | tf_op jit(solution)/shard_map/ppermute | solution.py:14
  32.6 11.5 %shard_map.127 = (f32[768,256]{1,0:T(8,128)S(1)}, bf16[768,256]{1,0:T(8,128)(2,1)S(1)}, bf16[96,1024]{1,0:T(8,128)(2,1)S(1)}, bf16[96,1024]{1,0:T(8,128)(2,1)S(1...) custom-call(s32[3]{0:T(128)S(1)} %pad_add_fusion.place_ref, ...), custom_call_target="tpu_custom_call" | custom-call | tf_op jit(solution)/shard_map/pallas_call | solution.py:280
  49.7 3.8 %collective-permute-done.11.refs_2_ = bf16[96,1024]{1,0:T(8,128)(2,1)S(1)} collective-permute-done((bf16[96,1024]{1,0:T(8,128)(2,1)S(1)}, bf16[96,1024]{1,0:T(8,128)(2,1)S(1)}, u32[]{:S(2)}, u32[]{:S(2)}) %collective-permute-start.11) | collective-permute-done | bytes 196640 | tf_op jit(solution)/shard_map/ppermute | solution.py:14
  53.5 5.1 %collective-permute-done.13.refs_3_ = bf16[96,1024]{1,0:T(8,128)(2,1)S(1)} collective-permute-done((bf16[96,1024]{1,0:T(8,128)(2,1)S(1)}, bf16[96,1024]{1,0:T(8,128)(2,1)S(1)}, u32[]{:S(2)}, u32[]{:S(2)}) %collective-permute-start.13) | collective-permute-done | bytes 196640 | tf_op jit(solution)/shard_map/ppermute | solution.py:14
  64.8 5.0 %collective-permute-done.18.refs_3_.refs_7_ = bf16[96,1024]{1,0:T(8,128)(2,1)S(1)} collective-permute-done((bf16[96,1024]{1,0:T(8,128)(2,1)S(1)}, bf16[96,1024]{1,0:T(8,128)(2,1)S(1)}, u32[]{:S(2)}, u32[]{:S(2)}) %collective-permute-start.18) | collective-permute-done | bytes 196640 | tf_op jit(solution)/shard_map/ppermute | solution.py:14
  73.7 10.7 %shard_map.128 = (bf16[768,256]{1,0:T(8,128)(2,1)S(1)}, bf16[96,1024]{1,0:T(8,128)(2,1)S(1)}, bf16[96,1024]{1,0:T(8,128)(2,1)S(1)}, bf16[96,1024]{1,0:T(8,128)(2...) custom-call(s32[3]{0:T(128)S(1)} %pad_add_fusion.place_ref, ...), custom_call_target="tpu_custom_call" | custom-call | tf_op jit(solution)/shard_map/pallas_call | solution.py:280
  89.9 4.0 %collective-permute-done.25.refs_2_ = bf16[96,1024]{1,0:T(8,128)(2,1)S(1)} collective-permute-done((bf16[96,1024]{1,0:T(8,128)(2,1)S(1)}, bf16[96,1024]{1,0:T(8,128)(2,1)S(1)}, u32[]{:S(2)}, u32[]{:S(2)}) %collective-permute-start.25) | collective-permute-done | bytes 196640 | tf_op jit(solution)/shard_map/ppermute | solution.py:14
  93.9 4.2 %collective-permute-done.27.refs_3_ = bf16[96,1024]{1,0:T(8,128)(2,1)S(1)} collective-permute-done((bf16[96,1024]{1,0:T(8,128)(2,1)S(1)}, bf16[96,1024]{1,0:T(8,128)(2,1)S(1)}, u32[]{:S(2)}, u32[]{:S(2)}) %collective-permute-start.27) | collective-permute-done | bytes 196640 | tf_op jit(solution)/shard_map/ppermute | solution.py:14
  114.8 3.9 %collective-permute-done.39.refs_7_ = bf16[96,256]{1,0:T(8,128)(2,1)S(1)} collective-permute-done((bf16[96,256]{1,0:T(8,128)(2,1)S(1)}, bf16[96,256]{1,0:T(8,128)(2,1)S(1)}, u32[]{:S(2)}, u32[]{:S(2)}) %collective-permute-start.39) | collective-permute-done | bytes 49184 | tf_op jit(solution)/shard_map/ppermute | solution.py:14
  118.7 4.1 %collective-permute-done.40.refs_8_ = bf16[96,256]{1,0:T(8,128)(2,1)S(1)} collective-permute-done((bf16[96,256]{1,0:T(8,128)(2,1)S(1)}, bf16[96,256]{1,0:T(8,128)(2,1)S(1)}, u32[]{:S(2)}, u32[]{:S(2)}) %collective-permute-start.40) | collective-permute-done | bytes 49184 | tf_op jit(solution)/shard_map/ppermute | solution.py:14
  124.0 5.1 %collective-permute-done.41.refs_9_ = bf16[96,256]{1,0:T(8,128)(2,1)S(1)} collective-permute-done((bf16[96,256]{1,0:T(8,128)(2,1)S(1)}, bf16[96,256]{1,0:T(8,128)(2,1)S(1)}, u32[]{:S(2)}, u32[]{:S(2)}) %collective-permute-start.41) | collective-permute-done | bytes 49184 | tf_op jit(solution)/shard_map/ppermute | solution.py:14
  131.3 4.3 %collective-permute-done.42.refs_10_ = bf16[96,256]{1,0:T(8,128)(2,1)S(1)} collective-permute-done((bf16[96,256]{1,0:T(8,128)(2,1)S(1)}, bf16[96,256]{1,0:T(8,128)(2,1)S(1)}, u32[]{:S(2)}, u32[]{:S(2)}) %collective-permute-start.42) | collective-permute-done | bytes 49184 | tf_op jit(solution)/shard_map/ppermute | solution.py:14
  144.3 4.9 %collective-permute-done.43 = bf16[160,256]{1,0:T(8,128)(2,1)S(1)} collective-permute-done((bf16[160,256]{1,0:T(8,128)(2,1)S(1)}, bf16[160,256]{1,0:T(8,128)(2,1)S(1)}, u32[]{:S(2)}, u32[]{:S(2)}) %collective-permute-start.43) | collective-permute-done | bytes 81952 | tf_op jit(solution)/shard_map/ppermute | solution.py:14
  151.6 22.6 %collective-permute-done.44 = bf16[160,256]{1,0:T(8,128)(2,1)S(1)} collective-permute-done((bf16[160,256]{1,0:T(8,128)(2,1)S(1)}, bf16[160,256]{1,0:T(8,128)(2,1)S(1)}, u32[]{:S(2)}, u32[]{:S(2)}) %collective-permute-start.44) | collective-permute-done | bytes 81952 | tf_op jit(solution)/shard_map/ppermute | solution.py:14
  179.0 15.6 %collective-permute-done.67.refs_2_ = bf16[768,256]{1,0:T(8,128)(2,1)S(1)} collective-permute-done((bf16[768,256]{1,0:T(8,128)(2,1)S(1)}, bf16[768,256]{1,0:T(8,128)(2,1)S(1)}, u32[]{:S(2)}, u32[]{:S(2)}) %collective-permute-start.67) | collective-permute-done | bytes 393248 | tf_op jit(solution)/shard_map/ppermute | solution.py:14
  194.6 16.5 %collective-permute-start.46 = (bf16[160,256]{1,0:T(8,128)(2,1)S(1)}, bf16[160,256]{1,0:T(8,128)(2,1)S(1)}, u32[]{:S(2)}, u32[]{:S(2)}) collective-permute-start(bf16[160,256]{1,0:T(8,128)(2,1)S(1)} %add_convert_fusion.9), channel_id=1, source_target_pairs={{0,1},{1,0},{2,3},{3,2},{4,5},{5,4},{6,7},{7,6},{8,9},{9,8},{10,11... | collective-permute-start | bytes 245768 | tf_op jit(solution)/shard_map/ppermute | solution.py:14
  219.6 4.8 %collective-permute-done.61.refs_15_ = bf16[576,256]{1,0:T(8,128)(2,1)S(1)} collective-permute-done((bf16[576,256]{1,0:T(8,128)(2,1)S(1)}, bf16[576,256]{1,0:T(8,128)(2,1)S(1)}, u32[]{:S(2)}, u32[]{:S(2)}) %collective-permute-start.61) | collective-permute-done | bytes 294944 | tf_op jit(solution)/shard_map/ppermute | solution.py:14
  225.4 9.7 %collective-permute-done.60.refs_14_ = bf16[576,256]{1,0:T(8,128)(2,1)S(1)} collective-permute-done((bf16[576,256]{1,0:T(8,128)(2,1)S(1)}, bf16[576,256]{1,0:T(8,128)(2,1)S(1)}, u32[]{:S(2)}, u32[]{:S(2)}) %collective-permute-start.60) | collective-permute-done | bytes 294944 | tf_op jit(solution)/shard_map/ppermute | solution.py:14
  238.1 4.0 %collective-permute-done.50.refs_2_ = bf16[160,1024]{1,0:T(8,128)(2,1)S(1)} collective-permute-done((bf16[160,1024]{1,0:T(8,128)(2,1)S(1)}, bf16[160,1024]{1,0:T(8,128)(2,1)S(1)}, u32[]{:S(2)}, u32[]{:S(2)}) %collective-permute-start.50) | collective-permute-done | bytes 327712 | tf_op jit(solution)/shard_map/ppermute | solution.py:14
  243.1 5.9 %correlate_kernel.3 = f32[3,3,256,256]{3,2,1,0:T(8,128)} custom-call(s32[3]{0:T(128)S(1)} %pad_add_fusion.place_ref, bf16[768,256]{1,0:T(8,128)(2,1)S(1)} %get-tuple-element.105.refs_0_, bf16[768,256]{1,0:T(8,128)(2,1)S(1)} %collective-permute-done.66.refs_1_, bf16[768,256]{1,0:T(8,128)(2,1)S(1)} %collective-permute-done.67.refs_2_, ...), custom_call_target="tpu_custom_call" | custom-call | tf_op jit(solution)/shard_map/correlate_kernel/pallas_call | solution.py:354
  249.0 4.1 %collective-permute-done.56.refs_1_ = bf16[768,256]{1,0:T(8,128)(2,1)S(1)} collective-permute-done((bf16[768,256]{1,0:T(8,128)(2,1)S(1)}, bf16[768,256]{1,0:T(8,128)(2,1)S(1)}, u32[]{:S(2)}, u32[]{:S(2)}) %collective-permute-start.56) | collective-permute-done | bytes 393248 | tf_op jit(solution)/shard_map/ppermute | solution.py:14
  253.1 6.0 %correlate_kernel.2 = f32[3,3,256,256]{3,2,1,0:T(8,128)} custom-call(s32[3]{0:T(128)S(1)} %pad_add_fusion.place_ref, bf16[768,256]{1,0:T(8,128)(2,1)S(1)} %get-tuple-element.103.refs_0_, bf16[768,256]{1,0:T(8,128)(2,1)S(1)} %collective-permute-done.56.refs_1_, bf16[768,256]{1,0:T(8,128)(2,1)S(1)} %collective-permute-done.57.refs_2_, ...), custom_call_target="tpu_custom_call" | custom-call | tf_op jit(solution)/shard_map/correlate_kernel/pallas_call | solution.py:354
  259.1 3.2 %unpack_kernel.1 = (f32[512,1024]{1,0:T(8,128)}, f32[1024,512]{1,0:T(8,128)}, f32[1152,128]{1,0:T(8,128)}, f32[9,128]{1,0:T(8,128)}) custom-call(s32[3]{0:T(128)S(1)} %pad_add_fusion.place_ref, bf16[160,1024]{1,0:T(8,128)(2,1)S(1)} %pad_maximum_fusion.refs_0_, bf16[160,1024]{1,0:T(8,128)(2,1)S(1)} %collective-permute-done.49.refs_1_, ...), custom_call_target="tpu_custom_call" | custom-call | tf_op jit(solution)/shard_map/unpack_kernel/pallas_call | solution.py:689
  (158 shorter events, 93.0 us)
Async XLA Ops:
  11.5 11.7 %collective-permute-start.4 = (bf16[96,1024]{1,0:T(8,128)(2,1)S(1)}, bf16[96,1024]{1,0:T(8,128)(2,1)S(1)}, u32[]{:S(2)}, u32[]{:S(2)}) collective-permute-start(bf16[96,1024]{1,0:T(8,128)(2,1)S(1)} %get-tuple-element.57.refs_0_.refs_5_.refs_4_), channel_id=1, source_target_pairs={{0,24},{4,28},{8,16},{12,20},{16,8},{20,12},{24,0},{28,4},{1,25},{... | collective-permute-start | bytes 589832 | tf_op jit(solution)/shard_map/ppermute | solution.py:14
  102.6 35.2 %collective-permute-start.30 = (bf16[160,1024]{1,0:T(8,128)(2,1)S(1)}, bf16[160,1024]{1,0:T(8,128)(2,1)S(1)}, u32[]{:S(2)}, u32[]{:S(2)}) collective-permute-start(bf16[160,1024]{1,0:T(8,128)(2,1)S(1)} %get-tuple-element.84), channel_id=1, source_target_pairs={{0,4},{4,0},{8,12},{12,8},{16,20},{20,16},{24,28},{28,24},{1,5},{5... | collective-permute-start | bytes 983048 | tf_op jit(solution)/shard_map/ppermute | solution.py:14
  103.2 34.6 %collective-permute-start.32 = (bf16[160,1024]{1,0:T(8,128)(2,1)S(1)}, bf16[160,1024]{1,0:T(8,128)(2,1)S(1)}, u32[]{:S(2)}, u32[]{:S(2)}) collective-permute-start(bf16[160,1024]{1,0:T(8,128)(2,1)S(1)} %add_convert_fusion.2), channel_id=1, source_target_pairs={{0,8},{4,12},{8,0},{12,4},{16,24},{20,28},{24,16},{28,20},{1,9},{5... | collective-permute-start | bytes 983048 | tf_op jit(solution)/shard_map/ppermute | solution.py:14
  104.5 33.3 %collective-permute-start.34 = (bf16[160,1024]{1,0:T(8,128)(2,1)S(1)}, bf16[160,1024]{1,0:T(8,128)(2,1)S(1)}, u32[]{:S(2)}, u32[]{:S(2)}) collective-permute-start(bf16[160,1024]{1,0:T(8,128)(2,1)S(1)} %add_convert_fusion.1), channel_id=1, source_target_pairs={{0,16},{4,20},{8,24},{12,28},{16,0},{20,4},{24,8},{28,12},{1,17},{... | collective-permute-start | bytes 983048 | tf_op jit(solution)/shard_map/ppermute | solution.py:14
  105.7 32.2 %collective-permute-start.36 = (bf16[160,1024]{1,0:T(8,128)(2,1)S(1)}, bf16[160,1024]{1,0:T(8,128)(2,1)S(1)}, u32[]{:S(2)}, u32[]{:S(2)}) collective-permute-start(bf16[160,1024]{1,0:T(8,128)(2,1)S(1)} %add_convert_fusion), channel_id=1, source_target_pairs={{0,24},{4,28},{8,16},{12,20},{16,8},{20,12},{24,0},{28,4},{1,25},{... | collective-permute-start | bytes 983048 | tf_op jit(solution)/shard_map/ppermute | solution.py:14
  135.6 41.4 %collective-permute-start.68 = (bf16[768,256]{1,0:T(8,128)(2,1)S(1)}, bf16[768,256]{1,0:T(8,128)(2,1)S(1)}, u32[]{:S(2)}, u32[]{:S(2)}) collective-permute-start(bf16[768,256]{1,0:T(8,128)(2,1)S(1)} %get-tuple-element.105.refs_0_), channel_id=1, source_target_pairs={{0,3},{1,2},{2,1},{3,0},{4,7},{5,6},{6,5},{7,4},{8,11},{9,10},{10,... | collective-permute-start | bytes 1179656 | tf_op jit(solution)/shard_map/ppermute | solution.py:14
  139.3 34.9 %collective-permute-start.44 = (bf16[160,256]{1,0:T(8,128)(2,1)S(1)}, bf16[160,256]{1,0:T(8,128)(2,1)S(1)}, u32[]{:S(2)}, u32[]{:S(2)}) collective-permute-start(bf16[160,256]{1,0:T(8,128)(2,1)S(1)} %get-tuple-element.99), channel_id=1, source_target_pairs={{0,2},{1,3},{2,0},{3,1},{4,6},{5,7},{6,4},{7,5},{8,10},{9,11},{10,... | collective-permute-start | bytes 245768 | tf_op jit(solution)/shard_map/ppermute | solution.py:14
  141.1 35.0 %collective-permute-start.45 = (bf16[160,256]{1,0:T(8,128)(2,1)S(1)}, bf16[160,256]{1,0:T(8,128)(2,1)S(1)}, u32[]{:S(2)}, u32[]{:S(2)}) collective-permute-start(bf16[160,256]{1,0:T(8,128)(2,1)S(1)} %get-tuple-element.100), channel_id=1, source_target_pairs={{0,3},{1,2},{2,1},{3,0},{4,7},{5,6},{6,5},{7,4},{8,11},{9,10},{10,... | collective-permute-start | bytes 245768 | tf_op jit(solution)/shard_map/ppermute | solution.py:14
  143.3 51.2 %collective-permute-start.67 = (bf16[768,256]{1,0:T(8,128)(2,1)S(1)}, bf16[768,256]{1,0:T(8,128)(2,1)S(1)}, u32[]{:S(2)}, u32[]{:S(2)}) collective-permute-start(bf16[768,256]{1,0:T(8,128)(2,1)S(1)} %get-tuple-element.105.refs_0_), channel_id=1, source_target_pairs={{0,2},{1,3},{2,0},{3,1},{4,6},{5,7},{6,4},{7,5},{8,10},{9,11},{10,... | collective-permute-start | bytes 1179656 | tf_op jit(solution)/shard_map/ppermute | solution.py:14
  149.1 65.9 %collective-permute-start.66 = (bf16[768,256]{1,0:T(8,128)(2,1)S(1)}, bf16[768,256]{1,0:T(8,128)(2,1)S(1)}, u32[]{:S(2)}, u32[]{:S(2)}) collective-permute-start(bf16[768,256]{1,0:T(8,128)(2,1)S(1)} %get-tuple-element.105.refs_0_), channel_id=1, source_target_pairs={{0,1},{1,0},{2,3},{3,2},{4,5},{5,4},{6,7},{7,6},{8,9},{9,8},{10,11... | collective-permute-start | bytes 1179656 | tf_op jit(solution)/shard_map/ppermute | solution.py:14
  174.2 42.3 %collective-permute-start.58 = (bf16[768,256]{1,0:T(8,128)(2,1)S(1)}, bf16[768,256]{1,0:T(8,128)(2,1)S(1)}, u32[]{:S(2)}, u32[]{:S(2)}) collective-permute-start(bf16[768,256]{1,0:T(8,128)(2,1)S(1)} %get-tuple-element.103.refs_0_), channel_id=1, source_target_pairs={{0,3},{1,2},{2,1},{3,0},{4,7},{5,6},{6,5},{7,4},{8,11},{9,10},{10,... | collective-permute-start | bytes 1179656 | tf_op jit(solution)/shard_map/ppermute | solution.py:14
  176.0 41.8 %collective-permute-start.57 = (bf16[768,256]{1,0:T(8,128)(2,1)S(1)}, bf16[768,256]{1,0:T(8,128)(2,1)S(1)}, u32[]{:S(2)}, u32[]{:S(2)}) collective-permute-start(bf16[768,256]{1,0:T(8,128)(2,1)S(1)} %get-tuple-element.103.refs_0_), channel_id=1, source_target_pairs={{0,2},{1,3},{2,0},{3,1},{4,6},{5,7},{6,4},{7,5},{8,10},{9,11},{10,... | collective-permute-start | bytes 1179656 | tf_op jit(solution)/shard_map/ppermute | solution.py:14
  177.0 17.6 %collective-permute-start.48 = (bf16[160,256]{1,0:T(8,128)(2,1)S(1)}, bf16[160,256]{1,0:T(8,128)(2,1)S(1)}, u32[]{:S(2)}, u32[]{:S(2)}) collective-permute-start(bf16[160,256]{1,0:T(8,128)(2,1)S(1)} %add_convert_fusion.9), channel_id=1, source_target_pairs={{0,3},{1,2},{2,1},{3,0},{4,7},{5,6},{6,5},{7,4},{8,11},{9,10},{10,... | collective-permute-start | bytes 245768 | tf_op jit(solution)/shard_map/ppermute | solution.py:14
  194.6 16.8 %collective-permute-start.47 = (bf16[160,256]{1,0:T(8,128)(2,1)S(1)}, bf16[160,256]{1,0:T(8,128)(2,1)S(1)}, u32[]{:S(2)}, u32[]{:S(2)}) collective-permute-start(bf16[160,256]{1,0:T(8,128)(2,1)S(1)} %add_convert_fusion.9), channel_id=1, source_target_pairs={{0,2},{1,3},{2,0},{3,1},{4,6},{5,7},{6,4},{7,5},{8,10},{9,11},{10,... | collective-permute-start | bytes 245768 | tf_op jit(solution)/shard_map/ppermute | solution.py:14
  194.6 18.9 %collective-permute-start.46 = (bf16[160,256]{1,0:T(8,128)(2,1)S(1)}, bf16[160,256]{1,0:T(8,128)(2,1)S(1)}, u32[]{:S(2)}, u32[]{:S(2)}) collective-permute-start(bf16[160,256]{1,0:T(8,128)(2,1)S(1)} %add_convert_fusion.9), channel_id=1, source_target_pairs={{0,1},{1,0},{2,3},{3,2},{4,5},{5,4},{6,7},{7,6},{8,9},{9,8},{10,11... | collective-permute-start | bytes 245768 | tf_op jit(solution)/shard_map/ppermute | solution.py:14
  215.0 22.5 %collective-permute-start.51 = (bf16[160,1024]{1,0:T(8,128)(2,1)S(1)}, bf16[160,1024]{1,0:T(8,128)(2,1)S(1)}, u32[]{:S(2)}, u32[]{:S(2)}) collective-permute-start(bf16[160,1024]{1,0:T(8,128)(2,1)S(1)} %pad_maximum_fusion.refs_0_), channel_id=1, source_target_pairs={{0,24},{4,28},{8,16},{12,20},{16,8},{20,12},{24,0},{28,4},{1,25},{... | collective-permute-start | bytes 983048 | tf_op jit(solution)/shard_map/ppermute | solution.py:14
  216.5 18.6 %collective-permute-start.60 = (bf16[576,256]{1,0:T(8,128)(2,1)S(1)}, bf16[576,256]{1,0:T(8,128)(2,1)S(1)}, u32[]{:S(2)}, u32[]{:S(2)}) collective-permute-start(bf16[576,256]{1,0:T(8,128)(2,1)S(1)} %get-tuple-element.104.refs_12_), channel_id=1, source_target_pairs={{0,16},{4,20},{8,24},{12,28},{16,0},{20,4},{24,8},{28,12},{1,17},{... | collective-permute-start | bytes 884744 | tf_op jit(solution)/shard_map/ppermute | solution.py:14
  217.9 19.7 %collective-permute-start.59 = (bf16[576,256]{1,0:T(8,128)(2,1)S(1)}, bf16[576,256]{1,0:T(8,128)(2,1)S(1)}, u32[]{:S(2)}, u32[]{:S(2)}) collective-permute-start(bf16[576,256]{1,0:T(8,128)(2,1)S(1)} %get-tuple-element.104.refs_12_), channel_id=1, source_target_pairs={{0,8},{4,12},{8,0},{12,4},{16,24},{20,28},{24,16},{28,20},{1,9},{5... | collective-permute-start | bytes 884744 | tf_op jit(solution)/shard_map/ppermute | solution.py:14
  218.6 23.4 %collective-permute-start.50 = (bf16[160,1024]{1,0:T(8,128)(2,1)S(1)}, bf16[160,1024]{1,0:T(8,128)(2,1)S(1)}, u32[]{:S(2)}, u32[]{:S(2)}) collective-permute-start(bf16[160,1024]{1,0:T(8,128)(2,1)S(1)} %pad_maximum_fusion.refs_0_), channel_id=1, source_target_pairs={{0,16},{4,20},{8,24},{12,28},{16,0},{20,4},{24,8},{28,12},{1,17},{... | collective-permute-start | bytes 983048 | tf_op jit(solution)/shard_map/ppermute | solution.py:14
  224.3 17.7 %collective-permute-start.49 = (bf16[160,1024]{1,0:T(8,128)(2,1)S(1)}, bf16[160,1024]{1,0:T(8,128)(2,1)S(1)}, u32[]{:S(2)}, u32[]{:S(2)}) collective-permute-start(bf16[160,1024]{1,0:T(8,128)(2,1)S(1)} %pad_maximum_fusion.refs_0_), channel_id=1, source_target_pairs={{0,8},{4,12},{8,0},{12,4},{16,24},{20,28},{24,16},{28,20},{1,9},{5... | collective-permute-start | bytes 983048 | tf_op jit(solution)/shard_map/ppermute | solution.py:14
  242.0 17.0 %collective-permute-start.52 = (bf16[160,1024]{1,0:T(8,128)(2,1)S(1)}, bf16[160,1024]{1,0:T(8,128)(2,1)S(1)}, u32[]{:S(2)}, u32[]{:S(2)}) collective-permute-start(bf16[160,1024]{1,0:T(8,128)(2,1)S(1)} %pad_maximum_fusion.refs_0_), channel_id=1, source_target_pairs={{0,4},{4,0},{8,12},{12,8},{16,20},{20,16},{24,28},{28,24},{1,5},{5... | collective-permute-start | bytes 983048 | tf_op jit(solution)/shard_map/ppermute | solution.py:14
  242.1 17.0 %collective-permute-start.55 = (bf16[160,1024]{1,0:T(8,128)(2,1)S(1)}, bf16[160,1024]{1,0:T(8,128)(2,1)S(1)}, u32[]{:S(2)}, u32[]{:S(2)}) collective-permute-start(bf16[160,1024]{1,0:T(8,128)(2,1)S(1)} %collective-permute-done.51.refs_3_), channel_id=1, source_target_pairs={{0,4},{4,0},{8,12},{12,8},{16,20},{20,16},{24,28},{28,24},{1,5},{5... | collective-permute-start | bytes 983048 | tf_op jit(solution)/shard_map/ppermute | solution.py:14
  242.6 16.5 %collective-permute-start.54 = (bf16[160,1024]{1,0:T(8,128)(2,1)S(1)}, bf16[160,1024]{1,0:T(8,128)(2,1)S(1)}, u32[]{:S(2)}, u32[]{:S(2)}) collective-permute-start(bf16[160,1024]{1,0:T(8,128)(2,1)S(1)} %collective-permute-done.50.refs_2_), channel_id=1, source_target_pairs={{0,4},{4,0},{8,12},{12,8},{16,20},{20,16},{24,28},{28,24},{1,5},{5... | collective-permute-start | bytes 983048 | tf_op jit(solution)/shard_map/ppermute | solution.py:14
  242.6 16.4 %collective-permute-start.53 = (bf16[160,1024]{1,0:T(8,128)(2,1)S(1)}, bf16[160,1024]{1,0:T(8,128)(2,1)S(1)}, u32[]{:S(2)}, u32[]{:S(2)}) collective-permute-start(bf16[160,1024]{1,0:T(8,128)(2,1)S(1)} %collective-permute-done.49.refs_1_), channel_id=1, source_target_pairs={{0,4},{4,0},{8,12},{12,8},{16,20},{20,16},{24,28},{28,24},{1,5},{5... | collective-permute-start | bytes 983048 | tf_op jit(solution)/shard_map/ppermute | solution.py:14
  (56 other events, 477.7 us)

commit v2 on v1

--- a/solution.py
+++ b/solution.py
@@ -45,6 +45,10 @@
 def lane_block(values, target, count):
     narrow = values.shape[-1] // count
     return lax.dynamic_slice_in_dim(values, target * narrow, narrow, axis=values.ndim - 1)
+
+
+def in_hbm(values):
+    return pltpu.with_memory_space_constraint(values, pltpu.HBM)
 
 
 def add_all(first, rest):
@@ -137,6 +141,24 @@
     )
 
 
+def fetch(source, target, sem):
+    copy = pltpu.make_async_copy(source, target, sem)
+    copy.start()
+    return copy
+
+
+def place_pieces(place_ref, pieces, target, blocks):
+    rows = pieces[0].shape[0]
+    for index, piece in enumerate(pieces):
+        start = block_start(place_ref, index % blocks, index // blocks, rows)
+        target[pl.ds(start, rows), :] = piece[...]
+
+
+def store_own_lanes(place_ref, source, rows, target):
+    narrow = target.shape[1]
+    target[...] = source[rows, pl.ds(pl.multiple_of(place_ref[2] * narrow, 128), narrow)]
+
+
 def store_rows(value, targets):
     rows = targets[0].shape[0]
     for index, target in enumerate(targets):
@@ -145,26 +167,35 @@
 
 def forward_kernel(place_ref, *refs, blocks, rows, across):
     pieces = refs[: 2 * blocks]
-    expand_hbm, reduce_hbm, pre_ref, exp_ref = refs[2 * blocks : 2 * blocks + 4]
-    own_refs = refs[2 * blocks + 4 : 3 * blocks + 4]
-    sent_refs = refs[3 * blocks + 4 : 4 * blocks + 4]
-    padded, shifted, expand_buf, reduce_buf, sems = refs[4 * blocks + 4 :]
+    outer_hbm, expand_hbm, reduce_hbm, slice_ref, pre_ref, exp_ref = refs[
+        2 * blocks : 2 * blocks + 6
+    ]
+    own_refs = refs[2 * blocks + 6 : 3 * blocks + 6]
+    sent_refs = refs[3 * blocks + 6 : 4 * blocks + 6]
+    gathered, outer_buf, padded, shifted, expand_buf, reduce_buf, sems = refs[4 * blocks + 6 :]
+    outer_copy = fetch(outer_hbm, outer_buf, sems.at[18])
     expand_copies, reduce_copies = weight_copies(
         expand_hbm, reduce_hbm, expand_buf, reduce_buf, sems
     )
-    for copy in expand_copies + reduce_copies:
+    for copy in expand_copies:
         copy.start()
     clear_edges(padded, across)
     clear_edges(shifted, across)
-    for index, piece in enumerate(pieces):
-        start = block_start(place_ref, index % blocks, index // blocks, rows, across)
-        padded[pl.ds(start, rows), :] = piece[...]
     inner = expand_hbm.shape[-1]
     base = expand_hbm.shape[-2]
     positions = pre_ref.shape[0]
+    inside = pl.ds(across, positions)
+    place_pieces(place_ref, pieces, gathered, blocks)
+    outer_copy.wait()
+    wait_all(expand_copies[:3])
+    for copy in reduce_copies:
+        copy.start()
+    padded[inside, :] = plain_dot(gathered[...], outer_buf[...]).astype(jnp.bfloat16)
+    store_own_lanes(place_ref, padded, inside, slice_ref)
     total = None
     for p in range(3):
-        wait_all(expand_copies[3 * p : 3 * p + 3])
+        if p > 0:
+            wait_all(expand_copies[3 * p : 3 * p + 3])
         term = plain_dot(
             padded[p * across : p * across + positions, :],
             expand_buf[p * base : (p + 1) * base, :],
@@ -179,7 +210,6 @@
     expanded = (pre * jax.nn.sigmoid(pre)).astype(jnp.bfloat16)
     exp_ref[...] = expanded
     wide = expanded.astype(jnp.float32)
-    inside = pl.ds(across, positions)
     shifted[inside, 0:inner] = from_left(wide, across).astype(jnp.bfloat16)
     shifted[inside, inner : 2 * inner] = expanded
     shifted[inside, 2 * inner : 3 * inner] = from_right(wide, across).astype(jnp.bfloat16)
@@ -197,10 +227,13 @@
 
 def backward_kernel(place_ref, *refs, blocks, rows, across):
     pieces = refs[: 2 * blocks]
-    expand_hbm, reduce_hbm, pre_ref, grad_ref = refs[2 * blocks : 2 * blocks + 4]
-    own_refs = refs[2 * blocks + 4 : 3 * blocks + 4]
-    sent_refs = refs[3 * blocks + 4 : 4 * blocks + 4]
-    padded, shifted, expand_buf, reduce_buf, sems = refs[4 * blocks + 4 :]
+    outer_hbm, expand_hbm, reduce_hbm, pre_ref, slice_ref, grad_ref = refs[
+        2 * blocks : 2 * blocks + 6
+    ]
+    own_refs = refs[2 * blocks + 6 : 3 * blocks + 6]
+    sent_refs = refs[3 * blocks + 6 : 4 * blocks + 6]
+    gathered, outer_buf, padded, shifted, expand_buf, reduce_buf, sems = refs[4 * blocks + 6 :]
+    outer_copy = fetch(outer_hbm, outer_buf, sems.at[18])
     expand_copies, reduce_copies = weight_copies(
         expand_hbm, reduce_hbm, expand_buf, reduce_buf, sems
     )
@@ -208,12 +241,14 @@
         copy.start()
     clear_edges(padded, across)
     clear_edges(shifted, across)
-    for index, piece in enumerate(pieces):
-        start = block_start(place_ref, index % blocks, index // blocks, rows, across)
-        padded[pl.ds(start, rows), :] = piece[...]
     inner = expand_hbm.shape[-1]
     base = expand_hbm.shape[-2]
     positions = pre_ref.shape[0]
+    inside = pl.ds(across, positions)
+    place_pieces(place_ref, pieces, gathered, blocks)
+    outer_copy.wait()
+    padded[inside, :] = transposed_dot(gathered[...], outer_buf[...]).astype(jnp.bfloat16)
+    store_own_lanes(place_ref, padded, inside, slice_ref)
     total = None
     for p in range(3):
         wait_all(reduce_copies[3 * p : 3 * p + 3])
@@ -232,7 +267,6 @@
     grad = (back * silu_slope(pre)).astype(jnp.bfloat16)
     grad_ref[...] = grad
     wide = grad.astype(jnp.float32)
-    inside = pl.ds(across, positions)
     shifted[inside, 0:inner] = from_right(wide, across).astype(jnp.bfloat16)
     shifted[inside, inner : 2 * inner] = grad
     shifted[inside, 2 * inner : 3 * inner] = from_left(wide, across).astype(jnp.bfloat16)
@@ -262,19 +296,23 @@
     return pltpu.CompilerParams(vmem_limit_bytes=limit)
 
 
-def bottleneck_call(kernel, place, pieces, expand_weight, reduce_weight, pre, across):
-    rows, base = pieces[0].shape
+def bottleneck_call(
+    kernel, place, pieces, outer_weight, expand_weight, reduce_weight, pre, across, samples
+):
+    rows, outer = pieces[0].shape
+    base = expand_weight.shape[-2]
     positions = len(pieces) * rows
     inner = expand_weight.shape[-1]
     inner_bf16 = jax.ShapeDtypeStruct((positions, inner), jnp.bfloat16)
     inner_f32 = jax.ShapeDtypeStruct((positions, inner), jnp.float32)
     parts = (jax.ShapeDtypeStruct((rows, base), jnp.bfloat16),) * len(pieces)
-    operands = [place, *pieces, expand_weight, reduce_weight]
-    specs = [SMEM_SPEC] + [VMEM_SPEC] * len(pieces) + [HBM_SPEC] * 2
+    operands = [place, *pieces, outer_weight, expand_weight, reduce_weight]
+    specs = [SMEM_SPEC] + [VMEM_SPEC] * len(pieces) + [HBM_SPEC] * 3
+    part = jax.ShapeDtypeStruct((positions, base // samples), jnp.bfloat16)
     if pre is None:
-        outs = (inner_f32, inner_bf16) + parts
+        outs = (part, inner_f32, inner_bf16) + parts
     else:
-        outs = (inner_bf16,) + parts
+        outs = (part, inner_bf16) + parts
         operands.append(pre)
         specs.append(VMEM_SPEC)
     return pl.pallas_call(
@@ -283,15 +321,18 @@
         in_specs=specs,
         out_specs=tuple(VMEM_SPEC for _ in outs),
         scratch_shapes=[
+            pltpu.VMEM((positions, outer), jnp.bfloat16),
+            pltpu.VMEM(outer_weight.shape, jnp.bfloat16),
             pltpu.VMEM((positions + 2 * across, base), jnp.bfloat16),
             pltpu.VMEM((positions + 2 * across, 3 * inner), jnp.bfloat16),
             pltpu.VMEM((3 * base, 3 * inner), jnp.bfloat16),
             pltpu.VMEM((9 * inner, base), jnp.bfloat16),
-            pltpu.SemaphoreType.DMA((18,)),
+            pltpu.SemaphoreType.DMA((19,)),
         ],
         compiler_params=granted(
-            (*pieces, expand_weight, reduce_weight), outs,
+            (*pieces, outer_weight, expand_weight, reduce_weight), outs,
             (
+                ((positions, outer), jnp.bfloat16),
                 ((positions + 2 * across, base), jnp.bfloat16),
                 ((positions + 2 * across, 3 * inner), jnp.bfloat16),
             ),
@@ -302,29 +343,28 @@
 
 def correlate_kernel(place_ref, *refs, count, blocks, across, first_slice, split_left):
     whole = refs[:count]
-    own = refs[count : count + 2 * blocks]
-    others = refs[count + 2 * blocks : count + 4 * blocks]
-    out_ref, joined, shifted = refs[count + 4 * blocks :]
-    rows = own[0].shape[0]
+    own = refs[count]
+    others = refs[count + 1 : count + 1 + 2 * blocks]
+    out_hbm, out_ref, joined, shifted, sems = refs[count + 1 + 2 * blocks :]
+    copies = []
+    rows = joined.shape[0] // (2 * blocks)
     outward = shifted.shape[-1] // 3
-    narrow = joined.shape[-1]
-    positions = whole[0].shape[0]
+    positions = joined.shape[0]
     clear_edges(shifted, across)
     inside = pl.ds(across, positions)
-    lane = pl.multiple_of(place_ref[2] * narrow, 128)
     for sample in range(count):
-        for index in range(2 * blocks):
-            start = block_start(place_ref, index % blocks, index // blocks, rows)
-            if sample == 0:
-                piece = own[index][:, pl.ds(lane, narrow)]
-            else:
-                first = (first_slice + sample - 1) * rows
-                piece = others[index][first : first + rows, :]
-            joined[pl.ds(start, rows), :] = piece
+        if sample == 0:
+            part = own[...]
+        else:
+            first = (first_slice + sample - 1) * rows
+            for index in range(2 * blocks):
+                start = block_start(place_ref, index % blocks, index // blocks, rows)
+                joined[pl.ds(start, rows), :] = others[index][first : first + rows, :]
+            part = joined[...]
         if split_left:
-            left, right = joined[...], whole[sample][...]
+            left, right = part, whole[sample][...]
         else:
-            left, right = whole[sample][...], joined[...]
+            left, right = whole[sample][...], part
         turned = jnp.transpose(left, (1, 0))
         wide = right.astype(jnp.float32)
         shifted[inside, 0:outward] = from_right(wide, across).astype(jnp.bfloat16)
@@ -339,36 +379,36 @@
                     out_ref[p, q] = piece
                 else:
                     out_ref[p, q] += piece
+            if sample == count - 1:
+                copies.append(fetch(out_ref.at[p], out_hbm.at[p], sems.at[p]))
+    wait_all(copies)
 
 
 def correlate_call(place, whole, own, others, first_slice, split_left, across):
     count = len(whole)
     positions, full_lanes = whole[0].shape
-    part_lanes = others[0].shape[1]
+    part_lanes = own.shape[1]
     inward, outward = (part_lanes, full_lanes) if split_left else (full_lanes, part_lanes)
     out = jax.ShapeDtypeStruct((3, 3, inward, outward), jnp.float32)
     scratch = (
         ((positions, part_lanes), jnp.bfloat16),
         ((positions + 2 * across, 3 * outward), jnp.bfloat16),
     )
+    operands = (*whole, own, *others)
     return pl.pallas_call(
         functools.partial(
-            correlate_kernel, count=count, blocks=len(own) // 2, across=across,
+            correlate_kernel, count=count, blocks=len(others) // 2, across=across,
             first_slice=first_slice, split_left=split_left,
         ),
         out_shape=out,
-        in_specs=[SMEM_SPEC] + [VMEM_SPEC] * (count + len(own) + len(others)),
-        out_specs=VMEM_SPEC,
-        scratch_shapes=[pltpu.VMEM(*item) for item in scratch],
-        compiler_params=granted((*whole, *own, *others), (out,), scratch, CORRELATE_MIB),
+        in_specs=[SMEM_SPEC] + [VMEM_SPEC] * len(operands),
+        out_specs=HBM_SPEC,
+        scratch_shapes=[pltpu.VMEM(out.shape, out.dtype)]
+        + [pltpu.VMEM(*item) for item in scratch]
+        + [pltpu.SemaphoreType.DMA((3,))],
+        compiler_params=granted(operands, (out,), scratch, CORRELATE_MIB),
         name="correlate_kernel",
-    )(place, *whole, *own, *others)
-
-
-def fetch(source, target, sem):
-    copy = pltpu.make_async_copy(source, target, sem)
-    copy.start()
-    return copy
+    )(place, *operands)
 
 
 def store_lane_blocks(place_ref, source, targets):
@@ -659,7 +699,10 @@
 
 def unpack_kernel(place_ref, *refs, blocks, count, shapes):
     pieces = refs[: 2 * blocks]
-    out_refs, pack_ref = refs[2 * blocks : -1], refs[-1]
+    outs = len(shapes)
+    out_hbms = refs[2 * blocks : 2 * blocks + outs]
+    out_refs = refs[2 * blocks + outs : 2 * blocks + 2 * outs]
+    pack_ref, sems = refs[2 * blocks + 2 * outs :]
     lanes = pack_ref.shape[1]
     rows = pieces[0].shape[0]
     narrow = lanes // count
@@ -671,7 +714,9 @@
                 :, mask * narrow : (mask + 1) * narrow
             ]
     base = 0
-    for out_ref, (height, width) in zip(out_refs, shapes):
+    copies = []
+    for place, (height, width) in enumerate(shapes):
+        out_ref = out_refs[place]
         times = lanes // width
         part = height // times
         for index in range(times):
@@ -680,6 +725,8 @@
             if kept > 0:
                 out_ref[index * part : index * part + kept, :] = value.astype(jnp.float32)[:kept, :]
         base += part
+        copies.append(fetch(out_ref, out_hbms[place], sems.at[place]))
+    wait_all(copies)
 
 
 def unpack_call(place, pieces, count, out_shapes, shapes):
@@ -692,8 +739,9 @@
         ),
         out_shape=outs,
         in_specs=[SMEM_SPEC] + [VMEM_SPEC] * len(pieces),
-        out_specs=(VMEM_SPEC,) * len(out_shapes),
-        scratch_shapes=[pltpu.VMEM(*scratch)],
+        out_specs=(HBM_SPEC,) * len(out_shapes),
+        scratch_shapes=[pltpu.VMEM(shape, jnp.float32) for shape in out_shapes]
+        + [pltpu.VMEM(*scratch), pltpu.SemaphoreType.DMA((len(out_shapes),))],
         compiler_params=granted(pieces, outs, (scratch,), SMALL_MIB),
         name="unpack_kernel",
     )(place, *pieces)
@@ -800,17 +848,21 @@
     below = lax.ppermute(crop_rows[0], "wide", backward)
     columns, hidden_pre, stacked, coarse, *coarse_sends = front_call(
         place, crop_rows.reshape(height * across, channels), above, below,
-        conv_weight.reshape(9 * channels, -1), down_weight, across, samples,
-    )
-    coarse_mine = gather_chips(coarse)
-    coarse_other = swap_cores(coarse_mine)
+        in_hbm(conv_weight.reshape(9 * channels, -1)), in_hbm(down_weight), across, samples,
+    )
+    stacked_mine = gather_chips(stacked)
+    stacked_other = swap_cores(stacked_mine)
     if own_kernels:
-        expand_pre, expanded, *partial = bottleneck_call(
-            forward_kernel, place, coarse_mine + coarse_other, expand_weight, reduce_weight,
-            None, low_across,
+        coarse_part, expand_pre, expanded, *partial = bottleneck_call(
+            forward_kernel, place, stacked_mine + stacked_other, down_weight,
+            in_hbm(expand_weight), in_hbm(reduce_weight), None, low_across, samples,
         )
     else:
-        coarse_all = join_blocks(jnp.stack(coarse_mine), jnp.stack(coarse_other))
+        stacked_all = join_blocks(jnp.stack(stacked_mine), jnp.stack(stacked_other))
+        coarse_all = jnp.dot(stacked_all, down_weight, preferred_element_type=jnp.float32).astype(
+            jnp.bfloat16
+        )
+        coarse_part = lane_block(coarse_all, lax.axis_index("samp"), samples)
         expand_grid = conv_in(coarse_all.reshape(*grid, base), expand_weight, 1, False)
         expanded_grid = jax.nn.silu(expand_grid).astype(jnp.bfloat16)
         partial = conv_in(expanded_grid, reduce_weight, 1, False).astype(jnp.bfloat16)
@@ -823,15 +875,17 @@
         place, first, terms, coarse, stacked, labels, class_weight.T, up_weight, loss_scale,
         class_lanes, samples,
     )
-    bottom_mine = gather_chips(bottom_grad)
-    bottom_other = swap_cores(bottom_mine)
+    grad_mine = gather_chips(stacked_grad)
+    grad_other = swap_cores(grad_mine)
     if own_kernels:
-        expanded_grad, *back = bottleneck_call(
-            backward_kernel, place, bottom_mine + bottom_other, expand_weight, reduce_weight,
-            expand_pre, low_across,
+        bottom_part, expanded_grad, *back = bottleneck_call(
+            backward_kernel, place, grad_mine + grad_other, up_weight, expand_weight,
+            reduce_weight, expand_pre, low_across, samples,
         )
     else:
-        bottom_all = join_blocks(jnp.stack(bottom_mine), jnp.stack(bottom_other))
+        grad_all = join_blocks(jnp.stack(grad_mine), jnp.stack(grad_other))
+        bottom_all = transposed_dot(grad_all, up_weight).astype(jnp.bfloat16)
+        bottom_part = lane_block(bottom_all, lax.axis_index("samp"), samples)
         expanded_back = conv_in(bottom_all.reshape(*grid, base), reduce_weight, -1, True)
         grad_grid = (expanded_back * silu_slope(expand_grid)).astype(jnp.bfloat16)
         back = conv_in(grad_grid, expand_weight, -1, True).astype(jnp.bfloat16)
@@ -877,22 +931,17 @@
 
     if own_kernels:
         reduce_grad = correlate_call(
-            place, expanded_samples, bottom_mine + bottom_other, slices_mine + slices_other,
+            place, expanded_samples, bottom_part, slices_mine + slices_other,
             samples - 1, False, low_across,
         )
         expand_grad = correlate_call(
-            place, grad_samples, coarse_mine + coarse_other, slices_mine + slices_other,
+            place, grad_samples, coarse_part, slices_mine + slices_other,
             0, True, low_across,
         )
     else:
 
-        def join_samples(mine, other, first_slice):
-            sample = lax.axis_index("samp")
-            mine_all = jnp.stack(mine)
-            other_all = jnp.stack(other)
-            joined_ = [
-                join_blocks(lane_block(mine_all, sample, samples), lane_block(other_all, sample, samples))
-            ]
+        def join_samples(own_part, first_slice):
+            joined_ = [own_part]
             for i in range(samples - 1):
                 span = slice((first_slice + i) * block_rows, (first_slice + i + 1) * block_rows)
                 joined_.append(
@@ -905,10 +954,10 @@
 
         reduce_grad = correlate_samples(
             jnp.stack(expanded_samples).reshape(samples, *grid, inner),
-            join_samples(bottom_mine, bottom_other, samples - 1),
+            join_samples(bottom_part, samples - 1),
         )
         expand_grad = correlate_samples(
-            join_samples(coarse_mine, coarse_other, 0),
+            join_samples(coarse_part, 0),
             jnp.stack(grad_samples).reshape(samples, *grid, inner),
         )
     return (

time: 263 us -> 254 us (0.966)
  local copies, waits for them, and re-layouts: 8.54 us -> 1.79 us
  waiting for transfers between devices: 126 us -> 120 us
  Pallas kernels: 45.1 us -> 49.9 us
    unnamed x22 -> x18, local copies, waits for them, and re-layouts: 7.78 us -> 0.94 us
    ppermute x67, waiting for transfers between devices: 125 us -> 119 us  [swap(): return lax.ppermute(values, axis, [(i, i ^ mask) for i in range(count)])]
    pallas_call x2, Pallas kernels: 22.2 us -> 26.4 us  [bottleneck_call(): pl.pallas_call(functools.partial(kernel, blocks=len(pieces) // 2, rows=ro...]
where the time goes in v2:
time: 254 us; the launch traced here: 253 us
  waiting for transfers between devices  120 us (47%)
  starting transfers between devices  79.9 us (31%)
  Pallas kernels  49.9 us (20%)
    ppermute x67, waiting for transfers between devices, swap(): return lax.ppermute(values, axis, [(i, i ^ mask) for i in range(count)])  119 us
    ppermute x67, starting transfers between devices, swap(): return lax.ppermute(values, axis, [(i, i ^ mask) for i in range(count)])  75.5 us
    pallas_call x2, Pallas kernels, bottleneck_call(): pl.pallas_call(functools.partial(kernel, blocks=len(pieces) // 2, rows=ro...  26.4 us
    pallas_call x2, Pallas kernels, correlate_call(): pl.pallas_call(functools.partial(correlate_kernel, count=count, blocks=le...  11.6 us
  transfers between devices with their start and end apart: 69, of which 31 were waited for; matrix products, arithmetic and copies ran while one was open for 0% of the time, Pallas kernels for 5%

profile of v2, /device:TPU:0, one launch (start us, length us, event | category | flops | bytes accessed | tf_op | source)
XLA Modules:
  0.0 253.5 jit_solution(9174334232078888436)
XLA Ops:
  2.8 3.0 %collective-permute-start = (bf16[96,128]{1,0:T(8,128)(2,1)S(1)}, bf16[96,128]{1,0:T(8,128)(2,1)S(1)}, u32[]{:S(2)}, u32[]{:S(2)}) collective-permute-start(bf16[96,128]{1,0:T(8,128)(2,1)S(1)} %get-tuple-element.113), channel_id=1, source_target_pairs={{0,4},{4,8},{8,12},{12,16},{16,20},{20,24},{24,28},{1,5},{5,9},{9,... | collective-permute-start | bytes 73736 | tf_op jit(solution)/shard_map/ppermute | solution.py:847
  10.2 5.9 %collective-permute-start.4 = (bf16[96,512]{1,0:T(8,128)(2,1)S(1)}, bf16[96,512]{1,0:T(8,128)(2,1)S(1)}, u32[]{:S(2)}, u32[]{:S(2)}) collective-permute-start(bf16[96,512]{1,0:T(8,128)(2,1)S(1)} %get-tuple-element.59.refs_0_.refs_6_), channel_id=1, source_target_pairs={{0,24},{4,28},{8,16},{12,20},{16,8},{20,12},{24,0},{28,4},{1,25},{... | collective-permute-start | bytes 294920 | tf_op jit(solution)/shard_map/ppermute | solution.py:14
  23.3 13.7 %shard_map.127 = (bf16[768,256]{1,0:T(8,128)(2,1)S(1)}, f32[768,256]{1,0:T(8,128)S(1)}, bf16[768,256]{1,0:T(8,128)(2,1)S(1)}, bf16[96,1024]{1,0:T(8,128)(2,1)S(1...) custom-call(s32[3]{0:T(128)S(1)} %pad_add_fusion.place_ref, ...), custom_call_target="tpu_custom_call" | custom-call | tf_op jit(solution)/shard_map/pallas_call | solution.py:318
  42.4 4.0 %collective-permute-done.11.refs_2_ = bf16[96,1024]{1,0:T(8,128)(2,1)S(1)} collective-permute-done((bf16[96,1024]{1,0:T(8,128)(2,1)S(1)}, bf16[96,1024]{1,0:T(8,128)(2,1)S(1)}, u32[]{:S(2)}, u32[]{:S(2)}) %collective-permute-start.11) | collective-permute-done | bytes 196640 | tf_op jit(solution)/shard_map/ppermute | solution.py:14
  46.5 4.6 %collective-permute-done.13.refs_3_ = bf16[96,1024]{1,0:T(8,128)(2,1)S(1)} collective-permute-done((bf16[96,1024]{1,0:T(8,128)(2,1)S(1)}, bf16[96,1024]{1,0:T(8,128)(2,1)S(1)}, u32[]{:S(2)}, u32[]{:S(2)}) %collective-permute-start.13) | collective-permute-done | bytes 196640 | tf_op jit(solution)/shard_map/ppermute | solution.py:14
  62.4 12.7 %shard_map.128 = (bf16[768,256]{1,0:T(8,128)(2,1)S(1)}, bf16[768,256]{1,0:T(8,128)(2,1)S(1)}, bf16[96,1024]{1,0:T(8,128)(2,1)S(1)}, bf16[96,1024]{1,0:T(8,128)(2...) custom-call(s32[3]{0:T(128)S(1)} %pad_add_fusion.place_ref, ...), custom_call_target="tpu_custom_call" | custom-call | tf_op jit(solution)/shard_map/pallas_call | solution.py:318
  80.5 4.0 %collective-permute-done.25.refs_2_ = bf16[96,1024]{1,0:T(8,128)(2,1)S(1)} collective-permute-done((bf16[96,1024]{1,0:T(8,128)(2,1)S(1)}, bf16[96,1024]{1,0:T(8,128)(2,1)S(1)}, u32[]{:S(2)}, u32[]{:S(2)}) %collective-permute-start.25) | collective-permute-done | bytes 196640 | tf_op jit(solution)/shard_map/ppermute | solution.py:14
  84.5 4.6 %collective-permute-done.27.refs_3_ = bf16[96,1024]{1,0:T(8,128)(2,1)S(1)} collective-permute-done((bf16[96,1024]{1,0:T(8,128)(2,1)S(1)}, bf16[96,1024]{1,0:T(8,128)(2,1)S(1)}, u32[]{:S(2)}, u32[]{:S(2)}) %collective-permute-start.27) | collective-permute-done | bytes 196640 | tf_op jit(solution)/shard_map/ppermute | solution.py:14
  100.9 2.9 %collective-permute-done.38.refs_6_ = bf16[96,256]{1,0:T(8,128)(2,1)S(1)} collective-permute-done((bf16[96,256]{1,0:T(8,128)(2,1)S(1)}, bf16[96,256]{1,0:T(8,128)(2,1)S(1)}, u32[]{:S(2)}, u32[]{:S(2)}) %collective-permute-start.38) | collective-permute-done | bytes 49184 | tf_op jit(solution)/shard_map/ppermute | solution.py:14
  106.0 3.9 %collective-permute-done.39.refs_7_ = bf16[96,256]{1,0:T(8,128)(2,1)S(1)} collective-permute-done((bf16[96,256]{1,0:T(8,128)(2,1)S(1)}, bf16[96,256]{1,0:T(8,128)(2,1)S(1)}, u32[]{:S(2)}, u32[]{:S(2)}) %collective-permute-start.39) | collective-permute-done | bytes 49184 | tf_op jit(solution)/shard_map/ppermute | solution.py:14
  109.8 4.1 %collective-permute-done.40.refs_8_ = bf16[96,256]{1,0:T(8,128)(2,1)S(1)} collective-permute-done((bf16[96,256]{1,0:T(8,128)(2,1)S(1)}, bf16[96,256]{1,0:T(8,128)(2,1)S(1)}, u32[]{:S(2)}, u32[]{:S(2)}) %collective-permute-start.40) | collective-permute-done | bytes 49184 | tf_op jit(solution)/shard_map/ppermute | solution.py:14
  115.2 5.1 %collective-permute-done.41.refs_9_ = bf16[96,256]{1,0:T(8,128)(2,1)S(1)} collective-permute-done((bf16[96,256]{1,0:T(8,128)(2,1)S(1)}, bf16[96,256]{1,0:T(8,128)(2,1)S(1)}, u32[]{:S(2)}, u32[]{:S(2)}) %collective-permute-start.41) | collective-permute-done | bytes 49184 | tf_op jit(solution)/shard_map/ppermute | solution.py:14
  122.5 4.3 %collective-permute-done.42.refs_10_ = bf16[96,256]{1,0:T(8,128)(2,1)S(1)} collective-permute-done((bf16[96,256]{1,0:T(8,128)(2,1)S(1)}, bf16[96,256]{1,0:T(8,128)(2,1)S(1)}, u32[]{:S(2)}, u32[]{:S(2)}) %collective-permute-start.42) | collective-permute-done | bytes 49184 | tf_op jit(solution)/shard_map/ppermute | solution.py:14
  135.5 4.9 %collective-permute-done.43 = bf16[160,256]{1,0:T(8,128)(2,1)S(1)} collective-permute-done((bf16[160,256]{1,0:T(8,128)(2,1)S(1)}, bf16[160,256]{1,0:T(8,128)(2,1)S(1)}, u32[]{:S(2)}, u32[]{:S(2)}) %collective-permute-start.43) | collective-permute-done | bytes 81952 | tf_op jit(solution)/shard_map/ppermute | solution.py:14
  142.8 22.6 %collective-permute-done.44 = bf16[160,256]{1,0:T(8,128)(2,1)S(1)} collective-permute-done((bf16[160,256]{1,0:T(8,128)(2,1)S(1)}, bf16[160,256]{1,0:T(8,128)(2,1)S(1)}, u32[]{:S(2)}, u32[]{:S(2)}) %collective-permute-start.44) | collective-permute-done | bytes 81952 | tf_op jit(solution)/shard_map/ppermute | solution.py:14
  170.2 15.6 %collective-permute-done.67.refs_2_ = bf16[768,256]{1,0:T(8,128)(2,1)S(1)} collective-permute-done((bf16[768,256]{1,0:T(8,128)(2,1)S(1)}, bf16[768,256]{1,0:T(8,128)(2,1)S(1)}, u32[]{:S(2)}, u32[]{:S(2)}) %collective-permute-start.67) | collective-permute-done | bytes 393248 | tf_op jit(solution)/shard_map/ppermute | solution.py:14
  185.8 16.5 %collective-permute-start.46 = (bf16[160,256]{1,0:T(8,128)(2,1)S(1)}, bf16[160,256]{1,0:T(8,128)(2,1)S(1)}, u32[]{:S(2)}, u32[]{:S(2)}) collective-permute-start(bf16[160,256]{1,0:T(8,128)(2,1)S(1)} %add_convert_fusion.9), channel_id=1, source_target_pairs={{0,1},{1,0},{2,3},{3,2},{4,5},{5,4},{6,7},{7,6},{8,9},{9,8},{10,11... | collective-permute-start | bytes 245768 | tf_op jit(solution)/shard_map/ppermute | solution.py:14
  210.4 5.1 %collective-permute-done.61.refs_8_ = bf16[576,256]{1,0:T(8,128)(2,1)S(1)} collective-permute-done((bf16[576,256]{1,0:T(8,128)(2,1)S(1)}, bf16[576,256]{1,0:T(8,128)(2,1)S(1)}, u32[]{:S(2)}, u32[]{:S(2)}) %collective-permute-start.61) | collective-permute-done | bytes 294944 | tf_op jit(solution)/shard_map/ppermute | solution.py:14
  216.3 10.0 %collective-permute-done.60.refs_7_ = bf16[576,256]{1,0:T(8,128)(2,1)S(1)} collective-permute-done((bf16[576,256]{1,0:T(8,128)(2,1)S(1)}, bf16[576,256]{1,0:T(8,128)(2,1)S(1)}, u32[]{:S(2)}, u32[]{:S(2)}) %collective-permute-start.60) | collective-permute-done | bytes 294944 | tf_op jit(solution)/shard_map/ppermute | solution.py:14
  228.9 4.3 %collective-permute-done.50.refs_2_ = bf16[160,1024]{1,0:T(8,128)(2,1)S(1)} collective-permute-done((bf16[160,1024]{1,0:T(8,128)(2,1)S(1)}, bf16[160,1024]{1,0:T(8,128)(2,1)S(1)}, u32[]{:S(2)}, u32[]{:S(2)}) %collective-permute-start.50) | collective-permute-done | bytes 327712 | tf_op jit(solution)/shard_map/ppermute | solution.py:14
  234.3 5.8 %correlate_kernel.3 = f32[3,3,256,256]{3,2,1,0:T(8,128)} custom-call(s32[3]{0:T(128)S(1)} %pad_add_fusion.place_ref, bf16[768,256]{1,0:T(8,128)(2,1)S(1)} %get-tuple-element.108.refs_0_, bf16[768,256]{1,0:T(8,128)(2,1)S(1)} %collective-permute-done.66.refs_1_, bf16[768,256]{1,0:T(8,128)(2,1)S(1)} %collective-permute-done.67.refs_2_, ...), custom_call_target="tpu_custom_call" | custom-call | tf_op jit(solution)/shard_map/correlate_kernel/pallas_call | solution.py:398
  240.0 4.2 %collective-permute-done.56.refs_1_ = bf16[768,256]{1,0:T(8,128)(2,1)S(1)} collective-permute-done((bf16[768,256]{1,0:T(8,128)(2,1)S(1)}, bf16[768,256]{1,0:T(8,128)(2,1)S(1)}, u32[]{:S(2)}, u32[]{:S(2)}) %collective-permute-start.56) | collective-permute-done | bytes 393248 | tf_op jit(solution)/shard_map/ppermute | solution.py:14
  244.3 5.8 %correlate_kernel.2 = f32[3,3,256,256]{3,2,1,0:T(8,128)} custom-call(s32[3]{0:T(128)S(1)} %pad_add_fusion.place_ref, bf16[768,256]{1,0:T(8,128)(2,1)S(1)} %get-tuple-element.105.refs_0_, bf16[768,256]{1,0:T(8,128)(2,1)S(1)} %collective-permute-done.56.refs_1_, bf16[768,256]{1,0:T(8,128)(2,1)S(1)} %collective-permute-done.57.refs_2_, ...), custom_call_target="tpu_custom_call" | custom-call | tf_op jit(solution)/shard_map/correlate_kernel/pallas_call | solution.py:398
  250.1 3.2 %unpack_kernel.1 = (f32[512,1024]{1,0:T(8,128)}, f32[1024,512]{1,0:T(8,128)}, f32[1152,128]{1,0:T(8,128)}, f32[9,128]{1,0:T(8,128)}) custom-call(s32[3]{0:T(128)S(1)} %pad_add_fusion.place_ref, bf16[160,1024]{1,0:T(8,128)(2,1)S(1)} %pad_maximum_fusion.refs_0_, bf16[160,1024]{1,0:T(8,128)(2,1)S(1)} %collective-permute-done.49.refs_1_, ...), custom_call_target="tpu_custom_call" | custom-call | tf_op jit(solution)/shard_map/unpack_kernel/pallas_call | solution.py:736
  (156 shorter events, 81.6 us)
Async XLA Ops:
  77.9 11.2 %collective-permute-start.27 = (bf16[96,1024]{1,0:T(8,128)(2,1)S(1)}, bf16[96,1024]{1,0:T(8,128)(2,1)S(1)}, u32[]{:S(2)}, u32[]{:S(2)}) collective-permute-start(bf16[96,1024]{1,0:T(8,128)(2,1)S(1)} %add_convert_fusion.4), channel_id=1, source_target_pairs={{0,16},{4,20},{8,24},{12,28},{16,0},{20,4},{24,8},{28,12},{1,17},{... | collective-permute-start | bytes 589832 | tf_op jit(solution)/shard_map/ppermute | solution.py:14
  93.8 35.3 %collective-permute-start.30 = (bf16[160,1024]{1,0:T(8,128)(2,1)S(1)}, bf16[160,1024]{1,0:T(8,128)(2,1)S(1)}, u32[]{:S(2)}, u32[]{:S(2)}) collective-permute-start(bf16[160,1024]{1,0:T(8,128)(2,1)S(1)} %get-tuple-element.86), channel_id=1, source_target_pairs={{0,4},{4,0},{8,12},{12,8},{16,20},{20,16},{24,28},{28,24},{1,5},{5... | collective-permute-start | bytes 983048 | tf_op jit(solution)/shard_map/ppermute | solution.py:14
  94.4 34.6 %collective-permute-start.32 = (bf16[160,1024]{1,0:T(8,128)(2,1)S(1)}, bf16[160,1024]{1,0:T(8,128)(2,1)S(1)}, u32[]{:S(2)}, u32[]{:S(2)}) collective-permute-start(bf16[160,1024]{1,0:T(8,128)(2,1)S(1)} %add_convert_fusion.2), channel_id=1, source_target_pairs={{0,8},{4,12},{8,0},{12,4},{16,24},{20,28},{24,16},{28,20},{1,9},{5... | collective-permute-start | bytes 983048 | tf_op jit(solution)/shard_map/ppermute | solution.py:14
  95.4 33.7 %collective-permute-start.34 = (bf16[160,1024]{1,0:T(8,128)(2,1)S(1)}, bf16[160,1024]{1,0:T(8,128)(2,1)S(1)}, u32[]{:S(2)}, u32[]{:S(2)}) collective-permute-start(bf16[160,1024]{1,0:T(8,128)(2,1)S(1)} %add_convert_fusion.1), channel_id=1, source_target_pairs={{0,16},{4,20},{8,24},{12,28},{16,0},{20,4},{24,8},{28,12},{1,17},{... | collective-permute-start | bytes 983048 | tf_op jit(solution)/shard_map/ppermute | solution.py:14
  96.9 32.2 %collective-permute-start.36 = (bf16[160,1024]{1,0:T(8,128)(2,1)S(1)}, bf16[160,1024]{1,0:T(8,128)(2,1)S(1)}, u32[]{:S(2)}, u32[]{:S(2)}) collective-permute-start(bf16[160,1024]{1,0:T(8,128)(2,1)S(1)} %add_convert_fusion), channel_id=1, source_target_pairs={{0,24},{4,28},{8,16},{12,20},{16,8},{20,12},{24,0},{28,4},{1,25},{... | collective-permute-start | bytes 983048 | tf_op jit(solution)/shard_map/ppermute | solution.py:14
  126.8 41.4 %collective-permute-start.68 = (bf16[768,256]{1,0:T(8,128)(2,1)S(1)}, bf16[768,256]{1,0:T(8,128)(2,1)S(1)}, u32[]{:S(2)}, u32[]{:S(2)}) collective-permute-start(bf16[768,256]{1,0:T(8,128)(2,1)S(1)} %get-tuple-element.108.refs_0_), channel_id=1, source_target_pairs={{0,3},{1,2},{2,1},{3,0},{4,7},{5,6},{6,5},{7,4},{8,11},{9,10},{10,... | collective-permute-start | bytes 1179656 | tf_op jit(solution)/shard_map/ppermute | solution.py:14
  130.5 34.9 %collective-permute-start.44 = (bf16[160,256]{1,0:T(8,128)(2,1)S(1)}, bf16[160,256]{1,0:T(8,128)(2,1)S(1)}, u32[]{:S(2)}, u32[]{:S(2)}) collective-permute-start(bf16[160,256]{1,0:T(8,128)(2,1)S(1)} %get-tuple-element.101), channel_id=1, source_target_pairs={{0,2},{1,3},{2,0},{3,1},{4,6},{5,7},{6,4},{7,5},{8,10},{9,11},{10,... | collective-permute-start | bytes 245768 | tf_op jit(solution)/shard_map/ppermute | solution.py:14
  132.2 35.0 %collective-permute-start.45 = (bf16[160,256]{1,0:T(8,128)(2,1)S(1)}, bf16[160,256]{1,0:T(8,128)(2,1)S(1)}, u32[]{:S(2)}, u32[]{:S(2)}) collective-permute-start(bf16[160,256]{1,0:T(8,128)(2,1)S(1)} %get-tuple-element.102), channel_id=1, source_target_pairs={{0,3},{1,2},{2,1},{3,0},{4,7},{5,6},{6,5},{7,4},{8,11},{9,10},{10,... | collective-permute-start | bytes 245768 | tf_op jit(solution)/shard_map/ppermute | solution.py:14
  134.5 51.2 %collective-permute-start.67 = (bf16[768,256]{1,0:T(8,128)(2,1)S(1)}, bf16[768,256]{1,0:T(8,128)(2,1)S(1)}, u32[]{:S(2)}, u32[]{:S(2)}) collective-permute-start(bf16[768,256]{1,0:T(8,128)(2,1)S(1)} %get-tuple-element.108.refs_0_), channel_id=1, source_target_pairs={{0,2},{1,3},{2,0},{3,1},{4,6},{5,7},{6,4},{7,5},{8,10},{9,11},{10,... | collective-permute-start | bytes 1179656 | tf_op jit(solution)/shard_map/ppermute | solution.py:14
  140.3 65.9 %collective-permute-start.66 = (bf16[768,256]{1,0:T(8,128)(2,1)S(1)}, bf16[768,256]{1,0:T(8,128)(2,1)S(1)}, u32[]{:S(2)}, u32[]{:S(2)}) collective-permute-start(bf16[768,256]{1,0:T(8,128)(2,1)S(1)} %get-tuple-element.108.refs_0_), channel_id=1, source_target_pairs={{0,1},{1,0},{2,3},{3,2},{4,5},{5,4},{6,7},{7,6},{8,9},{9,8},{10,11... | collective-permute-start | bytes 1179656 | tf_op jit(solution)/shard_map/ppermute | solution.py:14
  165.4 42.3 %collective-permute-start.58 = (bf16[768,256]{1,0:T(8,128)(2,1)S(1)}, bf16[768,256]{1,0:T(8,128)(2,1)S(1)}, u32[]{:S(2)}, u32[]{:S(2)}) collective-permute-start(bf16[768,256]{1,0:T(8,128)(2,1)S(1)} %get-tuple-element.105.refs_0_), channel_id=1, source_target_pairs={{0,3},{1,2},{2,1},{3,0},{4,7},{5,6},{6,5},{7,4},{8,11},{9,10},{10,... | collective-permute-start | bytes 1179656 | tf_op jit(solution)/shard_map/ppermute | solution.py:14
  167.2 41.5 %collective-permute-start.57 = (bf16[768,256]{1,0:T(8,128)(2,1)S(1)}, bf16[768,256]{1,0:T(8,128)(2,1)S(1)}, u32[]{:S(2)}, u32[]{:S(2)}) collective-permute-start(bf16[768,256]{1,0:T(8,128)(2,1)S(1)} %get-tuple-element.105.refs_0_), channel_id=1, source_target_pairs={{0,2},{1,3},{2,0},{3,1},{4,6},{5,7},{6,4},{7,5},{8,10},{9,11},{10,... | collective-permute-start | bytes 1179656 | tf_op jit(solution)/shard_map/ppermute | solution.py:14
  168.2 17.6 %collective-permute-start.48 = (bf16[160,256]{1,0:T(8,128)(2,1)S(1)}, bf16[160,256]{1,0:T(8,128)(2,1)S(1)}, u32[]{:S(2)}, u32[]{:S(2)}) collective-permute-start(bf16[160,256]{1,0:T(8,128)(2,1)S(1)} %add_convert_fusion.9), channel_id=1, source_target_pairs={{0,3},{1,2},{2,1},{3,0},{4,7},{5,6},{6,5},{7,4},{8,11},{9,10},{10,... | collective-permute-start | bytes 245768 | tf_op jit(solution)/shard_map/ppermute | solution.py:14
  185.8 16.8 %collective-permute-start.47 = (bf16[160,256]{1,0:T(8,128)(2,1)S(1)}, bf16[160,256]{1,0:T(8,128)(2,1)S(1)}, u32[]{:S(2)}, u32[]{:S(2)}) collective-permute-start(bf16[160,256]{1,0:T(8,128)(2,1)S(1)} %add_convert_fusion.9), channel_id=1, source_target_pairs={{0,2},{1,3},{2,0},{3,1},{4,6},{5,7},{6,4},{7,5},{8,10},{9,11},{10,... | collective-permute-start | bytes 245768 | tf_op jit(solution)/shard_map/ppermute | solution.py:14
  185.8 18.9 %collective-permute-start.46 = (bf16[160,256]{1,0:T(8,128)(2,1)S(1)}, bf16[160,256]{1,0:T(8,128)(2,1)S(1)}, u32[]{:S(2)}, u32[]{:S(2)}) collective-permute-start(bf16[160,256]{1,0:T(8,128)(2,1)S(1)} %add_convert_fusion.9), channel_id=1, source_target_pairs={{0,1},{1,0},{2,3},{3,2},{4,5},{5,4},{6,7},{7,6},{8,9},{9,8},{10,11... | collective-permute-start | bytes 245768 | tf_op jit(solution)/shard_map/ppermute | solution.py:14
  206.2 22.2 %collective-permute-start.51 = (bf16[160,1024]{1,0:T(8,128)(2,1)S(1)}, bf16[160,1024]{1,0:T(8,128)(2,1)S(1)}, u32[]{:S(2)}, u32[]{:S(2)}) collective-permute-start(bf16[160,1024]{1,0:T(8,128)(2,1)S(1)} %pad_maximum_fusion.refs_0_), channel_id=1, source_target_pairs={{0,24},{4,28},{8,16},{12,20},{16,8},{20,12},{24,0},{28,4},{1,25},{... | collective-permute-start | bytes 983048 | tf_op jit(solution)/shard_map/ppermute | solution.py:14
  207.7 18.6 %collective-permute-start.60 = (bf16[576,256]{1,0:T(8,128)(2,1)S(1)}, bf16[576,256]{1,0:T(8,128)(2,1)S(1)}, u32[]{:S(2)}, u32[]{:S(2)}) collective-permute-start(bf16[576,256]{1,0:T(8,128)(2,1)S(1)} %get-tuple-element.107.refs_5_), channel_id=1, source_target_pairs={{0,16},{4,20},{8,24},{12,28},{16,0},{20,4},{24,8},{28,12},{1,17},{... | collective-permute-start | bytes 884744 | tf_op jit(solution)/shard_map/ppermute | solution.py:14
  208.8 19.7 %collective-permute-start.59 = (bf16[576,256]{1,0:T(8,128)(2,1)S(1)}, bf16[576,256]{1,0:T(8,128)(2,1)S(1)}, u32[]{:S(2)}, u32[]{:S(2)}) collective-permute-start(bf16[576,256]{1,0:T(8,128)(2,1)S(1)} %get-tuple-element.107.refs_5_), channel_id=1, source_target_pairs={{0,8},{4,12},{8,0},{12,4},{16,24},{20,28},{24,16},{28,20},{1,9},{5... | collective-permute-start | bytes 884744 | tf_op jit(solution)/shard_map/ppermute | solution.py:14
  209.8 23.4 %collective-permute-start.50 = (bf16[160,1024]{1,0:T(8,128)(2,1)S(1)}, bf16[160,1024]{1,0:T(8,128)(2,1)S(1)}, u32[]{:S(2)}, u32[]{:S(2)}) collective-permute-start(bf16[160,1024]{1,0:T(8,128)(2,1)S(1)} %pad_maximum_fusion.refs_0_), channel_id=1, source_target_pairs={{0,16},{4,20},{8,24},{12,28},{16,0},{20,4},{24,8},{28,12},{1,17},{... | collective-permute-start | bytes 983048 | tf_op jit(solution)/shard_map/ppermute | solution.py:14
  215.5 17.7 %collective-permute-start.49 = (bf16[160,1024]{1,0:T(8,128)(2,1)S(1)}, bf16[160,1024]{1,0:T(8,128)(2,1)S(1)}, u32[]{:S(2)}, u32[]{:S(2)}) collective-permute-start(bf16[160,1024]{1,0:T(8,128)(2,1)S(1)} %pad_maximum_fusion.refs_0_), channel_id=1, source_target_pairs={{0,8},{4,12},{8,0},{12,4},{16,24},{20,28},{24,16},{28,20},{1,9},{5... | collective-permute-start | bytes 983048 | tf_op jit(solution)/shard_map/ppermute | solution.py:14
  233.2 16.8 %collective-permute-start.52 = (bf16[160,1024]{1,0:T(8,128)(2,1)S(1)}, bf16[160,1024]{1,0:T(8,128)(2,1)S(1)}, u32[]{:S(2)}, u32[]{:S(2)}) collective-permute-start(bf16[160,1024]{1,0:T(8,128)(2,1)S(1)} %pad_maximum_fusion.refs_0_), channel_id=1, source_target_pairs={{0,4},{4,0},{8,12},{12,8},{16,20},{20,16},{24,28},{28,24},{1,5},{5... | collective-permute-start | bytes 983048 | tf_op jit(solution)/shard_map/ppermute | solution.py:14
  233.2 16.8 %collective-permute-start.55 = (bf16[160,1024]{1,0:T(8,128)(2,1)S(1)}, bf16[160,1024]{1,0:T(8,128)(2,1)S(1)}, u32[]{:S(2)}, u32[]{:S(2)}) collective-permute-start(bf16[160,1024]{1,0:T(8,128)(2,1)S(1)} %collective-permute-done.51.refs_3_), channel_id=1, source_target_pairs={{0,4},{4,0},{8,12},{12,8},{16,20},{20,16},{24,28},{28,24},{1,5},{5... | collective-permute-start | bytes 983048 | tf_op jit(solution)/shard_map/ppermute | solution.py:14
  233.7 16.3 %collective-permute-start.54 = (bf16[160,1024]{1,0:T(8,128)(2,1)S(1)}, bf16[160,1024]{1,0:T(8,128)(2,1)S(1)}, u32[]{:S(2)}, u32[]{:S(2)}) collective-permute-start(bf16[160,1024]{1,0:T(8,128)(2,1)S(1)} %collective-permute-done.50.refs_2_), channel_id=1, source_target_pairs={{0,4},{4,0},{8,12},{12,8},{16,20},{20,16},{24,28},{28,24},{1,5},{5... | collective-permute-start | bytes 983048 | tf_op jit(solution)/shard_map/ppermute | solution.py:14
  233.8 16.3 %collective-permute-start.53 = (bf16[160,1024]{1,0:T(8,128)(2,1)S(1)}, bf16[160,1024]{1,0:T(8,128)(2,1)S(1)}, u32[]{:S(2)}, u32[]{:S(2)}) collective-permute-start(bf16[160,1024]{1,0:T(8,128)(2,1)S(1)} %collective-permute-done.49.refs_1_), channel_id=1, source_target_pairs={{0,4},{4,0},{8,12},{12,8},{16,20},{20,16},{24,28},{28,24},{1,5},{5... | collective-permute-start | bytes 983048 | tf_op jit(solution)/shard_map/ppermute | solution.py:14
  (54 other events, 560.4 us)

commit v3 on v2

--- a/solution.py
+++ b/solution.py
@@ -92,28 +92,31 @@
     padded[total - across : total, :] = blank
 
 
-def weight_copies(expand_hbm, reduce_hbm, expand_buf, reduce_buf, sems):
+def expand_copies_of(expand_hbm, expand_buf, sems):
     inner = expand_hbm.shape[-1]
     base = expand_hbm.shape[-2]
-    expand_copies = []
-    reduce_copies = []
-    for p in range(3):
-        for q in range(3):
-            expand_copies.append(
-                pltpu.make_async_copy(
-                    expand_hbm.at[p, q],
-                    expand_buf.at[pl.ds(p * base, base), pl.ds(q * inner, inner)],
-                    sems.at[3 * p + q],
-                )
-            )
-            reduce_copies.append(
-                pltpu.make_async_copy(
-                    reduce_hbm.at[p, q],
-                    reduce_buf.at[pl.ds((3 * p + q) * inner, inner), :],
-                    sems.at[9 + 3 * p + q],
-                )
-            )
-    return expand_copies, reduce_copies
+    return [
+        pltpu.make_async_copy(
+            expand_hbm.at[p, q],
+            expand_buf.at[pl.ds(p * base, base), pl.ds(q * inner, inner)],
+            sems.at[3 * p + q],
+        )
+        for p in range(3)
+        for q in range(3)
+    ]
+
+
+def reduce_copies_of(reduce_hbm, reduce_buf, sems):
+    inner = reduce_hbm.shape[-2]
+    return [
+        pltpu.make_async_copy(
+            reduce_hbm.at[p, q],
+            reduce_buf.at[pl.ds((3 * p + q) * inner, inner), :],
+            sems.at[3 * p + q],
+        )
+        for p in range(3)
+        for q in range(3)
+    ]
 
 
 def wait_all(copies):
@@ -167,35 +170,26 @@
 
 def forward_kernel(place_ref, *refs, blocks, rows, across):
     pieces = refs[: 2 * blocks]
-    outer_hbm, expand_hbm, reduce_hbm, slice_ref, pre_ref, exp_ref = refs[
-        2 * blocks : 2 * blocks + 6
+    outer_ref, expand_buf, reduce_hbm, slice_ref, pre_ref, exp_ref, reduce_buf = refs[
+        2 * blocks : 2 * blocks + 7
     ]
-    own_refs = refs[2 * blocks + 6 : 3 * blocks + 6]
-    sent_refs = refs[3 * blocks + 6 : 4 * blocks + 6]
-    gathered, outer_buf, padded, shifted, expand_buf, reduce_buf, sems = refs[4 * blocks + 6 :]
-    outer_copy = fetch(outer_hbm, outer_buf, sems.at[18])
-    expand_copies, reduce_copies = weight_copies(
-        expand_hbm, reduce_hbm, expand_buf, reduce_buf, sems
-    )
-    for copy in expand_copies:
+    own_refs = refs[2 * blocks + 7 : 3 * blocks + 7]
+    sent_refs = refs[3 * blocks + 7 : 4 * blocks + 7]
+    gathered, padded, shifted, sems = refs[4 * blocks + 7 :]
+    reduce_copies = reduce_copies_of(reduce_hbm, reduce_buf, sems)
+    for copy in reduce_copies:
         copy.start()
     clear_edges(padded, across)
     clear_edges(shifted, across)
-    inner = expand_hbm.shape[-1]
-    base = expand_hbm.shape[-2]
+    inner = pre_ref.shape[1]
+    base = padded.shape[1]
     positions = pre_ref.shape[0]
     inside = pl.ds(across, positions)
     place_pieces(place_ref, pieces, gathered, blocks)
-    outer_copy.wait()
-    wait_all(expand_copies[:3])
-    for copy in reduce_copies:
-        copy.start()
-    padded[inside, :] = plain_dot(gathered[...], outer_buf[...]).astype(jnp.bfloat16)
+    padded[inside, :] = plain_dot(gathered[...], outer_ref[...]).astype(jnp.bfloat16)
     store_own_lanes(place_ref, padded, inside, slice_ref)
     total = None
     for p in range(3):
-        if p > 0:
-            wait_all(expand_copies[3 * p : 3 * p + 3])
         term = plain_dot(
             padded[p * across : p * across + positions, :],
             expand_buf[p * base : (p + 1) * base, :],
@@ -215,43 +209,33 @@
     shifted[inside, 2 * inner : 3 * inner] = from_right(wide, across).astype(jnp.bfloat16)
     wait_all(reduce_copies)
     for half, targets in ((1, sent_refs), (0, own_refs)):
-        left = jnp.concatenate(
-            [
-                gather_blocks(shifted, place_ref, half, p * across, rows, blocks)
-                for p in range(3)
-            ],
-            axis=1,
-        )
-        store_rows(plain_dot(left, reduce_buf[...]).astype(jnp.bfloat16), targets)
+        out = None
+        for p in range(3):
+            left = gather_blocks(shifted, place_ref, half, p * across, rows, blocks)
+            term = plain_dot(left, reduce_buf[3 * p * inner : 3 * (p + 1) * inner, :])
+            out = term if out is None else out + term
+        store_rows(out.astype(jnp.bfloat16), targets)
 
 
 def backward_kernel(place_ref, *refs, blocks, rows, across):
     pieces = refs[: 2 * blocks]
-    outer_hbm, expand_hbm, reduce_hbm, pre_ref, slice_ref, grad_ref = refs[
+    outer_ref, expand_buf, reduce_buf, pre_ref, slice_ref, grad_ref = refs[
         2 * blocks : 2 * blocks + 6
     ]
     own_refs = refs[2 * blocks + 6 : 3 * blocks + 6]
     sent_refs = refs[3 * blocks + 6 : 4 * blocks + 6]
-    gathered, outer_buf, padded, shifted, expand_buf, reduce_buf, sems = refs[4 * blocks + 6 :]
-    outer_copy = fetch(outer_hbm, outer_buf, sems.at[18])
-    expand_copies, reduce_copies = weight_copies(
-        expand_hbm, reduce_hbm, expand_buf, reduce_buf, sems
-    )
-    for copy in reduce_copies + expand_copies:
-        copy.start()
+    gathered, padded, shifted = refs[4 * blocks + 6 :]
     clear_edges(padded, across)
     clear_edges(shifted, across)
-    inner = expand_hbm.shape[-1]
-    base = expand_hbm.shape[-2]
+    inner = pre_ref.shape[1]
+    base = padded.shape[1]
     positions = pre_ref.shape[0]
     inside = pl.ds(across, positions)
     place_pieces(place_ref, pieces, gathered, blocks)
-    outer_copy.wait()
-    padded[inside, :] = transposed_dot(gathered[...], outer_buf[...]).astype(jnp.bfloat16)
+    padded[inside, :] = transposed_dot(gathered[...], outer_ref[...]).astype(jnp.bfloat16)
     store_own_lanes(place_ref, padded, inside, slice_ref)
     total = None
     for p in range(3):
-        wait_all(reduce_copies[3 * p : 3 * p + 3])
         start = (2 - p) * across
         term = transposed_dot(
             padded[start : start + positions, :],
@@ -270,7 +254,6 @@
     shifted[inside, 0:inner] = from_right(wide, across).astype(jnp.bfloat16)
     shifted[inside, inner : 2 * inner] = grad
     shifted[inside, 2 * inner : 3 * inner] = from_left(wide, across).astype(jnp.bfloat16)
-    wait_all(expand_copies)
     for half, targets in ((1, sent_refs), (0, own_refs)):
         out = None
         for p in range(3):
@@ -297,48 +280,41 @@
 
 
 def bottleneck_call(
-    kernel, place, pieces, outer_weight, expand_weight, reduce_weight, pre, across, samples
+    kernel, place, pieces, outer_weight, expand_held, reduce_held, pre, across, samples
 ):
     rows, outer = pieces[0].shape
-    base = expand_weight.shape[-2]
+    base = expand_held.shape[0] // 3
+    inner = expand_held.shape[1] // 3
     positions = len(pieces) * rows
-    inner = expand_weight.shape[-1]
     inner_bf16 = jax.ShapeDtypeStruct((positions, inner), jnp.bfloat16)
     inner_f32 = jax.ShapeDtypeStruct((positions, inner), jnp.float32)
+    held = jax.ShapeDtypeStruct((9 * inner, base), jnp.bfloat16)
     parts = (jax.ShapeDtypeStruct((rows, base), jnp.bfloat16),) * len(pieces)
-    operands = [place, *pieces, outer_weight, expand_weight, reduce_weight]
-    specs = [SMEM_SPEC] + [VMEM_SPEC] * len(pieces) + [HBM_SPEC] * 3
     part = jax.ShapeDtypeStruct((positions, base // samples), jnp.bfloat16)
+    operands = [*pieces, outer_weight, expand_held, reduce_held]
+    specs = [SMEM_SPEC] + [VMEM_SPEC] * (len(pieces) + 2)
+    scratch = (
+        ((positions, outer), jnp.bfloat16),
+        ((positions + 2 * across, base), jnp.bfloat16),
+        ((positions + 2 * across, 3 * inner), jnp.bfloat16),
+    )
     if pre is None:
-        outs = (part, inner_f32, inner_bf16) + parts
+        outs = (part, inner_f32, inner_bf16, held) + parts
+        specs += [HBM_SPEC]
+        sems = [pltpu.SemaphoreType.DMA((9,))]
     else:
         outs = (part, inner_bf16) + parts
         operands.append(pre)
-        specs.append(VMEM_SPEC)
+        specs += [VMEM_SPEC] * 2
+        sems = []
     return pl.pallas_call(
         functools.partial(kernel, blocks=len(pieces) // 2, rows=rows, across=across),
         out_shape=outs,
         in_specs=specs,
         out_specs=tuple(VMEM_SPEC for _ in outs),
-        scratch_shapes=[
-            pltpu.VMEM((positions, outer), jnp.bfloat16),
-            pltpu.VMEM(outer_weight.shape, jnp.bfloat16),
-            pltpu.VMEM((positions + 2 * across, base), jnp.bfloat16),
-            pltpu.VMEM((positions + 2 * across, 3 * inner), jnp.bfloat16),
-            pltpu.VMEM((3 * base, 3 * inner), jnp.bfloat16),
-            pltpu.VMEM((9 * inner, base), jnp.bfloat16),
-            pltpu.SemaphoreType.DMA((19,)),
-        ],
-        compiler_params=granted(
-            (*pieces, outer_weight, expand_weight, reduce_weight), outs,
-            (
-                ((positions, outer), jnp.bfloat16),
-                ((positions + 2 * across, base), jnp.bfloat16),
-                ((positions + 2 * across, 3 * inner), jnp.bfloat16),
-            ),
-            BOTTLENECK_MIB,
-        ),
-    )(*operands)
+        scratch_shapes=[pltpu.VMEM(*item) for item in scratch] + sems,
+        compiler_params=granted(operands, outs, scratch, BOTTLENECK_MIB),
+    )(place, *operands)
 
 
 def correlate_kernel(place_ref, *refs, count, blocks, across, first_slice, split_left):
@@ -418,17 +394,25 @@
         target[...] = source[:, pl.ds(lane, narrow)]
 
 
-def front_kernel(place_ref, crop_ref, above_ref, below_ref, conv_hbm, down_hbm, *refs, across):
-    columns_ref, pre_ref, stacked_ref, coarse_ref = refs[:4]
-    slice_refs = refs[4:-5]
-    near_ref, grid_ref, conv_buf, down_buf, sems = refs[-5:]
-    conv_copy = fetch(conv_hbm, conv_buf, sems.at[0])
-    down_copy = fetch(down_hbm, down_buf, sems.at[1])
-    positions = crop_ref.shape[0]
-    channels = crop_ref.shape[1]
-    near_ref[0:across, :] = above_ref[...]
-    near_ref[across : across + positions, :] = crop_ref[...]
-    near_ref[across + positions :, :] = below_ref[...]
+def front_kernel(
+    place_ref, cross_ref, core_row_ref, crop_hbm, conv_hbm, down_hbm, *refs, across, hold
+):
+    held, refs = (refs[:1], refs[1:]) if hold else ((), refs)
+    columns_ref, pre_ref, stacked_ref, coarse_ref, down_buf = refs[:5]
+    slice_refs = refs[5 + hold : -4]
+    near_ref, grid_ref, conv_buf, sems = refs[-4:]
+    positions, channels = crop_hbm.shape
+    crop_copy = fetch(crop_hbm, near_ref.at[pl.ds(across, positions), :], sems.at[11])
+    conv_copy = fetch(conv_hbm, conv_buf, sems.at[9])
+    down_copy = fetch(down_hbm, down_buf, sems.at[10])
+    expand_copies = expand_copies_of(held[0], refs[5], sems) if hold else []
+    for copy in expand_copies:
+        copy.start()
+    core = place_ref[0]
+    far = across + positions
+    near_ref[pl.ds(pl.multiple_of(core * far, 16), across), :] = cross_ref[...]
+    near_ref[pl.ds(pl.multiple_of((1 - core) * far, 16), across), :] = core_row_ref[...]
+    crop_copy.wait()
     wide = near_ref[...].astype(jnp.float32)
     columns_ref[:, 0:channels] = from_left(wide, across).astype(jnp.bfloat16)
     columns_ref[:, channels : 2 * channels] = near_ref[...]
@@ -453,9 +437,13 @@
     down_copy.wait()
     coarse_ref[...] = plain_dot(stacked, down_buf[...]).astype(jnp.bfloat16)
     store_lane_blocks(place_ref, coarse_ref, slice_refs)
-
-
-def front_call(place, crop, above, below, conv_flat, down_weight, across, samples):
+    wait_all(expand_copies)
+
+
+def front_call(
+    place, crop, cross, core_row, conv_flat, down_weight, expand_weight, across, samples
+):
+    hold = expand_weight is not None
     positions, channels = crop.shape
     out = conv_flat.shape[1]
     low = positions // 4
@@ -465,23 +453,27 @@
         jax.ShapeDtypeStruct((low, 4 * out), jnp.float32),
         jax.ShapeDtypeStruct((low, 4 * out), jnp.bfloat16),
         jax.ShapeDtypeStruct((low, base), jnp.bfloat16),
-    )
+        jax.ShapeDtypeStruct(down_weight.shape, jnp.bfloat16),
+    )
+    weights = (conv_flat, down_weight)
+    if hold:
+        weights += (expand_weight,)
+        outs += (jax.ShapeDtypeStruct((3 * base, 3 * expand_weight.shape[-1]), jnp.bfloat16),)
     outs += (jax.ShapeDtypeStruct((low, base // samples), jnp.bfloat16),) * (samples - 1)
     scratch = (
         ((positions + 2 * across, channels), jnp.bfloat16),
         ((positions, out), jnp.float32),
         (conv_flat.shape, jnp.bfloat16),
-        (down_weight.shape, jnp.bfloat16),
     )
     return pl.pallas_call(
-        functools.partial(front_kernel, across=across),
+        functools.partial(front_kernel, across=across, hold=int(hold)),
         out_shape=outs,
-        in_specs=[SMEM_SPEC] + [VMEM_SPEC] * 3 + [HBM_SPEC] * 2,
+        in_specs=[SMEM_SPEC] + [VMEM_SPEC] * 2 + [HBM_SPEC] * (1 + len(weights)),
         out_specs=(VMEM_SPEC,) * len(outs),
-        scratch_shapes=[pltpu.VMEM(*item) for item in scratch] + [pltpu.SemaphoreType.DMA((2,))],
-        compiler_params=granted((crop, above, below), outs, scratch, SMALL_MIB),
+        scratch_shapes=[pltpu.VMEM(*item) for item in scratch] + [pltpu.SemaphoreType.DMA((12,))],
+        compiler_params=granted((crop, cross, core_row), outs, scratch, SMALL_MIB),
         name="front_kernel",
-    )(place, crop, above, below, conv_flat, down_weight)
+    )(place, cross, core_row, crop, *weights)
 
 
 def middle_kernel(place_ref, *refs, count, loss_scale, class_count):
@@ -842,20 +834,24 @@
     class_lanes = 128
     own_kernels = inner % 128 == 0 and narrow % 128 == 0
 
-    forward = [(i, i + 1) for i in range(wide - 1)]
-    backward = [(target, source) for source, target in forward]
-    above = lax.ppermute(crop_rows[height - 1], "wide", forward)
-    below = lax.ppermute(crop_rows[0], "wide", backward)
-    columns, hidden_pre, stacked, coarse, *coarse_sends = front_call(
-        place, crop_rows.reshape(height * across, channels), above, below,
-        in_hbm(conv_weight.reshape(9 * channels, -1)), in_hbm(down_weight), across, samples,
-    )
+    first_row, last_row = crop_rows[0], crop_rows[height - 1]
+    even = own % 2 == 0
+    pairs = [(i, i + 1) for i in range(1, wide - 1, 2)]
+    pairs += [(target, source) for source, target in pairs]
+    cross = lax.ppermute(jnp.where(even, first_row, last_row), "wide", pairs)
+    core_row = swap(jnp.where(even, last_row, first_row), "wide", 1)
+    columns, hidden_pre, stacked, coarse, down_held, *rest = front_call(
+        place, in_hbm(crop_rows.reshape(height * across, channels)), cross, core_row,
+        in_hbm(conv_weight.reshape(9 * channels, -1)), in_hbm(down_weight),
+        in_hbm(expand_weight) if own_kernels else None, across, samples,
+    )
+    expand_held, coarse_sends = (rest[0], rest[1:]) if own_kernels else (None, rest)
     stacked_mine = gather_chips(stacked)
     stacked_other = swap_cores(stacked_mine)
     if own_kernels:
-        coarse_part, expand_pre, expanded, *partial = bottleneck_call(
-            forward_kernel, place, stacked_mine + stacked_other, down_weight,
-            in_hbm(expand_weight), in_hbm(reduce_weight), None, low_across, samples,
+        coarse_part, expand_pre, expanded, reduce_held, *partial = bottleneck_call(
+            forward_kernel, place, stacked_mine + stacked_other, down_held, expand_held,
+            in_hbm(reduce_weight), None, low_across, samples,
         )
     else:
         stacked_all = join_blocks(jnp.stack(stacked_mine), jnp.stack(stacked_other))
@@ -879,8 +875,8 @@
     grad_other = swap_cores(grad_mine)
     if own_kernels:
         bottom_part, expanded_grad, *back = bottleneck_call(
-            backward_kernel, place, grad_mine + grad_other, up_weight, expand_weight,
-            reduce_weight, expand_pre, low_across, samples,
+            backward_kernel, place, grad_mine + grad_other, up_weight, expand_held,
+            reduce_held, expand_pre, low_across, samples,
         )
     else:
         grad_all = join_blocks(jnp.stack(grad_mine), jnp.stack(grad_other))

time: 254 us -> 248 us (0.976)
    ppermute x2 -> x1, starting transfers between devices: 4.31 us -> 0.65 us  [step(): cross = lax.ppermute(jnp.where(even, first_row, last_row), 'wide', pairs)]
    pallas_call x2, Pallas kernels: 26.4 us -> 22.9 us  [bottleneck_call(): pl.pallas_call(functools.partial(kernel, blocks=len(pieces) // 2, rows=ro...]
    ppermute x67 -> x68, starting transfers between devices: 75.5 us -> 76.9 us  [swap(): return lax.ppermute(values, axis, [(i, i ^ mask) for i in range(count)])]
    ppermute x67 -> x68, waiting for transfers between devices: 119 us -> 121 us  [swap(): return lax.ppermute(values, axis, [(i, i ^ mask) for i in range(count)])]
  transfers between devices with their start and end apart: 69 -> 69, of which waited for: 31 -> 32; matrix products, arithmetic and copies ran while one was open for 0% -> 0% of each run, Pallas kernels for 5% -> 5%
where the time goes in v3:
time: 248 us
  waiting for transfers between devices  121 us (49%)
  starting transfers between devices  77.6 us (31%)
  Pallas kernels  47.4 us (19%)
    ppermute x68, waiting for transfers between devices, swap(): return lax.ppermute(values, axis, [(i, i ^ mask) for i in range(count)])  121 us
    ppermute x68, starting transfers between devices, swap(): return lax.ppermute(values, axis, [(i, i ^ mask) for i in range(count)])  76.9 us
    pallas_call x2, Pallas kernels, bottleneck_call(): pl.pallas_call(functools.partial(kernel, blocks=len(pieces) // 2, rows=ro...  22.9 us
    pallas_call x2, Pallas kernels, correlate_call(): pl.pallas_call(functools.partial(correlate_kernel, count=count, blocks=le...  11.6 us
  transfers between devices with their start and end apart: 69, of which 32 were waited for; matrix products, arithmetic and copies ran while one was open for 0% of the time, Pallas kernels for 5%

profile of v3, /device:TPU:0, one launch (start us, length us, event | category | flops | bytes accessed | tf_op | source)
XLA Modules:
  0.0 248.2 jit_solution(13012154046109075282)
XLA Ops:
  2.8 3.4 %front_kernel.1 = (bf16[576,384]{1,0:T(8,128)(2,1)S(1)}, f32[96,512]{1,0:T(8,128)S(1)}, bf16[96,512]{1,0:T(8,128)(2,1)S(1)}, bf16[96,1024]{1,0:T(8,128)(2,1)S(1)...) custom-call(s32[3]{0:T(128)S(1)} %pad_add_fusion.place_ref, ...), custom_call_target="tpu_custom_call" | custom-call | tf_op jit(solution)/shard_map/front_kernel/pallas_call | solution.py:468
  6.2 7.8 %collective-permute-start.4 = (bf16[96,512]{1,0:T(8,128)(2,1)S(1)}, bf16[96,512]{1,0:T(8,128)(2,1)S(1)}, u32[]{:S(2)}, u32[]{:S(2)}) collective-permute-start(bf16[96,512]{1,0:T(8,128)(2,1)S(1)} %get-tuple-element.62.refs_0_.refs_6_), channel_id=1, source_target_pairs={{0,24},{4,28},{8,16},{12,20},{16,8},{20,12},{24,0},{28,4},{1,25},{... | collective-permute-start | bytes 294920 | tf_op jit(solution)/shard_map/ppermute | solution.py:14
  21.4 12.2 %shard_map.127 = (bf16[768,256]{1,0:T(8,128)(2,1)S(1)}, f32[768,256]{1,0:T(8,128)S(1)}, bf16[768,256]{1,0:T(8,128)(2,1)S(1)}, bf16[2304,1024]{1,0:T(8,128)(2,1)S...) custom-call(s32[3]{0:T(128)S(1)} %pad_add_fusion.place_ref, ...), custom_call_target="tpu_custom_call" | custom-call | tf_op jit(solution)/shard_map/pallas_call | solution.py:310
  39.2 3.8 %collective-permute-done.11.refs_2_ = bf16[96,1024]{1,0:T(8,128)(2,1)S(1)} collective-permute-done((bf16[96,1024]{1,0:T(8,128)(2,1)S(1)}, bf16[96,1024]{1,0:T(8,128)(2,1)S(1)}, u32[]{:S(2)}, u32[]{:S(2)}) %collective-permute-start.11) | collective-permute-done | bytes 196640 | tf_op jit(solution)/shard_map/ppermute | solution.py:14
  43.0 5.2 %collective-permute-done.13.refs_3_ = bf16[96,1024]{1,0:T(8,128)(2,1)S(1)} collective-permute-done((bf16[96,1024]{1,0:T(8,128)(2,1)S(1)}, bf16[96,1024]{1,0:T(8,128)(2,1)S(1)}, u32[]{:S(2)}, u32[]{:S(2)}) %collective-permute-start.13) | collective-permute-done | bytes 196640 | tf_op jit(solution)/shard_map/ppermute | solution.py:14
  59.3 10.7 %shard_map.128 = (bf16[768,256]{1,0:T(8,128)(2,1)S(1)}, bf16[768,256]{1,0:T(8,128)(2,1)S(1)}, bf16[96,1024]{1,0:T(8,128)(2,1)S(1)}, bf16[96,1024]{1,0:T(8,128)(2...) custom-call(s32[3]{0:T(128)S(1)} %pad_add_fusion.place_ref, ...), custom_call_target="tpu_custom_call" | custom-call | tf_op jit(solution)/shard_map/pallas_call | solution.py:310
  75.4 4.0 %collective-permute-done.25.refs_2_ = bf16[96,1024]{1,0:T(8,128)(2,1)S(1)} collective-permute-done((bf16[96,1024]{1,0:T(8,128)(2,1)S(1)}, bf16[96,1024]{1,0:T(8,128)(2,1)S(1)}, u32[]{:S(2)}, u32[]{:S(2)}) %collective-permute-start.25) | collective-permute-done | bytes 196640 | tf_op jit(solution)/shard_map/ppermute | solution.py:14
  79.4 4.4 %collective-permute-done.27.refs_3_ = bf16[96,1024]{1,0:T(8,128)(2,1)S(1)} collective-permute-done((bf16[96,1024]{1,0:T(8,128)(2,1)S(1)}, bf16[96,1024]{1,0:T(8,128)(2,1)S(1)}, u32[]{:S(2)}, u32[]{:S(2)}) %collective-permute-start.27) | collective-permute-done | bytes 196640 | tf_op jit(solution)/shard_map/ppermute | solution.py:14
  95.6 2.9 %collective-permute-done.38.refs_6_ = bf16[96,256]{1,0:T(8,128)(2,1)S(1)} collective-permute-done((bf16[96,256]{1,0:T(8,128)(2,1)S(1)}, bf16[96,256]{1,0:T(8,128)(2,1)S(1)}, u32[]{:S(2)}, u32[]{:S(2)}) %collective-permute-start.38) | collective-permute-done | bytes 49184 | tf_op jit(solution)/shard_map/ppermute | solution.py:14
  100.7 3.9 %collective-permute-done.39.refs_7_ = bf16[96,256]{1,0:T(8,128)(2,1)S(1)} collective-permute-done((bf16[96,256]{1,0:T(8,128)(2,1)S(1)}, bf16[96,256]{1,0:T(8,128)(2,1)S(1)}, u32[]{:S(2)}, u32[]{:S(2)}) %collective-permute-start.39) | collective-permute-done | bytes 49184 | tf_op jit(solution)/shard_map/ppermute | solution.py:14
  104.6 4.1 %collective-permute-done.40.refs_8_ = bf16[96,256]{1,0:T(8,128)(2,1)S(1)} collective-permute-done((bf16[96,256]{1,0:T(8,128)(2,1)S(1)}, bf16[96,256]{1,0:T(8,128)(2,1)S(1)}, u32[]{:S(2)}, u32[]{:S(2)}) %collective-permute-start.40) | collective-permute-done | bytes 49184 | tf_op jit(solution)/shard_map/ppermute | solution.py:14
  109.9 5.1 %collective-permute-done.41.refs_9_ = bf16[96,256]{1,0:T(8,128)(2,1)S(1)} collective-permute-done((bf16[96,256]{1,0:T(8,128)(2,1)S(1)}, bf16[96,256]{1,0:T(8,128)(2,1)S(1)}, u32[]{:S(2)}, u32[]{:S(2)}) %collective-permute-start.41) | collective-permute-done | bytes 49184 | tf_op jit(solution)/shard_map/ppermute | solution.py:14
  117.2 4.3 %collective-permute-done.42.refs_10_ = bf16[96,256]{1,0:T(8,128)(2,1)S(1)} collective-permute-done((bf16[96,256]{1,0:T(8,128)(2,1)S(1)}, bf16[96,256]{1,0:T(8,128)(2,1)S(1)}, u32[]{:S(2)}, u32[]{:S(2)}) %collective-permute-start.42) | collective-permute-done | bytes 49184 | tf_op jit(solution)/shard_map/ppermute | solution.py:14
  130.2 4.9 %collective-permute-done.43 = bf16[160,256]{1,0:T(8,128)(2,1)S(1)} collective-permute-done((bf16[160,256]{1,0:T(8,128)(2,1)S(1)}, bf16[160,256]{1,0:T(8,128)(2,1)S(1)}, u32[]{:S(2)}, u32[]{:S(2)}) %collective-permute-start.43) | collective-permute-done | bytes 81952 | tf_op jit(solution)/shard_map/ppermute | solution.py:14
  136.6 27.7 %collective-permute-done.44 = bf16[160,256]{1,0:T(8,128)(2,1)S(1)} collective-permute-done((bf16[160,256]{1,0:T(8,128)(2,1)S(1)}, bf16[160,256]{1,0:T(8,128)(2,1)S(1)}, u32[]{:S(2)}, u32[]{:S(2)}) %collective-permute-start.44) | collective-permute-done | bytes 81952 | tf_op jit(solution)/shard_map/ppermute | solution.py:14
  168.8 11.6 %collective-permute-done.67.refs_2_ = bf16[768,256]{1,0:T(8,128)(2,1)S(1)} collective-permute-done((bf16[768,256]{1,0:T(8,128)(2,1)S(1)}, bf16[768,256]{1,0:T(8,128)(2,1)S(1)}, u32[]{:S(2)}, u32[]{:S(2)}) %collective-permute-start.67) | collective-permute-done | bytes 393248 | tf_op jit(solution)/shard_map/ppermute | solution.py:14
  180.5 16.5 %collective-permute-start.46 = (bf16[160,256]{1,0:T(8,128)(2,1)S(1)}, bf16[160,256]{1,0:T(8,128)(2,1)S(1)}, u32[]{:S(2)}, u32[]{:S(2)}) collective-permute-start(bf16[160,256]{1,0:T(8,128)(2,1)S(1)} %add_convert_fusion.9), channel_id=1, source_target_pairs={{0,1},{1,0},{2,3},{3,2},{4,5},{5,4},{6,7},{7,6},{8,9},{9,8},{10,11... | collective-permute-start | bytes 245768 | tf_op jit(solution)/shard_map/ppermute | solution.py:14
  205.5 4.8 %collective-permute-done.61.refs_8_ = bf16[576,256]{1,0:T(8,128)(2,1)S(1)} collective-permute-done((bf16[576,256]{1,0:T(8,128)(2,1)S(1)}, bf16[576,256]{1,0:T(8,128)(2,1)S(1)}, u32[]{:S(2)}, u32[]{:S(2)}) %collective-permute-start.61) | collective-permute-done | bytes 294944 | tf_op jit(solution)/shard_map/ppermute | solution.py:14
  211.3 9.7 %collective-permute-done.60.refs_7_ = bf16[576,256]{1,0:T(8,128)(2,1)S(1)} collective-permute-done((bf16[576,256]{1,0:T(8,128)(2,1)S(1)}, bf16[576,256]{1,0:T(8,128)(2,1)S(1)}, u32[]{:S(2)}, u32[]{:S(2)}) %collective-permute-start.60) | collective-permute-done | bytes 294944 | tf_op jit(solution)/shard_map/ppermute | solution.py:14
  223.7 4.3 %collective-permute-done.50.refs_2_ = bf16[160,1024]{1,0:T(8,128)(2,1)S(1)} collective-permute-done((bf16[160,1024]{1,0:T(8,128)(2,1)S(1)}, bf16[160,1024]{1,0:T(8,128)(2,1)S(1)}, u32[]{:S(2)}, u32[]{:S(2)}) %collective-permute-start.50) | collective-permute-done | bytes 327712 | tf_op jit(solution)/shard_map/ppermute | solution.py:14
  229.0 5.8 %correlate_kernel.2 = f32[3,3,256,256]{3,2,1,0:T(8,128)} custom-call(s32[3]{0:T(128)S(1)} %pad_add_fusion.place_ref, bf16[768,256]{1,0:T(8,128)(2,1)S(1)} %get-tuple-element.111.refs_0_, bf16[768,256]{1,0:T(8,128)(2,1)S(1)} %collective-permute-done.56.refs_1_, bf16[768,256]{1,0:T(8,128)(2,1)S(1)} %collective-permute-done.57.refs_2_, ...), custom_call_target="tpu_custom_call" | custom-call | tf_op jit(solution)/shard_map/correlate_kernel/pallas_call | solution.py:374
  234.8 4.2 %collective-permute-done.66.refs_1_ = bf16[768,256]{1,0:T(8,128)(2,1)S(1)} collective-permute-done((bf16[768,256]{1,0:T(8,128)(2,1)S(1)}, bf16[768,256]{1,0:T(8,128)(2,1)S(1)}, u32[]{:S(2)}, u32[]{:S(2)}) %collective-permute-start.66) | collective-permute-done | bytes 393248 | tf_op jit(solution)/shard_map/ppermute | solution.py:14
  239.0 5.8 %correlate_kernel.3 = f32[3,3,256,256]{3,2,1,0:T(8,128)} custom-call(s32[3]{0:T(128)S(1)} %pad_add_fusion.place_ref, bf16[768,256]{1,0:T(8,128)(2,1)S(1)} %get-tuple-element.114.refs_0_, bf16[768,256]{1,0:T(8,128)(2,1)S(1)} %collective-permute-done.66.refs_1_, bf16[768,256]{1,0:T(8,128)(2,1)S(1)} %collective-permute-done.67.refs_2_, ...), custom_call_target="tpu_custom_call" | custom-call | tf_op jit(solution)/shard_map/correlate_kernel/pallas_call | solution.py:374
  244.8 3.2 %unpack_kernel.1 = (f32[512,1024]{1,0:T(8,128)}, f32[1024,512]{1,0:T(8,128)}, f32[1152,128]{1,0:T(8,128)}, f32[9,128]{1,0:T(8,128)}) custom-call(s32[3]{0:T(128)S(1)} %pad_add_fusion.place_ref, bf16[160,1024]{1,0:T(8,128)(2,1)S(1)} %pad_maximum_fusion.refs_0_, bf16[160,1024]{1,0:T(8,128)(2,1)S(1)} %collective-permute-done.49.refs_1_, ...), custom_call_target="tpu_custom_call" | custom-call | tf_op jit(solution)/shard_map/unpack_kernel/pallas_call | solution.py:728
  (144 shorter events, 76.9 us)
Async XLA Ops:
  37.0 11.2 %collective-permute-start.13 = (bf16[96,1024]{1,0:T(8,128)(2,1)S(1)}, bf16[96,1024]{1,0:T(8,128)(2,1)S(1)}, u32[]{:S(2)}, u32[]{:S(2)}) collective-permute-start(bf16[96,1024]{1,0:T(8,128)(2,1)S(1)} %add_convert_fusion.7), channel_id=1, source_target_pairs={{0,16},{4,20},{8,24},{12,28},{16,0},{20,4},{24,8},{28,12},{1,17},{... | collective-permute-start | bytes 589832 | tf_op jit(solution)/shard_map/ppermute | solution.py:14
  88.5 35.2 %collective-permute-start.30 = (bf16[160,1024]{1,0:T(8,128)(2,1)S(1)}, bf16[160,1024]{1,0:T(8,128)(2,1)S(1)}, u32[]{:S(2)}, u32[]{:S(2)}) collective-permute-start(bf16[160,1024]{1,0:T(8,128)(2,1)S(1)} %get-tuple-element.92), channel_id=1, source_target_pairs={{0,4},{4,0},{8,12},{12,8},{16,20},{20,16},{24,28},{28,24},{1,5},{5... | collective-permute-start | bytes 983048 | tf_op jit(solution)/shard_map/ppermute | solution.py:14
  89.2 34.6 %collective-permute-start.32 = (bf16[160,1024]{1,0:T(8,128)(2,1)S(1)}, bf16[160,1024]{1,0:T(8,128)(2,1)S(1)}, u32[]{:S(2)}, u32[]{:S(2)}) collective-permute-start(bf16[160,1024]{1,0:T(8,128)(2,1)S(1)} %add_convert_fusion.2), channel_id=1, source_target_pairs={{0,8},{4,12},{8,0},{12,4},{16,24},{20,28},{24,16},{28,20},{1,9},{5... | collective-permute-start | bytes 983048 | tf_op jit(solution)/shard_map/ppermute | solution.py:14
  90.4 33.4 %collective-permute-start.34 = (bf16[160,1024]{1,0:T(8,128)(2,1)S(1)}, bf16[160,1024]{1,0:T(8,128)(2,1)S(1)}, u32[]{:S(2)}, u32[]{:S(2)}) collective-permute-start(bf16[160,1024]{1,0:T(8,128)(2,1)S(1)} %add_convert_fusion.1), channel_id=1, source_target_pairs={{0,16},{4,20},{8,24},{12,28},{16,0},{20,4},{24,8},{28,12},{1,17},{... | collective-permute-start | bytes 983048 | tf_op jit(solution)/shard_map/ppermute | solution.py:14
  91.4 32.4 %collective-permute-start.36 = (bf16[160,1024]{1,0:T(8,128)(2,1)S(1)}, bf16[160,1024]{1,0:T(8,128)(2,1)S(1)}, u32[]{:S(2)}, u32[]{:S(2)}) collective-permute-start(bf16[160,1024]{1,0:T(8,128)(2,1)S(1)} %add_convert_fusion), channel_id=1, source_target_pairs={{0,24},{4,28},{8,16},{12,20},{16,8},{20,12},{24,0},{28,4},{1,25},{... | collective-permute-start | bytes 983048 | tf_op jit(solution)/shard_map/ppermute | solution.py:14
  121.5 45.3 %collective-permute-start.68 = (bf16[768,256]{1,0:T(8,128)(2,1)S(1)}, bf16[768,256]{1,0:T(8,128)(2,1)S(1)}, u32[]{:S(2)}, u32[]{:S(2)}) collective-permute-start(bf16[768,256]{1,0:T(8,128)(2,1)S(1)} %get-tuple-element.114.refs_0_), channel_id=1, source_target_pairs={{0,3},{1,2},{2,1},{3,0},{4,7},{5,6},{6,5},{7,4},{8,11},{9,10},{10,... | collective-permute-start | bytes 1179656 | tf_op jit(solution)/shard_map/ppermute | solution.py:14
  125.2 39.1 %collective-permute-start.44 = (bf16[160,256]{1,0:T(8,128)(2,1)S(1)}, bf16[160,256]{1,0:T(8,128)(2,1)S(1)}, u32[]{:S(2)}, u32[]{:S(2)}) collective-permute-start(bf16[160,256]{1,0:T(8,128)(2,1)S(1)} %get-tuple-element.107), channel_id=1, source_target_pairs={{0,2},{1,3},{2,0},{3,1},{4,6},{5,7},{6,4},{7,5},{8,10},{9,11},{10,... | collective-permute-start | bytes 245768 | tf_op jit(solution)/shard_map/ppermute | solution.py:14
  127.0 37.4 %collective-permute-start.45 = (bf16[160,256]{1,0:T(8,128)(2,1)S(1)}, bf16[160,256]{1,0:T(8,128)(2,1)S(1)}, u32[]{:S(2)}, u32[]{:S(2)}) collective-permute-start(bf16[160,256]{1,0:T(8,128)(2,1)S(1)} %get-tuple-element.108), channel_id=1, source_target_pairs={{0,3},{1,2},{2,1},{3,0},{4,7},{5,6},{6,5},{7,4},{8,11},{9,10},{10,... | collective-permute-start | bytes 245768 | tf_op jit(solution)/shard_map/ppermute | solution.py:14
  129.2 51.2 %collective-permute-start.67 = (bf16[768,256]{1,0:T(8,128)(2,1)S(1)}, bf16[768,256]{1,0:T(8,128)(2,1)S(1)}, u32[]{:S(2)}, u32[]{:S(2)}) collective-permute-start(bf16[768,256]{1,0:T(8,128)(2,1)S(1)} %get-tuple-element.114.refs_0_), channel_id=1, source_target_pairs={{0,2},{1,3},{2,0},{3,1},{4,6},{5,7},{6,4},{7,5},{8,10},{9,11},{10,... | collective-permute-start | bytes 1179656 | tf_op jit(solution)/shard_map/ppermute | solution.py:14
  135.0 65.6 %collective-permute-start.58 = (bf16[768,256]{1,0:T(8,128)(2,1)S(1)}, bf16[768,256]{1,0:T(8,128)(2,1)S(1)}, u32[]{:S(2)}, u32[]{:S(2)}) collective-permute-start(bf16[768,256]{1,0:T(8,128)(2,1)S(1)} %get-tuple-element.111.refs_0_), channel_id=1, source_target_pairs={{0,3},{1,2},{2,1},{3,0},{4,7},{5,6},{6,5},{7,4},{8,11},{9,10},{10,... | collective-permute-start | bytes 1179656 | tf_op jit(solution)/shard_map/ppermute | solution.py:14
  164.3 38.1 %collective-permute-start.57 = (bf16[768,256]{1,0:T(8,128)(2,1)S(1)}, bf16[768,256]{1,0:T(8,128)(2,1)S(1)}, u32[]{:S(2)}, u32[]{:S(2)}) collective-permute-start(bf16[768,256]{1,0:T(8,128)(2,1)S(1)} %get-tuple-element.111.refs_0_), channel_id=1, source_target_pairs={{0,2},{1,3},{2,0},{3,1},{4,6},{5,7},{6,4},{7,5},{8,10},{9,11},{10,... | collective-permute-start | bytes 1179656 | tf_op jit(solution)/shard_map/ppermute | solution.py:14
  164.3 39.2 %collective-permute-start.56 = (bf16[768,256]{1,0:T(8,128)(2,1)S(1)}, bf16[768,256]{1,0:T(8,128)(2,1)S(1)}, u32[]{:S(2)}, u32[]{:S(2)}) collective-permute-start(bf16[768,256]{1,0:T(8,128)(2,1)S(1)} %get-tuple-element.111.refs_0_), channel_id=1, source_target_pairs={{0,1},{1,0},{2,3},{3,2},{4,5},{5,4},{6,7},{7,6},{8,9},{9,8},{10,11... | collective-permute-start | bytes 1179656 | tf_op jit(solution)/shard_map/ppermute | solution.py:14
  166.8 13.7 %collective-permute-start.48 = (bf16[160,256]{1,0:T(8,128)(2,1)S(1)}, bf16[160,256]{1,0:T(8,128)(2,1)S(1)}, u32[]{:S(2)}, u32[]{:S(2)}) collective-permute-start(bf16[160,256]{1,0:T(8,128)(2,1)S(1)} %add_convert_fusion.9), channel_id=1, source_target_pairs={{0,3},{1,2},{2,1},{3,0},{4,7},{5,6},{6,5},{7,4},{8,11},{9,10},{10,... | collective-permute-start | bytes 245768 | tf_op jit(solution)/shard_map/ppermute | solution.py:14
  180.5 16.8 %collective-permute-start.47 = (bf16[160,256]{1,0:T(8,128)(2,1)S(1)}, bf16[160,256]{1,0:T(8,128)(2,1)S(1)}, u32[]{:S(2)}, u32[]{:S(2)}) collective-permute-start(bf16[160,256]{1,0:T(8,128)(2,1)S(1)} %add_convert_fusion.9), channel_id=1, source_target_pairs={{0,2},{1,3},{2,0},{3,1},{4,6},{5,7},{6,4},{7,5},{8,10},{9,11},{10,... | collective-permute-start | bytes 245768 | tf_op jit(solution)/shard_map/ppermute | solution.py:14
  180.5 18.9 %collective-permute-start.46 = (bf16[160,256]{1,0:T(8,128)(2,1)S(1)}, bf16[160,256]{1,0:T(8,128)(2,1)S(1)}, u32[]{:S(2)}, u32[]{:S(2)}) collective-permute-start(bf16[160,256]{1,0:T(8,128)(2,1)S(1)} %add_convert_fusion.9), channel_id=1, source_target_pairs={{0,1},{1,0},{2,3},{3,2},{4,5},{5,4},{6,7},{7,6},{8,9},{9,8},{10,11... | collective-permute-start | bytes 245768 | tf_op jit(solution)/shard_map/ppermute | solution.py:14
  200.7 22.5 %collective-permute-start.51 = (bf16[160,1024]{1,0:T(8,128)(2,1)S(1)}, bf16[160,1024]{1,0:T(8,128)(2,1)S(1)}, u32[]{:S(2)}, u32[]{:S(2)}) collective-permute-start(bf16[160,1024]{1,0:T(8,128)(2,1)S(1)} %pad_maximum_fusion.refs_0_), channel_id=1, source_target_pairs={{0,24},{4,28},{8,16},{12,20},{16,8},{20,12},{24,0},{28,4},{1,25},{... | collective-permute-start | bytes 983048 | tf_op jit(solution)/shard_map/ppermute | solution.py:14
  202.4 18.6 %collective-permute-start.60 = (bf16[576,256]{1,0:T(8,128)(2,1)S(1)}, bf16[576,256]{1,0:T(8,128)(2,1)S(1)}, u32[]{:S(2)}, u32[]{:S(2)}) collective-permute-start(bf16[576,256]{1,0:T(8,128)(2,1)S(1)} %get-tuple-element.113.refs_5_), channel_id=1, source_target_pairs={{0,16},{4,20},{8,24},{12,28},{16,0},{20,4},{24,8},{28,12},{1,17},{... | collective-permute-start | bytes 884744 | tf_op jit(solution)/shard_map/ppermute | solution.py:14
  203.5 19.7 %collective-permute-start.59 = (bf16[576,256]{1,0:T(8,128)(2,1)S(1)}, bf16[576,256]{1,0:T(8,128)(2,1)S(1)}, u32[]{:S(2)}, u32[]{:S(2)}) collective-permute-start(bf16[576,256]{1,0:T(8,128)(2,1)S(1)} %get-tuple-element.113.refs_5_), channel_id=1, source_target_pairs={{0,8},{4,12},{8,0},{12,4},{16,24},{20,28},{24,16},{28,20},{1,9},{5... | collective-permute-start | bytes 884744 | tf_op jit(solution)/shard_map/ppermute | solution.py:14
  204.2 23.7 %collective-permute-start.50 = (bf16[160,1024]{1,0:T(8,128)(2,1)S(1)}, bf16[160,1024]{1,0:T(8,128)(2,1)S(1)}, u32[]{:S(2)}, u32[]{:S(2)}) collective-permute-start(bf16[160,1024]{1,0:T(8,128)(2,1)S(1)} %pad_maximum_fusion.refs_0_), channel_id=1, source_target_pairs={{0,16},{4,20},{8,24},{12,28},{16,0},{20,4},{24,8},{28,12},{1,17},{... | collective-permute-start | bytes 983048 | tf_op jit(solution)/shard_map/ppermute | solution.py:14
  210.2 17.7 %collective-permute-start.49 = (bf16[160,1024]{1,0:T(8,128)(2,1)S(1)}, bf16[160,1024]{1,0:T(8,128)(2,1)S(1)}, u32[]{:S(2)}, u32[]{:S(2)}) collective-permute-start(bf16[160,1024]{1,0:T(8,128)(2,1)S(1)} %pad_maximum_fusion.refs_0_), channel_id=1, source_target_pairs={{0,8},{4,12},{8,0},{12,4},{16,24},{20,28},{24,16},{28,20},{1,9},{5... | collective-permute-start | bytes 983048 | tf_op jit(solution)/shard_map/ppermute | solution.py:14
  228.0 16.8 %collective-permute-start.52 = (bf16[160,1024]{1,0:T(8,128)(2,1)S(1)}, bf16[160,1024]{1,0:T(8,128)(2,1)S(1)}, u32[]{:S(2)}, u32[]{:S(2)}) collective-permute-start(bf16[160,1024]{1,0:T(8,128)(2,1)S(1)} %pad_maximum_fusion.refs_0_), channel_id=1, source_target_pairs={{0,4},{4,0},{8,12},{12,8},{16,20},{20,16},{24,28},{28,24},{1,5},{5... | collective-permute-start | bytes 983048 | tf_op jit(solution)/shard_map/ppermute | solution.py:14
  228.0 16.8 %collective-permute-start.55 = (bf16[160,1024]{1,0:T(8,128)(2,1)S(1)}, bf16[160,1024]{1,0:T(8,128)(2,1)S(1)}, u32[]{:S(2)}, u32[]{:S(2)}) collective-permute-start(bf16[160,1024]{1,0:T(8,128)(2,1)S(1)} %collective-permute-done.51.refs_3_), channel_id=1, source_target_pairs={{0,4},{4,0},{8,12},{12,8},{16,20},{20,16},{24,28},{28,24},{1,5},{5... | collective-permute-start | bytes 983048 | tf_op jit(solution)/shard_map/ppermute | solution.py:14
  228.5 16.3 %collective-permute-start.54 = (bf16[160,1024]{1,0:T(8,128)(2,1)S(1)}, bf16[160,1024]{1,0:T(8,128)(2,1)S(1)}, u32[]{:S(2)}, u32[]{:S(2)}) collective-permute-start(bf16[160,1024]{1,0:T(8,128)(2,1)S(1)} %collective-permute-done.50.refs_2_), channel_id=1, source_target_pairs={{0,4},{4,0},{8,12},{12,8},{16,20},{20,16},{24,28},{28,24},{1,5},{5... | collective-permute-start | bytes 983048 | tf_op jit(solution)/shard_map/ppermute | solution.py:14
  228.6 16.2 %collective-permute-start.53 = (bf16[160,1024]{1,0:T(8,128)(2,1)S(1)}, bf16[160,1024]{1,0:T(8,128)(2,1)S(1)}, u32[]{:S(2)}, u32[]{:S(2)}) collective-permute-start(bf16[160,1024]{1,0:T(8,128)(2,1)S(1)} %collective-permute-done.49.refs_1_), channel_id=1, source_target_pairs={{0,4},{4,0},{8,12},{12,8},{16,20},{20,16},{24,28},{28,24},{1,5},{5... | collective-permute-start | bytes 983048 | tf_op jit(solution)/shard_map/ppermute | solution.py:14
  (49 other events, 335.6 us)

commit v4 on v3

--- a/solution.py
+++ b/solution.py
@@ -593,6 +593,11 @@
     )
 
 
+def pack_start(place_ref, relative, half, rows, lanes):
+    start = pl.multiple_of((place_ref[1] ^ relative) * rows, 16)
+    return start, pl.multiple_of((place_ref[0] ^ half) * lanes, 128)
+
+
 def pack_kernel(place_ref, *refs, count, blocks, rows, across):
     first_ref, terms = refs[0], refs[1:count]
     (
@@ -655,20 +660,20 @@
     if base < pack_ref.shape[0]:
         pack_ref[base:, :] = jnp.zeros((pack_ref.shape[0] - base, lanes), pack_ref.dtype)
     for index, target in enumerate(targets):
-        start = block_start(place_ref, index % blocks, index // blocks, rows)
-        target[...] = pack_ref[pl.ds(start, rows), :]
+        start, lane = pack_start(place_ref, index % blocks, index // blocks, rows, lanes // 2)
+        target[...] = pack_ref[pl.ds(start, rows), pl.ds(lane, lanes // 2)]
 
 
 def pack_call(place, first, terms, operands, filled, blocks, across):
     lanes = first.shape[1]
     channels = operands[5].shape[1] // 3
     positions = 4 * first.shape[0]
-    unit = 32 * blocks
+    unit = 16 * blocks
     padded = -(-filled // unit) * unit
-    block = jax.ShapeDtypeStruct((padded // (2 * blocks), lanes), jnp.bfloat16)
+    block = jax.ShapeDtypeStruct((padded // blocks, lanes // 2), jnp.bfloat16)
     return pl.pallas_call(
         functools.partial(
-            pack_kernel, count=1 + len(terms), blocks=blocks, rows=padded // (2 * blocks),
+            pack_kernel, count=1 + len(terms), blocks=blocks, rows=padded // blocks,
             across=across,
         ),
         out_shape=(block,) * (2 * blocks),
@@ -697,11 +702,13 @@
     pack_ref, sems = refs[2 * blocks + 2 * outs :]
     lanes = pack_ref.shape[1]
     rows = pieces[0].shape[0]
-    narrow = lanes // count
+    narrow = lanes // (2 * count)
     for index, piece in enumerate(pieces):
-        start = block_start(place_ref, index % blocks, index // blocks, rows)
+        start, core_lane = pack_start(
+            place_ref, index % blocks, index // blocks, rows, lanes // 2
+        )
         for mask in range(count):
-            lane = pl.multiple_of((place_ref[2] ^ mask) * narrow, 128)
+            lane = pl.multiple_of(core_lane + (place_ref[2] ^ mask) * narrow, 128)
             pack_ref[pl.ds(start, rows), pl.ds(lane, narrow)] = piece[
                 :, mask * narrow : (mask + 1) * narrow
             ]
@@ -724,7 +731,7 @@
 def unpack_call(place, pieces, count, out_shapes, shapes):
     rows, lanes = pieces[0].shape
     outs = tuple(jax.ShapeDtypeStruct(shape, jnp.float32) for shape in out_shapes)
-    scratch = ((rows * len(pieces), lanes), jnp.bfloat16)
+    scratch = ((rows * len(pieces) // 2, 2 * lanes), jnp.bfloat16)
     return pl.pallas_call(
         functools.partial(
             unpack_kernel, blocks=len(pieces) // 2, count=count, shapes=shapes

time: 248 us -> 246 us (level)
  starting transfers between devices: 77.6 us -> 68.4 us
  waiting for transfers between devices: 121 us -> 127 us
    ppermute x68, starting transfers between devices: 76.9 us -> 67.8 us  [swap(): return lax.ppermute(values, axis, [(i, i ^ mask) for i in range(count)])]
    ppermute x68, waiting for transfers between devices: 121 us -> 127 us  [swap(): return lax.ppermute(values, axis, [(i, i ^ mask) for i in range(count)])]
where the time goes in v4:
time: 246 us
  waiting for transfers between devices  127 us (52%)
  starting transfers between devices  68.4 us (28%)
  Pallas kernels  47.7 us (19%)
    ppermute x68, waiting for transfers between devices, swap(): return lax.ppermute(values, axis, [(i, i ^ mask) for i in range(count)])  127 us
    ppermute x68, starting transfers between devices, swap(): return lax.ppermute(values, axis, [(i, i ^ mask) for i in range(count)])  67.8 us
    pallas_call x2, Pallas kernels, bottleneck_call(): pl.pallas_call(functools.partial(kernel, blocks=len(pieces) // 2, rows=ro...  22.9 us
    pallas_call x2, Pallas kernels, correlate_call(): pl.pallas_call(functools.partial(correlate_kernel, count=count, blocks=le...  11.6 us
  transfers between devices with their start and end apart: 69, of which 32 were waited for; matrix products, arithmetic and copies ran while one was open for 0% of the time, Pallas kernels for 5%

profile of v4, /device:TPU:0, one launch (start us, length us, event | category | flops | bytes accessed | tf_op | source)
XLA Modules:
  0.0 245.9 jit_solution(5401929257778948769)
XLA Ops:
  6.2 7.8 %collective-permute-start.4 = (bf16[96,512]{1,0:T(8,128)(2,1)S(1)}, bf16[96,512]{1,0:T(8,128)(2,1)S(1)}, u32[]{:S(2)}, u32[]{:S(2)}) collective-permute-start(bf16[96,512]{1,0:T(8,128)(2,1)S(1)} %get-tuple-element.62.refs_0_.refs_6_), channel_id=1, source_target_pairs={{0,24},{4,28},{8,16},{12,20},{16,8},{20,12},{24,0},{28,4},{1,25},{... | collective-permute-start | bytes 294920 | tf_op jit(solution)/shard_map/ppermute | solution.py:14
  21.4 12.2 %shard_map.127 = (bf16[768,256]{1,0:T(8,128)(2,1)S(1)}, f32[768,256]{1,0:T(8,128)S(1)}, bf16[768,256]{1,0:T(8,128)(2,1)S(1)}, bf16[2304,1024]{1,0:T(8,128)(2,1)S...) custom-call(s32[3]{0:T(128)S(1)} %pad_add_fusion.place_ref, ...), custom_call_target="tpu_custom_call" | custom-call | tf_op jit(solution)/shard_map/pallas_call | solution.py:310
  39.2 3.8 %collective-permute-done.11.refs_2_ = bf16[96,1024]{1,0:T(8,128)(2,1)S(1)} collective-permute-done((bf16[96,1024]{1,0:T(8,128)(2,1)S(1)}, bf16[96,1024]{1,0:T(8,128)(2,1)S(1)}, u32[]{:S(2)}, u32[]{:S(2)}) %collective-permute-start.11) | collective-permute-done | bytes 196640 | tf_op jit(solution)/shard_map/ppermute | solution.py:14
  43.0 5.2 %collective-permute-done.13.refs_3_ = bf16[96,1024]{1,0:T(8,128)(2,1)S(1)} collective-permute-done((bf16[96,1024]{1,0:T(8,128)(2,1)S(1)}, bf16[96,1024]{1,0:T(8,128)(2,1)S(1)}, u32[]{:S(2)}, u32[]{:S(2)}) %collective-permute-start.13) | collective-permute-done | bytes 196640 | tf_op jit(solution)/shard_map/ppermute | solution.py:14
  59.3 10.7 %shard_map.128 = (bf16[768,256]{1,0:T(8,128)(2,1)S(1)}, bf16[768,256]{1,0:T(8,128)(2,1)S(1)}, bf16[96,1024]{1,0:T(8,128)(2,1)S(1)}, bf16[96,1024]{1,0:T(8,128)(2...) custom-call(s32[3]{0:T(128)S(1)} %pad_add_fusion.place_ref, ...), custom_call_target="tpu_custom_call" | custom-call | tf_op jit(solution)/shard_map/pallas_call | solution.py:310
  75.4 4.0 %collective-permute-done.25.refs_2_ = bf16[96,1024]{1,0:T(8,128)(2,1)S(1)} collective-permute-done((bf16[96,1024]{1,0:T(8,128)(2,1)S(1)}, bf16[96,1024]{1,0:T(8,128)(2,1)S(1)}, u32[]{:S(2)}, u32[]{:S(2)}) %collective-permute-start.25) | collective-permute-done | bytes 196640 | tf_op jit(solution)/shard_map/ppermute | solution.py:14
  79.4 4.4 %collective-permute-done.27.refs_3_ = bf16[96,1024]{1,0:T(8,128)(2,1)S(1)} collective-permute-done((bf16[96,1024]{1,0:T(8,128)(2,1)S(1)}, bf16[96,1024]{1,0:T(8,128)(2,1)S(1)}, u32[]{:S(2)}, u32[]{:S(2)}) %collective-permute-start.27) | collective-permute-done | bytes 196640 | tf_op jit(solution)/shard_map/ppermute | solution.py:14
  96.4 5.7 %collective-permute-done.39.refs_7_ = bf16[96,256]{1,0:T(8,128)(2,1)S(1)} collective-permute-done((bf16[96,256]{1,0:T(8,128)(2,1)S(1)}, bf16[96,256]{1,0:T(8,128)(2,1)S(1)}, u32[]{:S(2)}, u32[]{:S(2)}) %collective-permute-start.39) | collective-permute-done | bytes 49184 | tf_op jit(solution)/shard_map/ppermute | solution.py:14
  102.2 4.1 %collective-permute-done.40.refs_8_ = bf16[96,256]{1,0:T(8,128)(2,1)S(1)} collective-permute-done((bf16[96,256]{1,0:T(8,128)(2,1)S(1)}, bf16[96,256]{1,0:T(8,128)(2,1)S(1)}, u32[]{:S(2)}, u32[]{:S(2)}) %collective-permute-start.40) | collective-permute-done | bytes 49184 | tf_op jit(solution)/shard_map/ppermute | solution.py:14
  106.2 5.2 %collective-permute-done.41.refs_9_ = bf16[96,256]{1,0:T(8,128)(2,1)S(1)} collective-permute-done((bf16[96,256]{1,0:T(8,128)(2,1)S(1)}, bf16[96,256]{1,0:T(8,128)(2,1)S(1)}, u32[]{:S(2)}, u32[]{:S(2)}) %collective-permute-start.41) | collective-permute-done | bytes 49184 | tf_op jit(solution)/shard_map/ppermute | solution.py:14
  111.5 6.3 %collective-permute-done.42.refs_10_ = bf16[96,256]{1,0:T(8,128)(2,1)S(1)} collective-permute-done((bf16[96,256]{1,0:T(8,128)(2,1)S(1)}, bf16[96,256]{1,0:T(8,128)(2,1)S(1)}, u32[]{:S(2)}, u32[]{:S(2)}) %collective-permute-start.42) | collective-permute-done | bytes 49184 | tf_op jit(solution)/shard_map/ppermute | solution.py:14
  118.8 4.4 %collective-permute-start.43 = (bf16[304,128]{1,0:T(8,128)(2,1)S(1)}, bf16[304,128]{1,0:T(8,128)(2,1)S(1)}, u32[]{:S(2)}, u32[]{:S(2)}) collective-permute-start(bf16[304,128]{1,0:T(8,128)(2,1)S(1)} %get-tuple-element.106), channel_id=1, source_target_pairs={{0,1},{1,0},{2,3},{3,2},{4,5},{5,4},{6,7},{7,6},{8,9},{9,8},{10,11... | collective-permute-start | bytes 233480 | tf_op jit(solution)/shard_map/ppermute | solution.py:14
  125.7 11.2 %collective-permute-done.43 = bf16[304,128]{1,0:T(8,128)(2,1)S(1)} collective-permute-done((bf16[304,128]{1,0:T(8,128)(2,1)S(1)}, bf16[304,128]{1,0:T(8,128)(2,1)S(1)}, u32[]{:S(2)}, u32[]{:S(2)}) %collective-permute-start.43) | collective-permute-done | bytes 77856 | tf_op jit(solution)/shard_map/ppermute | solution.py:14
  136.9 4.3 %collective-permute-start.58 = (bf16[768,256]{1,0:T(8,128)(2,1)S(1)}, bf16[768,256]{1,0:T(8,128)(2,1)S(1)}, u32[]{:S(2)}, u32[]{:S(2)}) collective-permute-start(bf16[768,256]{1,0:T(8,128)(2,1)S(1)} %get-tuple-element.111.refs_0_), channel_id=1, source_target_pairs={{0,3},{1,2},{2,1},{3,0},{4,7},{5,6},{6,5},{7,4},{8,11},{9,10},{10,... | collective-permute-start | bytes 1179656 | tf_op jit(solution)/shard_map/ppermute | solution.py:14
  141.2 27.5 %collective-permute-done.44 = bf16[304,128]{1,0:T(8,128)(2,1)S(1)} collective-permute-done((bf16[304,128]{1,0:T(8,128)(2,1)S(1)}, bf16[304,128]{1,0:T(8,128)(2,1)S(1)}, u32[]{:S(2)}, u32[]{:S(2)}) %collective-permute-start.44) | collective-permute-done | bytes 77856 | tf_op jit(solution)/shard_map/ppermute | solution.py:14
  173.3 11.4 %collective-permute-done.48 = bf16[304,128]{1,0:T(8,128)(2,1)S(1)} collective-permute-done((bf16[304,128]{1,0:T(8,128)(2,1)S(1)}, bf16[304,128]{1,0:T(8,128)(2,1)S(1)}, u32[]{:S(2)}, u32[]{:S(2)}) %collective-permute-start.48) | collective-permute-done | bytes 77856 | tf_op jit(solution)/shard_map/ppermute | solution.py:14
  184.7 10.3 %collective-permute-start.46 = (bf16[304,128]{1,0:T(8,128)(2,1)S(1)}, bf16[304,128]{1,0:T(8,128)(2,1)S(1)}, u32[]{:S(2)}, u32[]{:S(2)}) collective-permute-start(bf16[304,128]{1,0:T(8,128)(2,1)S(1)} %add_convert_fusion.9), channel_id=1, source_target_pairs={{0,1},{1,0},{2,3},{3,2},{4,5},{5,4},{6,7},{7,6},{8,9},{9,8},{10,11... | collective-permute-start | bytes 233480 | tf_op jit(solution)/shard_map/ppermute | solution.py:14
  203.4 4.8 %collective-permute-done.61.refs_8_ = bf16[576,256]{1,0:T(8,128)(2,1)S(1)} collective-permute-done((bf16[576,256]{1,0:T(8,128)(2,1)S(1)}, bf16[576,256]{1,0:T(8,128)(2,1)S(1)}, u32[]{:S(2)}, u32[]{:S(2)}) %collective-permute-start.61) | collective-permute-done | bytes 294944 | tf_op jit(solution)/shard_map/ppermute | solution.py:14
  209.2 9.5 %collective-permute-done.60.refs_7_ = bf16[576,256]{1,0:T(8,128)(2,1)S(1)} collective-permute-done((bf16[576,256]{1,0:T(8,128)(2,1)S(1)}, bf16[576,256]{1,0:T(8,128)(2,1)S(1)}, u32[]{:S(2)}, u32[]{:S(2)}) %collective-permute-start.60) | collective-permute-done | bytes 294944 | tf_op jit(solution)/shard_map/ppermute | solution.py:14
  220.8 4.4 %collective-permute-done.50.refs_2_ = bf16[304,512]{1,0:T(8,128)(2,1)S(1)} collective-permute-done((bf16[304,512]{1,0:T(8,128)(2,1)S(1)}, bf16[304,512]{1,0:T(8,128)(2,1)S(1)}, u32[]{:S(2)}, u32[]{:S(2)}) %collective-permute-start.50) | collective-permute-done | bytes 311328 | tf_op jit(solution)/shard_map/ppermute | solution.py:14
  226.3 5.8 %correlate_kernel.2 = f32[3,3,256,256]{3,2,1,0:T(8,128)} custom-call(s32[3]{0:T(128)S(1)} %pad_add_fusion.place_ref, bf16[768,256]{1,0:T(8,128)(2,1)S(1)} %get-tuple-element.111.refs_0_, bf16[768,256]{1,0:T(8,128)(2,1)S(1)} %collective-permute-done.56.refs_1_, bf16[768,256]{1,0:T(8,128)(2,1)S(1)} %collective-permute-done.57.refs_2_, ...), custom_call_target="tpu_custom_call" | custom-call | tf_op jit(solution)/shard_map/correlate_kernel/pallas_call | solution.py:374
  232.1 4.2 %collective-permute-done.66.refs_1_ = bf16[768,256]{1,0:T(8,128)(2,1)S(1)} collective-permute-done((bf16[768,256]{1,0:T(8,128)(2,1)S(1)}, bf16[768,256]{1,0:T(8,128)(2,1)S(1)}, u32[]{:S(2)}, u32[]{:S(2)}) %collective-permute-start.66) | collective-permute-done | bytes 393248 | tf_op jit(solution)/shard_map/ppermute | solution.py:14
  236.3 5.8 %correlate_kernel.3 = f32[3,3,256,256]{3,2,1,0:T(8,128)} custom-call(s32[3]{0:T(128)S(1)} %pad_add_fusion.place_ref, bf16[768,256]{1,0:T(8,128)(2,1)S(1)} %get-tuple-element.114.refs_0_, bf16[768,256]{1,0:T(8,128)(2,1)S(1)} %collective-permute-done.66.refs_1_, bf16[768,256]{1,0:T(8,128)(2,1)S(1)} %collective-permute-done.67.refs_2_, ...), custom_call_target="tpu_custom_call" | custom-call | tf_op jit(solution)/shard_map/correlate_kernel/pallas_call | solution.py:374
  242.1 3.6 %unpack_kernel.1 = (f32[512,1024]{1,0:T(8,128)}, f32[1024,512]{1,0:T(8,128)}, f32[1152,128]{1,0:T(8,128)}, f32[9,128]{1,0:T(8,128)}) custom-call(s32[3]{0:T(128)S(1)} %pad_add_fusion.place_ref, bf16[304,512]{1,0:T(8,128)(2,1)S(1)} %pad_maximum_fusion.refs_0_, bf16[304,512]{1,0:T(8,128)(2,1)S(1)} %collective-permute-done.49.refs_1_, ...), custom_call_target="tpu_custom_call" | custom-call | tf_op jit(solution)/shard_map/unpack_kernel/pallas_call | solution.py:735
  (144 shorter events, 68.1 us)
Async XLA Ops:
  91.1 26.7 %collective-permute-start.30 = (bf16[304,512]{1,0:T(8,128)(2,1)S(1)}, bf16[304,512]{1,0:T(8,128)(2,1)S(1)}, u32[]{:S(2)}, u32[]{:S(2)}) collective-permute-start(bf16[304,512]{1,0:T(8,128)(2,1)S(1)} %get-tuple-element.92), channel_id=1, source_target_pairs={{0,4},{4,0},{8,12},{12,8},{16,20},{20,16},{24,28},{28,24},{1,5},{5... | collective-permute-start | bytes 933896 | tf_op jit(solution)/shard_map/ppermute | solution.py:14
  91.7 26.1 %collective-permute-start.32 = (bf16[304,512]{1,0:T(8,128)(2,1)S(1)}, bf16[304,512]{1,0:T(8,128)(2,1)S(1)}, u32[]{:S(2)}, u32[]{:S(2)}) collective-permute-start(bf16[304,512]{1,0:T(8,128)(2,1)S(1)} %add_convert_fusion.2), channel_id=1, source_target_pairs={{0,8},{4,12},{8,0},{12,4},{16,24},{20,28},{24,16},{28,20},{1,9},{5... | collective-permute-start | bytes 933896 | tf_op jit(solution)/shard_map/ppermute | solution.py:14
  93.2 24.7 %collective-permute-start.34 = (bf16[304,512]{1,0:T(8,128)(2,1)S(1)}, bf16[304,512]{1,0:T(8,128)(2,1)S(1)}, u32[]{:S(2)}, u32[]{:S(2)}) collective-permute-start(bf16[304,512]{1,0:T(8,128)(2,1)S(1)} %add_convert_fusion.1), channel_id=1, source_target_pairs={{0,16},{4,20},{8,24},{12,28},{16,0},{20,4},{24,8},{28,12},{1,17},{... | collective-permute-start | bytes 933896 | tf_op jit(solution)/shard_map/ppermute | solution.py:14
  94.4 23.5 %collective-permute-start.36 = (bf16[304,512]{1,0:T(8,128)(2,1)S(1)}, bf16[304,512]{1,0:T(8,128)(2,1)S(1)}, u32[]{:S(2)}, u32[]{:S(2)}) collective-permute-start(bf16[304,512]{1,0:T(8,128)(2,1)S(1)} %add_convert_fusion), channel_id=1, source_target_pairs={{0,24},{4,28},{8,16},{12,20},{16,8},{20,12},{24,0},{28,4},{1,25},{... | collective-permute-start | bytes 933896 | tf_op jit(solution)/shard_map/ppermute | solution.py:14
  117.8 53.2 %collective-permute-start.68 = (bf16[768,256]{1,0:T(8,128)(2,1)S(1)}, bf16[768,256]{1,0:T(8,128)(2,1)S(1)}, u32[]{:S(2)}, u32[]{:S(2)}) collective-permute-start(bf16[768,256]{1,0:T(8,128)(2,1)S(1)} %get-tuple-element.114.refs_0_), channel_id=1, source_target_pairs={{0,3},{1,2},{2,1},{3,0},{4,7},{5,6},{6,5},{7,4},{8,11},{9,10},{10,... | collective-permute-start | bytes 1179656 | tf_op jit(solution)/shard_map/ppermute | solution.py:14
  117.8 55.5 %collective-permute-start.67 = (bf16[768,256]{1,0:T(8,128)(2,1)S(1)}, bf16[768,256]{1,0:T(8,128)(2,1)S(1)}, u32[]{:S(2)}, u32[]{:S(2)}) collective-permute-start(bf16[768,256]{1,0:T(8,128)(2,1)S(1)} %get-tuple-element.114.refs_0_), channel_id=1, source_target_pairs={{0,2},{1,3},{2,0},{3,1},{4,6},{5,7},{6,4},{7,5},{8,10},{9,11},{10,... | collective-permute-start | bytes 1179656 | tf_op jit(solution)/shard_map/ppermute | solution.py:14
  118.8 18.1 %collective-permute-start.43 = (bf16[304,128]{1,0:T(8,128)(2,1)S(1)}, bf16[304,128]{1,0:T(8,128)(2,1)S(1)}, u32[]{:S(2)}, u32[]{:S(2)}) collective-permute-start(bf16[304,128]{1,0:T(8,128)(2,1)S(1)} %get-tuple-element.106), channel_id=1, source_target_pairs={{0,1},{1,0},{2,3},{3,2},{4,5},{5,4},{6,7},{7,6},{8,9},{9,8},{10,11... | collective-permute-start | bytes 233480 | tf_op jit(solution)/shard_map/ppermute | solution.py:14
  123.3 45.5 %collective-permute-start.44 = (bf16[304,128]{1,0:T(8,128)(2,1)S(1)}, bf16[304,128]{1,0:T(8,128)(2,1)S(1)}, u32[]{:S(2)}, u32[]{:S(2)}) collective-permute-start(bf16[304,128]{1,0:T(8,128)(2,1)S(1)} %get-tuple-element.107), channel_id=1, source_target_pairs={{0,2},{1,3},{2,0},{3,1},{4,6},{5,7},{6,4},{7,5},{8,10},{9,11},{10,... | collective-permute-start | bytes 233480 | tf_op jit(solution)/shard_map/ppermute | solution.py:14
  123.3 45.5 %collective-permute-start.45 = (bf16[304,128]{1,0:T(8,128)(2,1)S(1)}, bf16[304,128]{1,0:T(8,128)(2,1)S(1)}, u32[]{:S(2)}, u32[]{:S(2)}) collective-permute-start(bf16[304,128]{1,0:T(8,128)(2,1)S(1)} %get-tuple-element.108), channel_id=1, source_target_pairs={{0,3},{1,2},{2,1},{3,0},{4,7},{5,6},{6,5},{7,4},{8,11},{9,10},{10,... | collective-permute-start | bytes 233480 | tf_op jit(solution)/shard_map/ppermute | solution.py:14
  136.9 62.0 %collective-permute-start.58 = (bf16[768,256]{1,0:T(8,128)(2,1)S(1)}, bf16[768,256]{1,0:T(8,128)(2,1)S(1)}, u32[]{:S(2)}, u32[]{:S(2)}) collective-permute-start(bf16[768,256]{1,0:T(8,128)(2,1)S(1)} %get-tuple-element.111.refs_0_), channel_id=1, source_target_pairs={{0,3},{1,2},{2,1},{3,0},{4,7},{5,6},{6,5},{7,4},{8,11},{9,10},{10,... | collective-permute-start | bytes 1179656 | tf_op jit(solution)/shard_map/ppermute | solution.py:14
  168.8 31.6 %collective-permute-start.57 = (bf16[768,256]{1,0:T(8,128)(2,1)S(1)}, bf16[768,256]{1,0:T(8,128)(2,1)S(1)}, u32[]{:S(2)}, u32[]{:S(2)}) collective-permute-start(bf16[768,256]{1,0:T(8,128)(2,1)S(1)} %get-tuple-element.111.refs_0_), channel_id=1, source_target_pairs={{0,2},{1,3},{2,0},{3,1},{4,6},{5,7},{6,4},{7,5},{8,10},{9,11},{10,... | collective-permute-start | bytes 1179656 | tf_op jit(solution)/shard_map/ppermute | solution.py:14
  168.8 32.2 %collective-permute-start.56 = (bf16[768,256]{1,0:T(8,128)(2,1)S(1)}, bf16[768,256]{1,0:T(8,128)(2,1)S(1)}, u32[]{:S(2)}, u32[]{:S(2)}) collective-permute-start(bf16[768,256]{1,0:T(8,128)(2,1)S(1)} %get-tuple-element.111.refs_0_), channel_id=1, source_target_pairs={{0,1},{1,0},{2,3},{3,2},{4,5},{5,4},{6,7},{7,6},{8,9},{9,8},{10,11... | collective-permute-start | bytes 1179656 | tf_op jit(solution)/shard_map/ppermute | solution.py:14
  171.1 13.6 %collective-permute-start.48 = (bf16[304,128]{1,0:T(8,128)(2,1)S(1)}, bf16[304,128]{1,0:T(8,128)(2,1)S(1)}, u32[]{:S(2)}, u32[]{:S(2)}) collective-permute-start(bf16[304,128]{1,0:T(8,128)(2,1)S(1)} %add_convert_fusion.9), channel_id=1, source_target_pairs={{0,3},{1,2},{2,1},{3,0},{4,7},{5,6},{6,5},{7,4},{8,11},{9,10},{10,... | collective-permute-start | bytes 233480 | tf_op jit(solution)/shard_map/ppermute | solution.py:14
  173.3 21.9 %collective-permute-start.47 = (bf16[304,128]{1,0:T(8,128)(2,1)S(1)}, bf16[304,128]{1,0:T(8,128)(2,1)S(1)}, u32[]{:S(2)}, u32[]{:S(2)}) collective-permute-start(bf16[304,128]{1,0:T(8,128)(2,1)S(1)} %add_convert_fusion.9), channel_id=1, source_target_pairs={{0,2},{1,3},{2,0},{3,1},{4,6},{5,7},{6,4},{7,5},{8,10},{9,11},{10,... | collective-permute-start | bytes 233480 | tf_op jit(solution)/shard_map/ppermute | solution.py:14
  184.7 12.7 %collective-permute-start.46 = (bf16[304,128]{1,0:T(8,128)(2,1)S(1)}, bf16[304,128]{1,0:T(8,128)(2,1)S(1)}, u32[]{:S(2)}, u32[]{:S(2)}) collective-permute-start(bf16[304,128]{1,0:T(8,128)(2,1)S(1)} %add_convert_fusion.9), channel_id=1, source_target_pairs={{0,1},{1,0},{2,3},{3,2},{4,5},{5,4},{6,7},{7,6},{8,9},{9,8},{10,11... | collective-permute-start | bytes 233480 | tf_op jit(solution)/shard_map/ppermute | solution.py:14
  198.9 21.4 %collective-permute-start.51 = (bf16[304,512]{1,0:T(8,128)(2,1)S(1)}, bf16[304,512]{1,0:T(8,128)(2,1)S(1)}, u32[]{:S(2)}, u32[]{:S(2)}) collective-permute-start(bf16[304,512]{1,0:T(8,128)(2,1)S(1)} %pad_maximum_fusion.refs_0_), channel_id=1, source_target_pairs={{0,24},{4,28},{8,16},{12,20},{16,8},{20,12},{24,0},{28,4},{1,25},{... | collective-permute-start | bytes 933896 | tf_op jit(solution)/shard_map/ppermute | solution.py:14
  200.4 18.3 %collective-permute-start.60 = (bf16[576,256]{1,0:T(8,128)(2,1)S(1)}, bf16[576,256]{1,0:T(8,128)(2,1)S(1)}, u32[]{:S(2)}, u32[]{:S(2)}) collective-permute-start(bf16[576,256]{1,0:T(8,128)(2,1)S(1)} %get-tuple-element.113.refs_5_), channel_id=1, source_target_pairs={{0,16},{4,20},{8,24},{12,28},{16,0},{20,4},{24,8},{28,12},{1,17},{... | collective-permute-start | bytes 884744 | tf_op jit(solution)/shard_map/ppermute | solution.py:14
  201.0 19.3 %collective-permute-start.59 = (bf16[576,256]{1,0:T(8,128)(2,1)S(1)}, bf16[576,256]{1,0:T(8,128)(2,1)S(1)}, u32[]{:S(2)}, u32[]{:S(2)}) collective-permute-start(bf16[576,256]{1,0:T(8,128)(2,1)S(1)} %get-tuple-element.113.refs_5_), channel_id=1, source_target_pairs={{0,8},{4,12},{8,0},{12,4},{16,24},{20,28},{24,16},{28,20},{1,9},{5... | collective-permute-start | bytes 884744 | tf_op jit(solution)/shard_map/ppermute | solution.py:14
  202.5 22.7 %collective-permute-start.50 = (bf16[304,512]{1,0:T(8,128)(2,1)S(1)}, bf16[304,512]{1,0:T(8,128)(2,1)S(1)}, u32[]{:S(2)}, u32[]{:S(2)}) collective-permute-start(bf16[304,512]{1,0:T(8,128)(2,1)S(1)} %pad_maximum_fusion.refs_0_), channel_id=1, source_target_pairs={{0,16},{4,20},{8,24},{12,28},{16,0},{20,4},{24,8},{28,12},{1,17},{... | collective-permute-start | bytes 933896 | tf_op jit(solution)/shard_map/ppermute | solution.py:14
  208.2 17.0 %collective-permute-start.49 = (bf16[304,512]{1,0:T(8,128)(2,1)S(1)}, bf16[304,512]{1,0:T(8,128)(2,1)S(1)}, u32[]{:S(2)}, u32[]{:S(2)}) collective-permute-start(bf16[304,512]{1,0:T(8,128)(2,1)S(1)} %pad_maximum_fusion.refs_0_), channel_id=1, source_target_pairs={{0,8},{4,12},{8,0},{12,4},{16,24},{20,28},{24,16},{28,20},{1,9},{5... | collective-permute-start | bytes 933896 | tf_op jit(solution)/shard_map/ppermute | solution.py:14
  225.2 16.8 %collective-permute-start.52 = (bf16[304,512]{1,0:T(8,128)(2,1)S(1)}, bf16[304,512]{1,0:T(8,128)(2,1)S(1)}, u32[]{:S(2)}, u32[]{:S(2)}) collective-permute-start(bf16[304,512]{1,0:T(8,128)(2,1)S(1)} %pad_maximum_fusion.refs_0_), channel_id=1, source_target_pairs={{0,4},{4,0},{8,12},{12,8},{16,20},{20,16},{24,28},{28,24},{1,5},{5... | collective-permute-start | bytes 933896 | tf_op jit(solution)/shard_map/ppermute | solution.py:14
  225.2 16.8 %collective-permute-start.55 = (bf16[304,512]{1,0:T(8,128)(2,1)S(1)}, bf16[304,512]{1,0:T(8,128)(2,1)S(1)}, u32[]{:S(2)}, u32[]{:S(2)}) collective-permute-start(bf16[304,512]{1,0:T(8,128)(2,1)S(1)} %collective-permute-done.51.refs_3_), channel_id=1, source_target_pairs={{0,4},{4,0},{8,12},{12,8},{16,20},{20,16},{24,28},{28,24},{1,5},{5... | collective-permute-start | bytes 933896 | tf_op jit(solution)/shard_map/ppermute | solution.py:14
  225.7 16.3 %collective-permute-start.54 = (bf16[304,512]{1,0:T(8,128)(2,1)S(1)}, bf16[304,512]{1,0:T(8,128)(2,1)S(1)}, u32[]{:S(2)}, u32[]{:S(2)}) collective-permute-start(bf16[304,512]{1,0:T(8,128)(2,1)S(1)} %collective-permute-done.50.refs_2_), channel_id=1, source_target_pairs={{0,4},{4,0},{8,12},{12,8},{16,20},{20,16},{24,28},{28,24},{1,5},{5... | collective-permute-start | bytes 933896 | tf_op jit(solution)/shard_map/ppermute | solution.py:14
  225.8 16.2 %collective-permute-start.53 = (bf16[304,512]{1,0:T(8,128)(2,1)S(1)}, bf16[304,512]{1,0:T(8,128)(2,1)S(1)}, u32[]{:S(2)}, u32[]{:S(2)}) collective-permute-start(bf16[304,512]{1,0:T(8,128)(2,1)S(1)} %collective-permute-done.49.refs_1_), channel_id=1, source_target_pairs={{0,4},{4,0},{8,12},{12,8},{16,20},{20,16},{24,28},{28,24},{1,5},{5... | collective-permute-start | bytes 933896 | tf_op jit(solution)/shard_map/ppermute | solution.py:14
  (49 other events, 341.8 us)
